TPU v7x, 256 devices: a whole 4x4x8 slice. The times are simulated.
256 devices in a mesh: face: 32 (over z, y_lo, core), depth: 8 (over y_hi, x).
Axes of the slice: x: 4, y: 4 (y_hi: 2, y_lo: 2; y = y_hi * 2 + y_lo), z: 8, core: 2. Of those that a mesh axis runs over, the one named last changes fastest.
Arguments:
- thermal_field: float32 [2, 32, 8, 2048], P(None, 'face', 'depth'), may hold values from -6 to 6
- lumped_storage: float32 [2, 32, 8, 2048], P(None, 'face', 'depth'), may hold values from 1 to 4
- simplex_vertices: int32 [2, 32, 8, 4, 8192], P(None, 'face', 'depth'), may hold values from 0 to 2047
- stiffness_entries: float32 [2, 32, 8, 10, 8192], P(None, 'face', 'depth'), may hold values from -0.3 to 2, as said below
- interface_vertices: int32 [2, 32, 8, 2, 256], P(None, 'face', 'depth'), may hold values from 0 to 2047, as said below
- touching_triangle_vertices: int32 [2, 32, 3, 1024], P(None, 'face'), may hold values from 0 to 2047
- partner_lookup: int32 [32, 1024], replicated, may hold values from 0 to 32767, as said below
- engaged_flags: int32 [32, 1024], P('face'), may hold values 0 or 1
- rotor_gap_quantities: float32 [3, 32, 1024], P(None, 'face'), may hold values from -6 to 6
- lining_orthogonal_motion: float32 [32, 1024], P('face'), may hold values from -6 to 6
- touching_transfer_factor: float32 [32, 1024], P('face'), may hold values from 2 to 16
Outputs:
- advanced_thermal_field: float32 [2, 32, 8, 2048], P(None, 'face', 'depth')
- pressure: float32 [32, 1024], P('face')
Inputs may be any that keep to these rules, and one draw needn't show every extreme that they name: `stiffness_entries`: diagonal entries (the first four components) lie in [1, 2], off-diagonal ones in [-0.3, -0.05]. `interface_vertices`: the two lists of one body on one device name 512 different nodes. Position i of a block's upper list and position i of the lower list of the block above are copies of one node. `partner_lookup`: A disc face may meet a pad face of any patch; several disc faces may meet one pad face.
All inputs are finite; a program needn't handle non-finite values. No bound on the sum of `engaged_flags` on one device may be relied on, other than what follows from the above.
Results may differ from a plain program's by a relative error of at most 0.00002.
Values sent between devices are 32-bit elements; how exact they have to be, the bound alone decides.
No kernel may reach another device: no remote copies, remote signals or barrier semaphores. Data moves between devices by JAX's collectives and lax.ppermute only.
A program may use at most 64 MiB of HBM per device.

v0:
```python
import jax
import jax.numpy as jnp
from jax import lax
from jax.sharding import PartitionSpec as P

increment_factor = 0.05
nitsche = 1.0
film_floor = 0.25


def padded_2(cells, sides, width):
    for axis, dim in sides:
        count = lax.axis_size(axis)
        ends = count - 1
        head = lax.slice_in_dim(cells, 0, width, axis=dim)
        tail = lax.slice_in_dim(cells, cells.shape[dim] - width, cells.shape[dim], axis=dim)
        cells = jnp.concatenate(
            [
                lax.ppermute(tail, axis, [(i, (i + 1) % count) for i in range(ends)]),
                cells,
                lax.ppermute(head, axis, [((i + 1) % count, i) for i in range(ends)]),
            ],
            axis=dim,
        )
    return cells


def element_residual(values, corners, entries):
    picked = values[corners]
    row_one = (
        entries[0] * picked[0]
        + entries[4] * picked[1]
        + entries[5] * picked[2]
        + entries[6] * picked[3]
    )
    row_two = (
        entries[4] * picked[0]
        + entries[1] * picked[1]
        + entries[7] * picked[2]
        + entries[8] * picked[3]
    )
    row_three = (
        entries[5] * picked[0]
        + entries[7] * picked[1]
        + entries[2] * picked[2]
        + entries[9] * picked[3]
    )
    row_four = (
        entries[6] * picked[0]
        + entries[8] * picked[1]
        + entries[9] * picked[2]
        + entries[3] * picked[3]
    )
    stacked = -jnp.stack([row_one, row_two, row_three, row_four])
    return jax.ops.segment_sum(
        stacked.reshape(-1), corners.reshape(-1), num_segments=values.shape[0]
    )


def touching_triangle_values(values, corners):
    picked = values[corners]
    return (picked[0] + picked[1] + picked[2]) / 3.0


def spread_faces(face_rates, corners, solid_vertex_total):
    shares = jnp.broadcast_to(face_rates / 3.0, corners.shape)
    return jax.ops.segment_sum(
        shares.reshape(-1), corners.reshape(-1), num_segments=solid_vertex_total
    )


def set_rims(values, low_at, up_at, low_set, up_set):
    return values.at[low_at].set(low_set).at[up_at].set(up_set)


def local(
    thermal_field,
    lumped_storage,
    simplex_vertices,
    stiffness_entries,
    interface_vertices,
    touching_triangle_vertices,
    partner_lookup,
    engaged_flags,
    rotor_gap_quantities,
    lining_orthogonal_motion,
    touching_transfer_factor,
):
    solid_vertex_total = thermal_field.shape[-1]
    patch_index = lax.axis_index("face")
    depth_index = lax.axis_index("depth")
    surface = (depth_index == 0).astype(jnp.float32)
    thermal_imbalance = jnp.stack(
        [
            element_residual(
                thermal_field[solid_selector, 0, 0],
                simplex_vertices[solid_selector, 0, 0],
                stiffness_entries[solid_selector, 0, 0],
            )
            for solid_selector in range(2)
        ]
    )
    rotor_triangle_values = touching_triangle_values(
        thermal_field[0, 0, 0], touching_triangle_vertices[0, 0]
    )
    lining_triangle_values = touching_triangle_values(
        thermal_field[1, 0, 0], touching_triangle_vertices[1, 0]
    )
    active_mask = engaged_flags[0].astype(jnp.float32)
    displace = rotor_gap_quantities[0, 0]
    opening = rotor_gap_quantities[1, 0]
    multiplier = rotor_gap_quantities[2, 0]
    weight = active_mask * touching_transfer_factor[0]
    own_match = lax.dynamic_slice_in_dim(partner_lookup, patch_index, 1, 0)[0]
    pad_normals, pad_traces = (
        lax.all_gather(lining_orthogonal_motion[0], "face", axis=0, tiled=True),
        lax.all_gather(lining_triangle_values, "face", axis=0, tiled=True),
    )
    pressure = active_mask * jnp.maximum(
        multiplier + nitsche * (displace - pad_normals[own_match] - opening), 0.0
    )
    disc_rate = weight * (film_floor + pressure) * (pad_traces[own_match] - rotor_triangle_values)
    spread = jax.ops.segment_sum(disc_rate, own_match, num_segments=partner_lookup.size)
    pad_rate = -lax.psum_scatter(spread, "face", scatter_dimension=0, tiled=True)
    nodal = jnp.stack(
        [
            spread_faces(disc_rate, touching_triangle_vertices[0, 0], solid_vertex_total),
            spread_faces(pad_rate, touching_triangle_vertices[1, 0], solid_vertex_total),
        ]
    )
    thermal_imbalance = thermal_imbalance + surface * nodal
    lower = interface_vertices[:, 0, 0, 0]
    upper = interface_vertices[:, 0, 0, 1]
    low_values = jnp.take_along_axis(thermal_imbalance, lower, axis=1)
    up_values = jnp.take_along_axis(thermal_imbalance, upper, axis=1)
    rows_both = jnp.stack([low_values.reshape(-1), up_values.reshape(-1)])
    padded = padded_2(rows_both, (("depth", 0),), 1)
    low_new = low_values + padded[0].reshape(low_values.shape)
    up_new = up_values + padded[3].reshape(up_values.shape)
    gathered_imbalance = jax.vmap(set_rims)(thermal_imbalance, lower, upper, low_new, up_new)
    advanced_thermal_field = (
        thermal_field + increment_factor * gathered_imbalance[:, None, None, :] / lumped_storage
    )
    return (advanced_thermal_field, pressure[None])


def solution(mesh):
    placed = (
        P(None, "face", "depth", None),
        P(None, "face", "depth", None),
        P(None, "face", "depth", None, None),
        P(None, "face", "depth", None, None),
        P(None, "face", "depth", None, None),
        P(None, "face", None, None),
        P(),
        P("face", None),
        P(None, "face", None),
        P("face", None),
        P("face", None),
    )
    return jax.shard_map(
        local,
        mesh=mesh,
        in_specs=placed,
        out_specs=(P(None, "face", "depth", None), P("face", None)),
        check_vma=False,
    )
```

profile of v0, /device:TPU:8, one launch (start us, length us, event | category | flops | bytes accessed | tf_op | source)
XLA Modules:
  0.0 951.9 jit_solution(17797581546140559378)
XLA Ops:
  7.2 0.0 all-reduce.3.cloned.1.call-start
  7.2 0.7 fusion.56
  7.9 0.8 compare_select_fusion.4
  8.8 17.4 %gather_fusion.3 = f32[3072]{0:T(1024)S(1)} fusion(f32[2048]{0:T(1024)S(1)} %bitcast.281, s32[3072]{0:T(1024)S(1)} %broadcast_clamp_fusion.3), kind=kCustom, calls=%fused_computation.5 | custom fusion | bytes 36864 | tf_op jit(solution)/shard_map/gather | solution.py:61
  26.2 0.0 copy-start.8
  26.2 34.3 %all-gather.1 = f32[1,32768]{1,0:T(1,128)S(1)} all-gather(f32[1,1024]{1,0:T(1,128)S(1)} %bitcast.324), channel_id=3, replica_groups=mesh['face'=32,'depth'=8] {'face'}, dimensions={1}, use_global_device_ids=true | all-gather | bytes 135168 | tf_op jit(solution)/shard_map/all_gather | solution.py:117
  60.6 34.4 %all-gather = f32[1,32768]{1,0:T(1,128)S(1)} all-gather(f32[1,1024]{1,0:T(1,128)S(1)} %copy-done.8), channel_id=2, replica_groups=mesh['face'=32,'depth'=8] {'face'}, dimensions={1}, use_global_device_ids=true | all-gather | bytes 135168 | tf_op jit(solution)/shard_map/all_gather | solution.py:116
  94.9 6.1 gather_fusion.4
  101.1 6.2 gather_fusion.2
  107.2 0.0 copy-start.4
  107.3 0.7 copy-done.4
  108.0 0.7 copy-done.6
  108.6 17.4 %gather_fusion.5 = f32[3072]{0:T(1024)S(1)} fusion(f32[2048]{0:T(1024)S(1)} %bitcast.279, s32[3072]{0:T(1024)S(1)} %broadcast_clamp_fusion.2), kind=kCustom, calls=%fused_computation.7 | custom fusion | bytes 36864 | tf_op jit(solution)/shard_map/gather | solution.py:61
  126.1 0.0 copy-start.1
  126.1 6.5 scatter_custom_fusion.3
  132.6 0.0 all-reduce.3.cloned.1.call-update
  132.7 0.1 fusion
  132.8 180.5 %gather_fusion.1 = f32[32768]{0:T(1024)S(1)} fusion(f32[2048]{0:T(1024)S(1)} %bitcast.282, s32[32768]{0:T(1024)S(1)} %broadcast_clamp_fusion), kind=kCustom, calls=%fused_computation.3 | custom fusion | bytes 393216 | tf_op jit(solution)/shard_map/gather | solution.py:29
  313.4 0.0 copy-start
  313.4 180.5 %gather_fusion = f32[32768]{0:T(1024)S(1)} fusion(f32[2048]{0:T(1024)S(1)} %bitcast.280, s32[32768]{0:T(1024)S(1)} %broadcast_clamp_fusion.1), kind=kCustom, calls=%fused_computation.2 | custom fusion | bytes 393216 | tf_op jit(solution)/shard_map/gather | solution.py:29
  494.0 0.2 fusion.15
  494.2 0.2 fusion.22
  494.4 0.2 fusion.27
  494.6 0.3 fusion.2
  495.0 0.0 copy-start.5
  495.0 0.7 copy-done.5
  495.7 172.5 %scatter_custom_fusion = f32[2048]{0:T(1024)S(1)} fusion(s32[32768]{0:T(1024)S(1)} %bitcast.308, f32[32768]{0:T(1024)S(1)} %bitcast.307, f32[]{:T(128)} %constant.19.clone.1), kind=kCustom, calls=%fused_computation.121 | custom fusion | flops 32768 | bytes 8196 | tf_op jit(solution)/shard_map/scatter-add | solution.py:55
  668.3 172.5 %scatter_custom_fusion.1 = f32[2048]{0:T(1024)S(1)} fusion(s32[32768]{0:T(1024)S(1)} %bitcast.310, f32[32768]{0:T(1024)S(1)} %bitcast.309, f32[]{:T(128)} %constant.19.clone.1), kind=kCustom, calls=%fused_computation.119 | custom fusion | flops 32768 | bytes 8196 | tf_op jit(solution)/shard_map/scatter-add | solution.py:55
  840.8 0.0 copy-start.10
  840.8 0.7 copy-done.10
  841.5 0.6 dynamic-slice
  842.7 16.7 %scatter_custom_fusion.2 = f32[2048]{0:T(1024)S(1)} fusion(s32[3072]{0:T(1024)S(1)} %bitcast.326, f32[3072]{0:T(1024)S(1)} %reshape.422, f32[]{:T(128)} %constant.19.clone.1), kind=kCustom, calls=%fused_computation.117 | custom fusion | flops 3072 | bytes 8196 | tf_op jit(solution)/shard_map/scatter-add | solution.py:67
  859.5 0.0 all-reduce.3.cloned.1.call-done
  859.5 0.7 fusion.38
  860.2 16.7 %scatter_custom_fusion.4 = f32[2048]{0:T(1024)S(1)} fusion(s32[3072]{0:T(1024)S(1)} %bitcast.325, f32[3072]{0:T(1024)S(1)} %reshape.438, f32[]{:T(128)} %constant.19.clone.1), kind=kCustom, calls=%fused_computation.115 | custom fusion | flops 3072 | bytes 8196 | tf_op jit(solution)/shard_map/scatter-add | solution.py:67
  876.9 4.8 gather_fusion.6
  881.8 1.3 collective-permute-start.1
  883.1 0.6 fusion.37
  883.7 4.8 gather_fusion.7
  888.6 0.5 broadcast.309
  889.1 0.7 reduce.7
  889.8 4.5 collective-permute-start
  894.4 1.3 collective-permute-done
  895.7 0.7 reduce.6
  896.4 24.0 %scatter_fusion = f32[2,2048]{1,0:T(2,128)S(1)} fusion(f32[2,2048]{1,0:T(2,128)S(1)} %maximum_add_fusion, s32[512]{0:T(512)S(1)} %bitcast.286, f32[512]{0:T(512)S(1)} %bitcast.328), kind=kCustom, calls=%fused_computation.13 | custom fusion | bytes 10240 | tf_op jit(solution)/shard_map/vmap()/scatter | solution.py:73
  920.4 0.0 copy-start.3
  920.4 24.0 %scatter_fusion.1 = f32[2,2048]{1,0:T(2,128)S(1)} fusion(f32[2,2048]{1,0:T(2,128)S(1)} %scatter_fusion, s32[512]{0:T(512)S(1)} %bitcast.285, f32[512]{0:T(512)S(1)} %bitcast.327), kind=kCustom, calls=%fused_computation.14 | custom fusion | bytes 10240 | tf_op jit(solution)/shard_map/vmap()/scatter | solution.py:73
  944.5 0.6 copy.27
  (54 shorter events, 0.5 us)
Async XLA Ops:
  7.2 852.3 %all-reduce.3.cloned.1.call-start = ((), (), s32[]{:S(2)}) async-start(), calls=%async_computation | async-start | bytes 262144
  7.9 0.8 copy-start.2
  26.2 34.4 %copy-start.8 = (f32[1,1024]{1,0:T(1,128)S(1)}, f32[1,1024]{1,0:T(1,128)}, u32[]{:S(2)}) copy-start(f32[1,1024]{1,0:T(1,128)} %param.22) | copy-start | bytes 12292
  107.2 0.7 copy-start.4
  107.9 0.7 copy-start.6
  108.6 17.4 %copy-start.9 = (f32[1,1024]{1,0:T(1,128)S(1)}, f32[1,1024]{1,0:T(1,128)}, u32[]{:S(2)}) copy-start(f32[1,1024]{1,0:T(1,128)} %param.23) | copy-start | bytes 12292
  126.1 6.6 copy-start.1
  313.4 180.6 %copy-start = (f32[2,1,1,10,8192]{4,2,3,1,0:T(1,128)S(1)}, f32[2,1,1,10,8192]{4,2,3,1,0:T(1,128)}, u32[]{:S(2)}) copy-start(f32[2,1,1,10,8192]{4,2,3,1,0:T(1,128)} %param.16) | copy-start | bytes 1966084
  495.0 0.7 copy-start.5
  840.8 0.7 copy-start.10
  881.8 6.8 collective-permute-start.1
  889.8 5.8 collective-permute-start
  920.4 24.0 %copy-start.3 = (f32[2,1,1,2048]{3,2,1,0:T(1,128)S(1)}, f32[2,1,1,2048]{3,2,1,0:T(1,128)}, u32[]{:S(2)}) copy-start(f32[2,1,1,2048]{3,2,1,0:T(1,128)} %param.13) | copy-start | bytes 49156
  920.4 24.0 %copy-start.7 = (f32[2,1,1,2048]{3,2,1,0:T(1,128)S(1)}, f32[2,1,1,2048]{3,2,1,0:T(1,128)}, u32[]{:S(2)}) copy-start(f32[2,1,1,2048]{3,2,1,0:T(1,128)} %param.14) | copy-start | bytes 49156
Sparse Core Ops, SparseCore 0:
  132.8 197.7 all-reduce.2
where the time goes:
time: 960 us; the launch traced here: 952 us
  local copies, waits for them, and re-layouts  471 us (49%)
  other arithmetic  390 us (41%)
  blocking collectives  68.7 us (7%)
  between operations  15.2 us (2%)
    gather x2, local copies, waits for them, and re-layouts, element_residual(): picked = values[corners]  361 us
    scatter-add x2, other arithmetic, element_residual(): jax.ops.segment_sum(stacked.reshape(-1), corners.reshape(-1), num_segment...  345 us
    scatter x2, local copies, waits for them, and re-layouts, set_rims(): return values.at[low_at].set(low_set).at[up_at].set(up_set)  48 us
    gather x2, local copies, waits for them, and re-layouts, touching_triangle_values(): picked = values[corners]  34.8 us
    all_gather x1, blocking collectives, local(): lax.all_gather(lining_orthogonal_motion[0], 'face', axis=0, tiled=True)  34.4 us
    all_gather x1, blocking collectives, local(): lax.all_gather(lining_triangle_values, 'face', axis=0, tiled=True)  34.3 us
    scatter-add x2, other arithmetic, spread_faces(): jax.ops.segment_sum(shares.reshape(-1), corners.reshape(-1), num_segments...  33.4 us
  transfers between devices with their start and end apart: 3, of which 1 were waited for; matrix products, arithmetic and copies ran while one was open for 77% of the time, Pallas kernels for 0%

commit v1 on v0

v1 whole, which is shorter than its diff:
```python
import jax
import jax.numpy as jnp
from jax import lax
from jax.experimental import pallas as pl
from jax.experimental.pallas import tpu as pltpu
from jax.sharding import PartitionSpec as P

increment_factor = 0.05
nitsche = 1.0
film_floor = 0.25

LANES = 128
ROWS = 8
LOW = 64


def lane_lookup(row_of, indices, row_total):
    lane = indices & (LANES - 1)
    row = indices >> 7
    level = [
        jnp.take_along_axis(row_of(r), lane, axis=1, mode="promise_in_bounds")
        for r in range(row_total)
    ]
    bit = 0
    while len(level) > 1:
        odd = ((row >> bit) & 1) == 1
        level = [jnp.where(odd, level[k + 1], level[k]) for k in range(0, len(level), 2)]
        bit += 1
    return level[0]


def wide(ref, row, *lead):
    return ref[(*lead, pl.ds(row, ROWS, stride=0), slice(None))]


def split(values):
    coarse = values.astype(jnp.bfloat16).astype(jnp.float32)
    fine = (values - coarse).astype(jnp.bfloat16).astype(jnp.float32)
    return coarse, fine


def high_keys(high_total):
    half = high_total // 2
    keys = []
    for k in range(high_total // ROWS):
        place = lax.broadcasted_iota(jnp.int32, (ROWS, LANES), 0) + k * ROWS
        keys.append((place % half) * 2 + place // half)
    return keys


def low_keys():
    return [lax.broadcasted_iota(jnp.int32, (ROWS, LANES), 0) + k * ROWS for k in range(LOW // ROWS)]


def scatter_operands(index, coarse, fine, highs, lows):
    high = index >> 6
    low = index & (LOW - 1)
    zero = jnp.zeros((ROWS, LANES), jnp.float32)
    hit = [high == key for key in highs]
    values = [jnp.where(h, coarse, zero) for h in hit] + [jnp.where(h, fine, zero) for h in hit]
    one_hot = [jnp.where(low == key, 1.0, 0.0) for key in lows]
    return (
        jnp.concatenate(values, axis=0).astype(jnp.bfloat16),
        jnp.concatenate(one_hot, axis=0).astype(jnp.bfloat16),
    )


def contract(slices):
    values = jnp.concatenate([s[0] for s in slices], axis=1)
    one_hot = jnp.concatenate([s[1] for s in slices], axis=1)
    return lax.dot_general(
        values, one_hot, (((1,), (1,)), ((), ())), preferred_element_type=jnp.float32
    )


def store_nodal(ref, lead, total, scale=None):
    high_total = total.shape[0] // 2
    both = total[:high_total] + total[high_total:]
    if scale is not None:
        both = both * scale
    half = high_total // 2
    ref[(*lead, slice(0, half), slice(0, LOW))] = both[:half]
    ref[(*lead, slice(0, half), slice(LOW, LANES))] = both[half:]


def vmem_specs(count):
    return [pl.BlockSpec(memory_space=pltpu.VMEM) for _ in range(count)]


def packet_kernel(field, corners, motion, engaged, gaps, factor, out):
    for body in range(2):
        picked = [
            lane_lookup(lambda r: wide(field, r, body), corners[body, c], 16) for c in range(3)
        ]
        out[1 + body if body == 0 else 1] = (picked[0] + picked[1] + picked[2]) / 3.0
        if body == 0:
            out[2] = out[1]
    out[0] = motion[...]
    out[3] = engaged[...].astype(jnp.float32) * factor[...]
    out[4] = gaps[2] + nitsche * (gaps[0] - gaps[1])


def element_kernel(field, vertices, entries, rims, out, rim_out, coarse_at, fine_at):
    highs = high_keys(32)
    lows = low_keys()
    chunks = vertices.shape[1] // (4 * ROWS)
    for body in range(2):

        def chunk(j, total):
            corner = [vertices[body, pl.ds(32 * j + c, ROWS, stride=4), :] for c in range(4)]
            picked = [lane_lookup(lambda r: wide(field, r, body), i, 16) for i in corner]
            k = [entries[body, e, pl.ds(pl.multiple_of(ROWS * j, ROWS), ROWS), :] for e in range(10)]
            order = ((0, 4, 5, 6), (4, 1, 7, 8), (5, 7, 2, 9), (6, 8, 9, 3))
            for c in range(4):
                o = order[c]
                row = (
                    k[o[0]] * picked[0]
                    + k[o[1]] * picked[1]
                    + k[o[2]] * picked[2]
                    + k[o[3]] * picked[3]
                )
                coarse, fine = split(row)
                coarse_at[c] = coarse
                fine_at[c] = fine
            for c in range(4):
                slices = [
                    scatter_operands(
                        wide(vertices, 32 * j + 4 * s + c, body),
                        wide(coarse_at, s, c),
                        wide(fine_at, s, c),
                        highs,
                        lows,
                    )
                    for s in range(ROWS)
                ]
                total = total + contract(slices)
            return total

        total = lax.fori_loop(0, chunks, chunk, jnp.zeros((64, LOW), jnp.float32))
        store_nodal(out, (body,), total, -1.0)
    rim_out[...] = rim_lookup(out, rims)


def rim_lookup(nodal, rims):
    index = rims[...]
    first = lane_lookup(lambda r: wide(nodal, r, 0), index, 16)
    second = lane_lookup(lambda r: wide(nodal, r, 1), index, 16)
    place = lax.broadcasted_iota(jnp.int32, (ROWS, LANES), 0)
    return jnp.where(place < 4, first, second)


def contact_kernel(
    where, packets, lookup, gaps, engaged, factor, corners, rims, pressure_out, nodal, rim_out, pads, coarse_at, fine_at
):
    face = where[0]
    surface = (where[1] == 0).astype(jnp.float32)
    own = lookup[face]

    def place_of(patch):
        away = patch ^ face
        return (
            ((away & 1) << 4) | ((away & 2) << 2) | (away & 4) | ((away & 8) >> 2) | ((away & 16) >> 4)
        )

    spot = (place_of(own >> 10) << 10) | (own & 1023)

    def one_packet(p, carry):
        normal, trace = carry
        mine = (spot >> 10) == p
        local = spot & 1023
        normal = jnp.where(mine, lane_lookup(lambda r: wide(packets, r, p, 0), local, 8), normal)
        trace = jnp.where(mine, lane_lookup(lambda r: wide(packets, r, p, 1), local, 8), trace)
        return normal, trace

    zero = jnp.zeros((ROWS, LANES), jnp.float32)
    pad_normal, pad_trace = lax.fori_loop(0, 32, one_packet, (zero, zero))
    active = engaged[...].astype(jnp.float32)
    pressure = active * jnp.maximum(gaps[2] + nitsche * (gaps[0] - pad_normal - gaps[1]), 0.0)
    pressure_out[...] = pressure
    disc_rate = (active * factor[...]) * (film_floor + pressure) * (pad_trace - packets[0, 2])

    highs = high_keys(16)
    lows = low_keys()

    def one_source(p, total):
        source = face ^ place_of(face ^ p)
        index = lookup[source]
        local = index & 1023
        normal = lane_lookup(lambda r: wide(packets, r, 0, 0), local, 8)
        trace = lane_lookup(lambda r: wide(packets, r, 0, 1), local, 8)
        rate = (
            packets[p, 3]
            * (film_floor + jnp.maximum(packets[p, 4] - nitsche * normal, 0.0))
            * (trace - packets[p, 2])
        )
        coarse, fine = split(jnp.where((index >> 10) == face, rate, 0.0))
        coarse_at[0] = coarse
        fine_at[0] = fine
        slices = [
            scatter_operands(
                wide(lookup, s, source) & 1023, wide(coarse_at, s, 0), wide(fine_at, s, 0), highs, lows
            )
            for s in range(ROWS)
        ]
        return total + contract(slices)

    total = lax.fori_loop(0, 32, one_source, jnp.zeros((32, LOW), jnp.float32))
    store_nodal(pads, (), total, -1.0)

    highs = high_keys(32)
    for body in range(2):
        rate = disc_rate if body == 0 else pads[...]
        coarse, fine = split(rate / 3.0 * surface)
        coarse_at[body] = coarse
        fine_at[body] = fine
        total = jnp.zeros((64, LOW), jnp.float32)
        for c in range(3):
            slices = [
                scatter_operands(
                    wide(corners, s, body, c), wide(coarse_at, s, body), wide(fine_at, s, body), highs, lows
                )
                for s in range(ROWS)
            ]
            total = total + contract(slices)
        store_nodal(nodal, (body,), total)
    rim_out[...] = rim_lookup(nodal, rims)


def advance_kernel(field, storage, element, contact, rims, from_below, from_above, contact_below, out, coarse_at, fine_at):
    highs = high_keys(32)
    lows = low_keys()
    place = lax.broadcasted_iota(jnp.int32, (ROWS, LANES), 0)
    below = from_below[...] + contact_below[...]
    values = jnp.where((place & 1) == 0, pltpu.roll(below, 7, 0), pltpu.roll(from_above[...], 1, 0))
    coarse, fine = split(values)
    coarse_at[...] = coarse
    fine_at[...] = fine
    for body in range(2):
        slices = [
            scatter_operands(wide(rims, s), wide(coarse_at, s), wide(fine_at, s), highs, lows)
            for s in range(4 * body, 4 * body + 4)
        ]
        store_nodal(out, (body,), contract(slices))
    total = element[...] + contact[...] + out[...]
    out[...] = field[...] + increment_factor * total / storage[...]


def f32(*shape):
    return jax.ShapeDtypeStruct(shape, jnp.float32)


def call(body, out, arguments, scratch=(), smem=0, name=None, cost=None):
    return pl.pallas_call(
        body,
        out_shape=out,
        in_specs=[pl.BlockSpec(memory_space=pltpu.SMEM)] * smem + vmem_specs(len(arguments) - smem),
        out_specs=jax.tree.map(lambda _: pl.BlockSpec(memory_space=pltpu.VMEM), out),
        scratch_shapes=[pltpu.VMEM(s, jnp.float32) for s in scratch],
        name=name,
        cost_estimate=cost,
    )(*arguments)


def local(
    thermal_field,
    lumped_storage,
    simplex_vertices,
    stiffness_entries,
    interface_vertices,
    touching_triangle_vertices,
    partner_lookup,
    engaged_flags,
    rotor_gap_quantities,
    lining_orthogonal_motion,
    touching_transfer_factor,
):
    field = thermal_field.reshape(2, 16, LANES)
    storage = lumped_storage.reshape(2, 16, LANES)
    vertices = simplex_vertices.reshape(2, 4, 64, LANES).transpose(0, 2, 1, 3).reshape(2, 256, LANES)
    entries = stiffness_entries.reshape(2, 10, 64, LANES)
    rims = interface_vertices.reshape(2, 2, 2, LANES).transpose(0, 2, 1, 3).reshape(8, LANES)
    corners = touching_triangle_vertices.reshape(2, 3, ROWS, LANES)
    lookup = partner_lookup.reshape(32, ROWS, LANES)
    engaged = engaged_flags.reshape(ROWS, LANES)
    gaps = rotor_gap_quantities.reshape(3, ROWS, LANES)
    motion = lining_orthogonal_motion.reshape(ROWS, LANES)
    factor = touching_transfer_factor.reshape(ROWS, LANES)
    where = jnp.stack([lax.axis_index("face"), lax.axis_index("depth")]).astype(jnp.int32)

    packets = call(
        packet_kernel,
        f32(5, ROWS, LANES),
        (field, corners, motion, engaged, gaps, factor),
        name="packet",
    )[None]
    for step in (16, 8, 4, 2, 1):
        other = lax.ppermute(packets, "face", [(i, i ^ step) for i in range(32)])
        packets = jnp.concatenate([packets, other], axis=0)

    element, rim_element = call(
        element_kernel,
        (f32(2, 16, LANES), f32(ROWS, LANES)),
        (field, vertices, entries, rims),
        scratch=((4, ROWS, LANES), (4, ROWS, LANES)),
        name="element",
    )
    up = [(i, i + 1) for i in range(7)]
    down = [(i + 1, i) for i in range(7)]
    from_below = lax.ppermute(rim_element, "depth", up)
    from_above = lax.ppermute(rim_element, "depth", down)

    pressure, contact, rim_contact = call(
        contact_kernel,
        (f32(ROWS, LANES), f32(2, 16, LANES), f32(ROWS, LANES)),
        (where, packets, lookup, gaps, engaged, factor, corners, rims),
        scratch=((ROWS, LANES), (2, ROWS, LANES), (2, ROWS, LANES)),
        smem=1,
        name="contact",
    )
    contact_below = lax.ppermute(rim_contact, "depth", [(0, 1)])
    advanced = call(
        advance_kernel,
        f32(2, 16, LANES),
        (field, storage, element, contact, rims, from_below, from_above, contact_below),
        scratch=((ROWS, LANES), (ROWS, LANES)),
        name="advance",
    )
    return advanced.reshape(thermal_field.shape), pressure.reshape(1, 1024)


def solution(mesh):
    placed = (
        P(None, "face", "depth", None),
        P(None, "face", "depth", None),
        P(None, "face", "depth", None, None),
        P(None, "face", "depth", None, None),
        P(None, "face", "depth", None, None),
        P(None, "face", None, None),
        P(),
        P("face", None),
        P(None, "face", None),
        P("face", None),
        P("face", None),
    )
    return jax.shard_map(
        local,
        mesh=mesh,
        in_specs=placed,
        out_specs=(P(None, "face", "depth", None), P("face", None)),
        check_vma=False,
    )
```

time: 960 us -> 65.8 us (0.07)
  local copies, waits for them, and re-layouts: 471 us -> 2.2 us
  other arithmetic: 390 us -> 1.4 us
  blocking collectives: 68.7 us -> 0 us
  Pallas kernels: 0 us -> 25.6 us
  starting transfers between devices: 5.88 us -> 20.9 us
  between operations: 15.2 us -> 0.75 us
  waiting for transfers between devices: 1.29 us -> 13.8 us
    gather x10 -> x0, local copies, waits for them, and re-layouts: 418 us -> none  [the longest x2 361 us: element_residual(): picked = values[corners]]
    scatter-add x5 -> x0, other arithmetic: 385 us -> none  [the longest x2 345 us: element_residual(): jax.ops.segment_sum(stacked.reshape(-1), corners.reshape(-1), num_segment...]
    all_gather x2 -> x0, blocking collectives: 68.7 us -> none  [the longest x1 34.4 us: local(): lax.all_gather(lining_orthogonal_motion[0], 'face', axis=0, tiled=True)]
    scatter x2 -> x0, local copies, waits for them, and re-layouts: 48 us -> none  [set_rims(): return values.at[low_at].set(low_set).at[up_at].set(up_set)]
    pallas_call x0 -> x4, Pallas kernels: none -> 25.6 us  [call(): pl.pallas_call(body, out_shape=out, in_specs=[pl.BlockSpec(memory_space=p...]
    ppermute x2 -> x8, starting transfers between devices: 5.84 us -> 20.9 us  [the longest x5 11.7 us: local(): other = lax.ppermute(packets, 'face', [(i, i ^ step) for i in range(32)])]
    ppermute x2 -> x8, waiting for transfers between devices: 1.26 us -> 13.8 us  [the longest x5 12.3 us: local(): other = lax.ppermute(packets, 'face', [(i, i ^ step) for i in range(32)])]
  transfers between devices with their start and end apart: 3 -> 8, of which waited for: 1 -> 5; matrix products, arithmetic and copies ran while one was open for 77% -> 2% of each run, Pallas kernels for 0% -> 35%
where the time goes in v1:
time: 65.8 us; the launch traced here: 64.7 us
  Pallas kernels  25.6 us (39%)
  starting transfers between devices  20.9 us (32%)
  waiting for transfers between devices  13.8 us (21%)
  local copies, waits for them, and re-layouts  2.2 us (3%)
  other arithmetic  1.4 us (2%)
  between operations  0.75 us (1%)
    pallas_call x4, Pallas kernels, call(): pl.pallas_call(body, out_shape=out, in_specs=[pl.BlockSpec(memory_space=p...  25.6 us
    ppermute x5, waiting for transfers between devices, local(): other = lax.ppermute(packets, 'face', [(i, i ^ step) for i in range(32)])  12.3 us
    ppermute x5, starting transfers between devices, local(): other = lax.ppermute(packets, 'face', [(i, i ^ step) for i in range(32)])  11.7 us
    ppermute x1, starting transfers between devices, local(): contact_below = lax.ppermute(rim_contact, 'depth', [(0, 1)])  4.53 us
    ppermute x1, starting transfers between devices, local(): from_below = lax.ppermute(rim_element, 'depth', up)  3.38 us
    unnamed x17, local copies, waits for them, and re-layouts  2.15 us
    ppermute x1, waiting for transfers between devices, local(): contact_below = lax.ppermute(rim_contact, 'depth', [(0, 1)])  1.48 us
  transfers between devices with their start and end apart: 8, of which 5 were waited for; matrix products, arithmetic and copies ran while one was open for 2% of the time, Pallas kernels for 35%

profile of v1, /device:TPU:8, one launch (start us, length us, event | category | flops | bytes accessed | tf_op | source)
XLA Modules:
  0.0 64.7 jit_solution(10405538415878547281)
XLA Ops:
  0.6 1.6 %packet.1 = f32[5,8,128]{2,1,0:T(8,128)} custom-call(f32[2,16,128]{2,1,0:T(8,128)} %bitcast.34, s32[2,3,8,128]{3,2,1,0:T(8,128)} %bitcast.38, f32[8,128]{1,0:T(8,128)} %bitcast.51, s32[8,128]{1,0:T(8,128)} %bitcast.45, f32[3,8,128]{2,1,0:T(8,128)} %bitcast.40, f32[8,128]{1,0:T(8,128)} %bitcast.47), custom_call_target="tpu_custom_call" | custom-call | tf_op jit(solution)/shard_map/packet/pallas_call | solution.py:253
  2.2 0.0 copy-start.1
  2.2 7.2 %collective-permute-start = (f32[1,5,8,128]{3,2,1,0:T(8,128)}, f32[1,5,8,128]{3,2,1,0:T(8,128)S(1)}, u32[]{:S(2)}, u32[]{:S(2)}) collective-permute-start(f32[1,5,8,128]{3,2,1,0:T(8,128)} %bitcast.29), channel_id=1, source_target_pairs={{0,128},{8,136},{16,144},{24,152},{32,160},{40,168},{48,176},{56,1... | collective-permute-start | bytes 61448 | tf_op jit(solution)/shard_map/ppermute | solution.py:297
  9.4 2.0 %collective-permute-done = f32[1,5,8,128]{3,2,1,0:T(8,128)S(1)} collective-permute-done((f32[1,5,8,128]{3,2,1,0:T(8,128)}, f32[1,5,8,128]{3,2,1,0:T(8,128)S(1)}, u32[]{:S(2)}, u32[]{:S(2)}) %collective-permute-start) | collective-permute-done | bytes 20512 | tf_op jit(solution)/shard_map/ppermute | solution.py:297
  11.4 0.7 %pad_maximum_fusion.2 = f32[2,5,8,128]{3,2,1,0:T(8,128)S(1)} fusion(f32[1,5,8,128]{3,2,1,0:T(8,128)S(1)} %collective-permute-done, f32[1,5,8,128]{3,2,1,0:T(8,128)} %bitcast.30), kind=kLoop, calls=%fused_computation.2 | loop fusion | flops 10240 | bytes 81920 | tf_op jit(solution)/shard_map/concatenate | solution.py:298
  12.2 1.9 %collective-permute-start.1 = (f32[2,5,8,128]{3,2,1,0:T(8,128)S(1)}, f32[2,5,8,128]{3,2,1,0:T(8,128)S(1)}, u32[]{:S(2)}, u32[]{:S(2)}) collective-permute-start(f32[2,5,8,128]{3,2,1,0:T(8,128)S(1)} %pad_maximum_fusion.2), channel_id=1, source_target_pairs={{0,64},{8,72},{16,80},{24,88},{32,96},{40,104},{48,112},{56,120},{... | collective-permute-start | bytes 122888 | tf_op jit(solution)/shard_map/ppermute | solution.py:297
  14.1 0.0 copy-done.1
  14.1 3.0 %collective-permute-done.1 = f32[2,5,8,128]{3,2,1,0:T(8,128)S(1)} collective-permute-done((f32[2,5,8,128]{3,2,1,0:T(8,128)S(1)}, f32[2,5,8,128]{3,2,1,0:T(8,128)S(1)}, u32[]{:S(2)}, u32[]{:S(2)}) %collective-permute-start.1) | collective-permute-done | bytes 40992 | tf_op jit(solution)/shard_map/ppermute | solution.py:297
  17.1 1.0 %collective-permute-start.2 = (f32[4,5,8,128]{3,2,1,0:T(8,128)S(1)}, f32[4,5,8,128]{3,2,1,0:T(8,128)S(1)}, u32[]{:S(2)}, u32[]{:S(2)}) collective-permute-start(f32[4,5,8,128]{3,2,1,0:T(8,128)S(1)} %pad_maximum_fusion.1), channel_id=1, source_target_pairs={{0,32},{8,40},{16,48},{24,56},{32,0},{40,8},{48,16},{56,24},{64,96... | collective-permute-start | bytes 245768 | tf_op jit(solution)/shard_map/ppermute | solution.py:297
  18.1 3.4 %collective-permute-done.2 = f32[4,5,8,128]{3,2,1,0:T(8,128)S(1)} collective-permute-done((f32[4,5,8,128]{3,2,1,0:T(8,128)S(1)}, f32[4,5,8,128]{3,2,1,0:T(8,128)S(1)}, u32[]{:S(2)}, u32[]{:S(2)}) %collective-permute-start.2) | collective-permute-done | bytes 81952 | tf_op jit(solution)/shard_map/ppermute | solution.py:297
  21.5 1.5 %collective-permute-start.3 = (f32[8,5,8,128]{3,2,1,0:T(8,128)S(1)}, f32[8,5,8,128]{3,2,1,0:T(8,128)S(1)}, u32[]{:S(2)}, u32[]{:S(2)}) collective-permute-start(f32[8,5,8,128]{3,2,1,0:T(8,128)S(1)} %pad_maximum_fusion), channel_id=1, source_target_pairs={{0,16},{8,24},{16,0},{24,8},{32,48},{40,56},{48,32},{56,40},{64,80... | collective-permute-start | bytes 491528 | tf_op jit(solution)/shard_map/ppermute | solution.py:297
  23.0 3.9 %collective-permute-done.3 = f32[8,5,8,128]{3,2,1,0:T(8,128)S(1)} collective-permute-done((f32[8,5,8,128]{3,2,1,0:T(8,128)S(1)}, f32[8,5,8,128]{3,2,1,0:T(8,128)S(1)}, u32[]{:S(2)}, u32[]{:S(2)}) %collective-permute-start.3) | collective-permute-done | bytes 163872 | tf_op jit(solution)/shard_map/ppermute | solution.py:297
  27.0 0.1 collective-permute-start.4
  27.1 0.0 copy-start.2
  27.1 9.0 %element.1 = (f32[2,16,128]{2,1,0:T(8,128)}, f32[8,128]{1,0:T(8,128)}) custom-call(f32[2,16,128]{2,1,0:T(8,128)} %bitcast.35, s32[2,256,128]{2,1,0:T(8,128)} %bitcast.33, f32[2,10,64,128]{3,2,1,0:T(8,128)} %bitcast.27, s32[8,128]{1,0:T(8,128)} %bitcast.42), custom_call_target="tpu_custom_call" | custom-call | tf_op jit(solution)/shard_map/element/pallas_call | solution.py:253
  36.1 3.4 %collective-permute-start.5 = (f32[8,128]{1,0:T(8,128)}, f32[8,128]{1,0:T(8,128)S(1)}, u32[]{:S(2)}, u32[]{:S(2)}) collective-permute-start(f32[8,128]{1,0:T(8,128)} %get-tuple-element.9), channel_id=1, source_target_pairs={{0,1},{1,2},{2,3},{3,4},{4,5},{5,6},{6,7},{8,9},{9,10},{10,11},{11... | collective-permute-start | bytes 12296 | tf_op jit(solution)/shard_map/ppermute | solution.py:309
  39.5 1.3 %collective-permute-start.6 = (f32[8,128]{1,0:T(8,128)}, f32[8,128]{1,0:T(8,128)S(1)}, u32[]{:S(2)}, u32[]{:S(2)}) collective-permute-start(f32[8,128]{1,0:T(8,128)} %get-tuple-element.9), channel_id=1, source_target_pairs={{1,0},{2,1},{3,2},{4,3},{5,4},{6,5},{7,6},{9,8},{10,9},{11,10},{12... | collective-permute-start | bytes 12296 | tf_op jit(solution)/shard_map/ppermute | solution.py:310
  40.8 0.0 copy-done.2
  40.8 0.7 %copy.16 = s32[4,8,8,128]{3,2,1,0:T(8,128)} copy(s32[4,8,8,128]{3,1,2,0:T(8,128)S(1)} %bitcast.37) | data formatting | bytes 262144
  41.5 0.6 pad_add_fusion.where
  42.1 0.0 collective-permute-done.4
  42.1 0.0 copy-start
  42.2 0.8 %copy-done = f32[32,5,8,128]{3,2,1,0:T(8,128)} copy-done((f32[32,5,8,128]{3,2,1,0:T(8,128)}, f32[32,5,8,128]{3,2,1,0:T(8,128)S(1)}, u32[]{:S(2)}) %copy-start) | copy-done | bytes 655384
  43.0 13.4 %contact.1 = (f32[8,128]{1,0:T(8,128)}, f32[2,16,128]{2,1,0:T(8,128)}, f32[8,128]{1,0:T(8,128)}) custom-call(s32[2]{0:T(128)} %pad_add_fusion.where, f32[32,5,8,128]{3,2,1,0:T(8,128)} %copy-done, s32[32,8,128]{2,1,0:T(8,128)} %bitcast.28, f32[3,8,128]{2,1,0:T(8,128)} %bitcast.41, s32[8,128]{1,0:T(8,128)} %bitcast.46, f32[8,128]{1,0:T(8,128)} %bitcast.48, ...), custom_call_target="tpu_custom_call" | custom-call | tf_op jit(solution)/shard_map/contact/pallas_call | solution.py:253
  56.4 4.5 %collective-permute-start.7 = (f32[8,128]{1,0:T(8,128)}, f32[8,128]{1,0:T(8,128)S(1)}, u32[]{:S(2)}, u32[]{:S(2)}) collective-permute-start(f32[8,128]{1,0:T(8,128)} %get-tuple-element.10), channel_id=1, source_target_pairs={{0,1},{8,9},{16,17},{24,25},{32,33},{40,41},{48,49},{56,57},{64,65... | collective-permute-start | bytes 12296 | tf_op jit(solution)/shard_map/ppermute | solution.py:320
  60.9 0.0 collective-permute-done.5.from_below
  60.9 0.0 copy-start.3
  60.9 0.0 collective-permute-done.6.from_above
  61.0 0.0 copy-start.4
  61.0 1.5 %collective-permute-done.7.contact_below = f32[8,128]{1,0:T(8,128)S(1)} collective-permute-done((f32[8,128]{1,0:T(8,128)}, f32[8,128]{1,0:T(8,128)S(1)}, u32[]{:S(2)}, u32[]{:S(2)}) %collective-permute-start.7) | collective-permute-done | bytes 4128 | tf_op jit(solution)/shard_map/ppermute | solution.py:320
  62.4 0.0 copy-start.5
  62.5 0.0 copy-done.3
  62.5 0.0 copy-done.4
  62.5 0.6 copy-done.5
  63.0 1.7 %advance.1 = f32[2,16,128]{2,1,0:T(8,128)} custom-call(f32[2,16,128]{2,1,0:T(8,128)} %bitcast.36, f32[2,16,128]{2,1,0:T(8,128)} %bitcast.49, f32[2,16,128]{2,1,0:T(8,128)} %get-tuple-element.7.element, f32[2,16,128]{2,1,0:T(8,128)} %get-tuple-element.8.contact, s32[8,128]{1,0:T(8,128)} %bitcast.44, f32[8,128]{1,0:T(8,128)} %copy-done.3, f32[8,128]{1,0:T(8,128)} %copy-done.4, ...), custom_call_target="tpu_custom_call" | custom-call | tf_op jit(solution)/shard_map/advance/pallas_call | solution.py:253
  (8 shorter events, 0.1 us)
Async XLA Ops:
  2.2 11.9 %copy-start.1 = (f32[5,8,128]{2,1,0:T(8,128)S(1)}, f32[5,8,128]{2,1,0:T(8,128)}, u32[]{:S(2)}) copy-start(f32[5,8,128]{2,1,0:T(8,128)} %packet.1) | copy-start | bytes 61444
  2.2 9.2 %collective-permute-start = (f32[1,5,8,128]{3,2,1,0:T(8,128)}, f32[1,5,8,128]{3,2,1,0:T(8,128)S(1)}, u32[]{:S(2)}, u32[]{:S(2)}) collective-permute-start(f32[1,5,8,128]{3,2,1,0:T(8,128)} %bitcast.29), channel_id=1, source_target_pairs={{0,128},{8,136},{16,144},{24,152},{32,160},{40,168},{48,176},{56,1... | collective-permute-start | bytes 61448 | tf_op jit(solution)/shard_map/ppermute | solution.py:297
  12.2 4.9 %collective-permute-start.1 = (f32[2,5,8,128]{3,2,1,0:T(8,128)S(1)}, f32[2,5,8,128]{3,2,1,0:T(8,128)S(1)}, u32[]{:S(2)}, u32[]{:S(2)}) collective-permute-start(f32[2,5,8,128]{3,2,1,0:T(8,128)S(1)} %pad_maximum_fusion.2), channel_id=1, source_target_pairs={{0,64},{8,72},{16,80},{24,88},{32,96},{40,104},{48,112},{56,120},{... | collective-permute-start | bytes 122888 | tf_op jit(solution)/shard_map/ppermute | solution.py:297
  17.1 4.4 %collective-permute-start.2 = (f32[4,5,8,128]{3,2,1,0:T(8,128)S(1)}, f32[4,5,8,128]{3,2,1,0:T(8,128)S(1)}, u32[]{:S(2)}, u32[]{:S(2)}) collective-permute-start(f32[4,5,8,128]{3,2,1,0:T(8,128)S(1)} %pad_maximum_fusion.1), channel_id=1, source_target_pairs={{0,32},{8,40},{16,48},{24,56},{32,0},{40,8},{48,16},{56,24},{64,96... | collective-permute-start | bytes 245768 | tf_op jit(solution)/shard_map/ppermute | solution.py:297
  21.5 5.4 %collective-permute-start.3 = (f32[8,5,8,128]{3,2,1,0:T(8,128)S(1)}, f32[8,5,8,128]{3,2,1,0:T(8,128)S(1)}, u32[]{:S(2)}, u32[]{:S(2)}) collective-permute-start(f32[8,5,8,128]{3,2,1,0:T(8,128)S(1)} %pad_maximum_fusion), channel_id=1, source_target_pairs={{0,16},{8,24},{16,0},{24,8},{32,48},{40,56},{48,32},{56,40},{64,80... | collective-permute-start | bytes 491528 | tf_op jit(solution)/shard_map/ppermute | solution.py:297
  27.0 15.1 %collective-permute-start.4 = (f32[16,5,8,128]{3,2,1,0:T(8,128)S(1)}, f32[16,5,8,128]{3,2,1,0:T(8,128)S(1)}, u32[]{:S(2)}, u32[]{:S(2)}) collective-permute-start(f32[16,5,8,128]{3,2,1,0:T(8,128)S(1)} %get-tuple-element.14), channel_id=1, source_target_pairs={{0,8},{8,0},{16,24},{24,16},{32,40},{40,32},{48,56},{56,48},{64,72... | collective-permute-start | bytes 983048 | tf_op jit(solution)/shard_map/ppermute | solution.py:297
  27.1 13.7 %copy-start.2 = (s32[32,1024]{1,0:T(8,128)S(1)}, s32[32,1024]{1,0:T(8,128)}, u32[]{:S(2)}) copy-start(s32[32,1024]{1,0:T(8,128)} %param.17) | copy-start | bytes 393220
  36.1 24.9 %collective-permute-start.5 = (f32[8,128]{1,0:T(8,128)}, f32[8,128]{1,0:T(8,128)S(1)}, u32[]{:S(2)}, u32[]{:S(2)}) collective-permute-start(f32[8,128]{1,0:T(8,128)} %get-tuple-element.9), channel_id=1, source_target_pairs={{0,1},{1,2},{2,3},{3,4},{4,5},{5,6},{6,7},{8,9},{9,10},{10,11},{11... | collective-permute-start | bytes 12296 | tf_op jit(solution)/shard_map/ppermute | solution.py:309
  39.5 21.5 %collective-permute-start.6 = (f32[8,128]{1,0:T(8,128)}, f32[8,128]{1,0:T(8,128)S(1)}, u32[]{:S(2)}, u32[]{:S(2)}) collective-permute-start(f32[8,128]{1,0:T(8,128)} %get-tuple-element.9), channel_id=1, source_target_pairs={{1,0},{2,1},{3,2},{4,3},{5,4},{6,5},{7,6},{9,8},{10,9},{11,10},{12... | collective-permute-start | bytes 12296 | tf_op jit(solution)/shard_map/ppermute | solution.py:310
  42.1 0.8 %copy-start = (f32[32,5,8,128]{3,2,1,0:T(8,128)}, f32[32,5,8,128]{3,2,1,0:T(8,128)S(1)}, u32[]{:S(2)}) copy-start(f32[32,5,8,128]{3,2,1,0:T(8,128)S(1)} %constant_dynamic-update-slice_fusion.5.packets) | copy-start | bytes 1966084
  56.4 6.1 %collective-permute-start.7 = (f32[8,128]{1,0:T(8,128)}, f32[8,128]{1,0:T(8,128)S(1)}, u32[]{:S(2)}, u32[]{:S(2)}) collective-permute-start(f32[8,128]{1,0:T(8,128)} %get-tuple-element.10), channel_id=1, source_target_pairs={{0,1},{8,9},{16,17},{24,25},{32,33},{40,41},{48,49},{56,57},{64,65... | collective-permute-start | bytes 12296 | tf_op jit(solution)/shard_map/ppermute | solution.py:320
  60.9 1.5 %copy-start.3 = (f32[8,128]{1,0:T(8,128)}, f32[8,128]{1,0:T(8,128)S(1)}, u32[]{:S(2)}) copy-start(f32[8,128]{1,0:T(8,128)S(1)} %collective-permute-done.5.from_below) | copy-start | bytes 12292
  61.0 1.5 %copy-start.4 = (f32[8,128]{1,0:T(8,128)}, f32[8,128]{1,0:T(8,128)S(1)}, u32[]{:S(2)}) copy-start(f32[8,128]{1,0:T(8,128)S(1)} %collective-permute-done.6.from_above) | copy-start | bytes 12292
  62.4 0.6 copy-start.5

commit v2 on v1

v2 whole, which is shorter than its diff:
```python
import functools

import jax
import jax.numpy as jnp
from jax import lax
from jax.experimental import pallas as pl
from jax.experimental.pallas import tpu as pltpu
from jax.sharding import PartitionSpec as P

increment_factor = 0.05
nitsche = 1.0
film_floor = 0.25

LANES = 128
ROWS = 8
LOW = 64
AHEAD = (-1, 0, 1, -4, -3, -2, 2, 3)
OWN = 1


def lane_lookup(row_of, indices, row_total):
    lane = indices & (LANES - 1)
    row = indices >> 7
    level = [
        jnp.take_along_axis(row_of(r), lane, axis=1, mode="promise_in_bounds")
        for r in range(row_total)
    ]
    bit = 0
    while len(level) > 1:
        odd = ((row >> bit) & 1) == 1
        level = [jnp.where(odd, level[k + 1], level[k]) for k in range(0, len(level), 2)]
        bit += 1
    return level[0]


def wide(ref, row, *lead):
    return ref[(*lead, pl.ds(row, ROWS, stride=0), slice(None))]


def split(values):
    coarse = values.astype(jnp.bfloat16).astype(jnp.float32)
    fine = (values - coarse).astype(jnp.bfloat16).astype(jnp.float32)
    return coarse, fine


def double(tile):
    return jnp.concatenate([tile, tile], axis=0).astype(jnp.bfloat16)


def keys(total, interleaved=False):
    out = []
    for k in range(total // 16):
        halves = []
        for h in range(2):
            place = lax.broadcasted_iota(jnp.int32, (ROWS, LANES), 0) + (16 * k + ROWS * h)
            if interleaved:
                place = (place % (total // 2)) * 2 + place // (total // 2)
            halves.append(place.astype(jnp.float32))
        out.append(jnp.concatenate(halves, axis=0).astype(jnp.bfloat16))
    return out


def scatter_operands(index, coarse, fine, highs, lows):
    high = double((index >> 6).astype(jnp.float32))
    low = double((index & (LOW - 1)).astype(jnp.float32))
    coarse = double(coarse)
    fine = double(fine)
    zero = jnp.zeros((16, LANES), jnp.bfloat16)
    one = jnp.ones((16, LANES), jnp.bfloat16)
    hit = [high == key for key in highs]
    values = [jnp.where(h, coarse, zero) for h in hit] + [jnp.where(h, fine, zero) for h in hit]
    one_hot = [jnp.where(low == key, one, zero) for key in lows]
    return jnp.concatenate(values, axis=0), jnp.concatenate(one_hot, axis=0)


def contract(slices):
    values = jnp.concatenate([s[0] for s in slices], axis=1)
    one_hot = jnp.concatenate([s[1] for s in slices], axis=1)
    return lax.dot_general(
        values, one_hot, (((1,), (1,)), ((), ())), preferred_element_type=jnp.float32
    )


def store_nodal(ref, lead, total, sign=1.0):
    high_total = total.shape[0] // 2
    both = (total[:high_total] + total[high_total:]) * sign
    half = high_total // 2
    ref[(*lead, slice(0, half), slice(0, LOW))] = both[:half]
    ref[(*lead, slice(0, half), slice(LOW, LANES))] = both[half:]


def packet_kernel(field, corners, motion, engaged, gaps, factor, out):
    trace = []
    for body in range(2):
        picked = [
            lane_lookup(lambda r: wide(field, r, body), corners[body, c], 16) for c in range(3)
        ]
        trace.append((picked[0] + picked[1] + picked[2]) / 3.0)
    out[0, 0] = motion[...]
    out[0, 1] = trace[1]
    out[0, 2] = trace[0]
    out[0, 3] = engaged[...].astype(jnp.float32) * factor[...]
    out[0, 4] = gaps[2] + nitsche * (gaps[0] - gaps[1])


def element_kernel(body, field, vertices, entries, out, coarse_at, fine_at):
    highs = keys(32, True)
    lows = keys(LOW)
    total = jnp.zeros((64, LOW), jnp.float32)
    order = ((0, 4, 5, 6), (4, 1, 7, 8), (5, 7, 2, 9), (6, 8, 9, 3))
    for j in range(8):
        here = slice(ROWS * j, ROWS * (j + 1))
        corner = [vertices[body, pl.ds(32 * j + c, ROWS, stride=4), :] for c in range(4)]
        picked = [lane_lookup(lambda r: wide(field, r, body), i, 16) for i in corner]
        k = [entries[body, e, here, :] for e in range(10)]
        for c in range(4):
            o = order[c]
            row = (
                k[o[0]] * picked[0]
                + k[o[1]] * picked[1]
                + k[o[2]] * picked[2]
                + k[o[3]] * picked[3]
            )
            coarse, fine = split(row)
            coarse_at[c, here] = coarse
            fine_at[c, here] = fine
        slices = [
            scatter_operands(
                wide(vertices, 32 * j + 4 * s + c, body),
                wide(coarse_at, ROWS * j + s, c),
                wide(fine_at, ROWS * j + s, c),
                highs,
                lows,
            )
            for c in range(4)
            for s in range(ROWS)
        ]
        total = total + contract(slices)
    store_nodal(out, (), total, -1.0)


def rim_lookup(first_row, second_row, index):
    first = lane_lookup(first_row, index, 16)
    second = lane_lookup(second_row, index, 16)
    place = lax.broadcasted_iota(jnp.int32, (ROWS, LANES), 0)
    return jnp.where(place < 4, first, second)


def rim_kernel(disc, pad, rims, out):
    out[...] = rim_lookup(lambda r: wide(disc, r), lambda r: wide(pad, r), rims[...])


def source_of(face, place):
    z = (face >> 2) + AHEAD[place % 8]
    near = (face & 3) ^ ((2 if place & 8 else 0) | (1 if place & 16 else 0))
    return ((z & 7) << 2) | near


def packet_work(face, places, packet_of, own, lookup, normal, trace, total, coarse_at, fine_at):
    highs = keys(16, True)
    lows = keys(LOW)
    mine = lookup[face]
    for group in range(0, len(places), 4):
        slices = []
        for n in range(group, group + 4):
            ref, at = packet_of(places[n])
            source = source_of(face, places[n])
            chosen = (mine >> 10) == source
            local = mine & 1023
            normal = jnp.where(chosen, lane_lookup(lambda r: wide(ref, r, at, 0), local, 8), normal)
            trace = jnp.where(chosen, lane_lookup(lambda r: wide(ref, r, at, 1), local, 8), trace)

            index = lookup[source]
            local = index & 1023
            pad_normal = lane_lookup(lambda r: wide(own, r, 0, 0), local, 8)
            pad_trace = lane_lookup(lambda r: wide(own, r, 0, 1), local, 8)
            rate = (
                ref[at, 3]
                * (film_floor + jnp.maximum(ref[at, 4] - nitsche * pad_normal, 0.0))
                * (pad_trace - ref[at, 2])
            )
            coarse, fine = split(jnp.where((index >> 10) == face, rate, 0.0))
            coarse_at[n] = coarse
            fine_at[n] = fine
            slices += [
                scatter_operands(
                    wide(lookup, s, source) & 1023,
                    wide(coarse_at, s, n),
                    wide(fine_at, s, n),
                    highs,
                    lows,
                )
                for s in range(ROWS)
            ]
        total = total + contract(slices)
    return normal, trace, total


def early_kernel(places, own_first, where, *refs):
    packets, lookup, own = refs[0], refs[1], refs[2]
    before, after, scratch = refs[3:-5], refs[-5:-2], refs[-2:]
    if own_first:
        zero = jnp.zeros((ROWS, LANES), jnp.float32)
        start = (zero, zero, jnp.zeros((32, LOW), jnp.float32))
    else:
        start = tuple(b[...] for b in before)
    done = packet_work(
        where[0], places, lambda p: (packets, p - places[0]), own, lookup, *start, *scratch
    )
    for ref, value in zip(after, done):
        ref[...] = value


def contact_kernel(
    places, where, packets, lookup, own, normal, trace, total, gaps, engaged, factor, corners, rims, disc, pad,
    pressure_out, nodal, rim_out, pads, coarse_at, fine_at,
):
    face = where[0]
    surface = (where[1] == 0).astype(jnp.float32)
    pad_normal, pad_trace, total = packet_work(
        face, places, lambda p: (packets, p - places[0]), own, lookup,
        normal[...], trace[...], total[...], coarse_at, fine_at,
    )
    active = engaged[...].astype(jnp.float32)
    pressure = active * jnp.maximum(gaps[2] + nitsche * (gaps[0] - pad_normal - gaps[1]), 0.0)
    pressure_out[...] = pressure
    disc_rate = (active * factor[...]) * (film_floor + pressure) * (pad_trace - own[0, 2])
    store_nodal(pads, (), total, -1.0)

    highs = keys(32, True)
    lows = keys(LOW)
    for body in range(2):
        rate = disc_rate if body == 0 else pads[...]
        coarse, fine = split(rate / 3.0 * surface)
        at = len(places) + body
        coarse_at[at] = coarse
        fine_at[at] = fine
        slices = [
            scatter_operands(
                wide(corners, s, body, c), wide(coarse_at, s, at), wide(fine_at, s, at), highs, lows
            )
            for c in range(3)
            for s in range(ROWS)
        ]
        store_nodal(nodal, (body,), contract(slices))
        nodal[body] = nodal[body] + (disc if body == 0 else pad)[...]
    rim_out[...] = rim_lookup(lambda r: wide(nodal, r, 0), lambda r: wide(nodal, r, 1), rims[...])


def advance_kernel(where, field, storage, nodal, rims, early, late, out, coarse_at, fine_at):
    highs = keys(32, True)
    lows = keys(LOW)
    place = lax.broadcasted_iota(jnp.int32, (ROWS, LANES), 0)
    even = (where[1] & 1) == 0
    above = jnp.where(even, late[...], early[...])
    below = jnp.where(even, early[...], late[...])
    values = jnp.where((place & 1) == 0, pltpu.roll(below, 7, 0), pltpu.roll(above, 1, 0))
    coarse, fine = split(values)
    coarse_at[...] = coarse
    fine_at[...] = fine
    for body in range(2):
        slices = [
            scatter_operands(wide(rims, s), wide(coarse_at, s), wide(fine_at, s), highs, lows)
            for s in range(4 * body, 4 * body + 4)
        ]
        store_nodal(out, (body,), contract(slices))
    total = nodal[...] + out[...]
    out[...] = field[...] + increment_factor * total / storage[...]


def here(*shape):
    return pltpu.VMEM(shape, jnp.float32)


def near(array):
    return pltpu.with_memory_space_constraint(array, pltpu.VMEM)


def call(body, out, arguments, scratch=(), smem=0, name=None, time=1.0):
    return pl.pallas_call(
        body,
        out_shape=out,
        in_specs=[pl.BlockSpec(memory_space=pltpu.SMEM)] * smem
        + [pl.BlockSpec(memory_space=pltpu.VMEM)] * (len(arguments) - smem),
        out_specs=jax.tree.map(lambda _: pl.BlockSpec(memory_space=pltpu.VMEM), out),
        scratch_shapes=[pltpu.VMEM(s, jnp.float32) for s in scratch],
        name=name,
        cost_estimate=pl.CostEstimate(
            flops=0, transcendentals=0, bytes_accessed=int(time * 3.6e6)
        ),
    )(*arguments)


def local(
    thermal_field,
    lumped_storage,
    simplex_vertices,
    stiffness_entries,
    interface_vertices,
    touching_triangle_vertices,
    partner_lookup,
    engaged_flags,
    rotor_gap_quantities,
    lining_orthogonal_motion,
    touching_transfer_factor,
):
    field = thermal_field.reshape(2, 16, LANES)
    storage = lumped_storage.reshape(2, 16, LANES)
    vertices = simplex_vertices.reshape(2, 4, 64, LANES).transpose(0, 2, 1, 3).reshape(2, 256, LANES)
    entries = stiffness_entries.reshape(2, 10, 64, LANES)
    rims = interface_vertices.reshape(2, 2, 2, LANES).transpose(0, 2, 1, 3).reshape(8, LANES)
    corners = touching_triangle_vertices.reshape(2, 3, ROWS, LANES)
    lookup = partner_lookup.reshape(32, ROWS, LANES)
    engaged = engaged_flags.reshape(ROWS, LANES)
    gaps = rotor_gap_quantities.reshape(3, ROWS, LANES)
    motion = lining_orthogonal_motion.reshape(ROWS, LANES)
    factor = touching_transfer_factor.reshape(ROWS, LANES)
    where = jnp.stack([lax.axis_index("face"), lax.axis_index("depth")]).astype(jnp.int32)
    tile = here(ROWS, LANES)

    def along(cells, step):
        return lax.ppermute(cells, "face", [(i, (i + 4 * step) % 32) for i in range(32)])

    def across(cells, bit):
        return lax.ppermute(cells, "face", [(i, i ^ bit) for i in range(32)])

    def element(body, temperatures):
        return call(
            functools.partial(element_kernel, body),
            here(16, LANES),
            (temperatures, vertices, entries),
            scratch=((4, 64, LANES), (4, 64, LANES)),
            name="element",
            time=2.5,
        )

    own = call(
        packet_kernel,
        here(1, 5, ROWS, LANES),
        (field, corners, motion, engaged, gaps, factor),
        name="packet",
    )
    behind = along(own, 1)
    ahead = along(own, -1)
    disc = element(0, field)
    behind, ahead, disc = lax.optimization_barrier((behind, ahead, disc))
    three = jnp.concatenate([behind, own, ahead], axis=0)
    three, again = lax.optimization_barrier((three, field))
    far_behind = along(three, 3)
    far_ahead = along(three[:2], -3)
    pad = element(1, again)
    far_behind, far_ahead, disc, pad = lax.optimization_barrier((far_behind, far_ahead, disc, pad))
    eight = jnp.concatenate([three, far_behind, far_ahead], axis=0)

    other = across(eight, 2)
    rim_element = call(rim_kernel, tile, (near(disc), near(pad), rims), name="rim", time=0.5)
    early = lax.ppermute(rim_element, "depth", [(1, 2), (2, 1), (3, 4), (4, 3), (5, 6), (6, 5)])
    sums = call(
        functools.partial(early_kernel, tuple(range(8)), True),
        (tile, tile, here(32, LOW)),
        (where, near(eight), lookup, near(own)),
        scratch=((8, ROWS, LANES), (8, ROWS, LANES)),
        smem=1,
        name="first_packets",
    )
    other, sums, early = lax.optimization_barrier((other, sums, early))
    sixteen = jnp.concatenate([eight, other], axis=0)
    last = across(sixteen, 1)
    sums = call(
        functools.partial(early_kernel, tuple(range(8, 16)), False),
        (tile, tile, here(32, LOW)),
        (where, near(other), lookup, near(own), *map(near, sums)),
        scratch=((8, ROWS, LANES), (8, ROWS, LANES)),
        smem=1,
        name="second_packets",
    )
    last, sums = lax.optimization_barrier((last, sums))
    pressure, nodal, rim_total = call(
        functools.partial(contact_kernel, tuple(range(16, 32))),
        (tile, here(2, 16, LANES), tile),
        (
            where, near(last), lookup, near(own), *map(near, sums),
            gaps, engaged, factor, corners, rims, near(disc), near(pad),
        ),
        scratch=((ROWS, LANES), (18, ROWS, LANES), (18, ROWS, LANES)),
        smem=1,
        name="contact",
    )
    late = lax.ppermute(rim_total, "depth", [(i, i ^ 1) for i in range(8)])
    advanced = call(
        advance_kernel,
        jax.ShapeDtypeStruct((2, 16, LANES), jnp.float32),
        (where, field, storage, near(nodal), rims, near(early), near(late)),
        scratch=((ROWS, LANES), (ROWS, LANES)),
        smem=1,
        name="advance",
    )
    return advanced.reshape(thermal_field.shape), pressure.reshape(1, 1024)


def solution(mesh):
    placed = (
        P(None, "face", "depth", None),
        P(None, "face", "depth", None),
        P(None, "face", "depth", None, None),
        P(None, "face", "depth", None, None),
        P(None, "face", "depth", None, None),
        P(None, "face", None, None),
        P(),
        P("face", None),
        P(None, "face", None),
        P("face", None),
        P("face", None),
    )
    return jax.shard_map(
        local,
        mesh=mesh,
        in_specs=placed,
        out_specs=(P(None, "face", "depth", None), P("face", None)),
        check_vma=False,
    )
```

time: 65.8 us -> 42.2 us (0.64)
  the two profiles are of different devices: /device:TPU:8 before, /device:TPU:38 now
where the time goes in v2:
time: 42.2 us; the launch traced here: 41.8 us
  Pallas kernels  14.2 us (34%)
  starting transfers between devices  13.8 us (33%)
  waiting for transfers between devices  11.2 us (27%)
  local copies, waits for them, and re-layouts  1.28 us (3%)
  between operations  0.71 us (2%)
  other arithmetic  0.69 us (2%)
    pallas_call x8, Pallas kernels, call(): pl.pallas_call(body, out_shape=out, in_specs=[pl.BlockSpec(memory_space=p...  14.2 us
    ppermute x4, starting transfers between devices, along(): lax.ppermute(cells, 'face', [(i, (i + 4 * step) % 32) for i in range(32)])  7.21 us
    ppermute x4, waiting for transfers between devices, along(): lax.ppermute(cells, 'face', [(i, (i + 4 * step) % 32) for i in range(32)])  6.38 us
    ppermute x1, starting transfers between devices, local(): lax.ppermute(rim_element, 'depth', [(1, 2), (2, 1), (3, 4), (4, 3), (5, 6...  4.72 us
    ppermute x1, waiting for transfers between devices, local(): late = lax.ppermute(rim_total, 'depth', [(i, i ^ 1) for i in range(8)])  3.01 us
    ppermute x2, starting transfers between devices, across(): return lax.ppermute(cells, 'face', [(i, i ^ bit) for i in range(32)])  1.76 us
    ppermute x1, waiting for transfers between devices, local(): lax.ppermute(rim_element, 'depth', [(1, 2), (2, 1), (3, 4), (4, 3), (5, 6...  1.62 us
    unnamed x6, local copies, waits for them, and re-layouts  1.27 us
  transfers between devices with their start and end apart: 8, of which 5 were waited for; matrix products, arithmetic and copies ran while one was open for 5% of the time, Pallas kernels for 22%

profile of v2, /device:TPU:38, one launch (start us, length us, event | category | flops | bytes accessed | tf_op | source)
XLA Modules:
  0.0 41.8 jit_solution(12894249745761576702)
XLA Ops:
  0.6 1.0 %packet.1.refs_2_.own = f32[1,5,8,128]{3,2,1,0:T(8,128)S(1)} custom-call(f32[2,16,128]{2,1,0:T(8,128)} %bitcast.32, s32[2,3,8,128]{3,2,1,0:T(8,128)} %bitcast.37, f32[8,128]{1,0:T(8,128)} %bitcast.50, s32[8,128]{1,0:T(8,128)} %bitcast.46, f32[3,8,128]{2,1,0:T(8,128)} %bitcast.39, f32[8,128]{1,0:T(8,128)} %bitcast.48), custom_call_target="tpu_custom_call" | custom-call | bytes 3600000 | tf_op jit(solution)/shard_map/packet/pallas_call | solution.py:280
  1.6 0.2 collective-permute-start.1
  1.8 1.9 %collective-permute-start = (f32[1,5,8,128]{3,2,1,0:T(8,128)S(1)}, f32[1,5,8,128]{3,2,1,0:T(8,128)S(1)}, u32[]{:S(2)}, u32[]{:S(2)}) collective-permute-start(f32[1,5,8,128]{3,2,1,0:T(8,128)S(1)} %packet.1.refs_2_.own), channel_id=1, source_target_pairs={{0,32},{8,40},{16,48},{24,56},{32,64},{40,72},{48,80},{56,88},{64,... | collective-permute-start | bytes 61448 | tf_op jit(solution)/shard_map/ppermute | solution.py:322
  3.7 2.7 %element.2.disc = f32[16,128]{1,0:T(8,128)S(1)} custom-call(f32[2,16,128]{2,1,0:T(8,128)} %bitcast.33, s32[2,256,128]{2,1,0:T(8,128)} %bitcast.30, f32[2,10,64,128]{3,2,1,0:T(8,128)} %bitcast.25), custom_call_target="tpu_custom_call" | custom-call | bytes 9000000 | tf_op jit(solution)/shard_map/element/pallas_call | solution.py:280
  6.4 0.0 collective-permute-done.1
  6.4 3.0 %collective-permute-done = f32[1,5,8,128]{3,2,1,0:T(8,128)S(1)} collective-permute-done((f32[1,5,8,128]{3,2,1,0:T(8,128)S(1)}, f32[1,5,8,128]{3,2,1,0:T(8,128)S(1)}, u32[]{:S(2)}, u32[]{:S(2)}) %collective-permute-start) | collective-permute-done | bytes 20512 | tf_op jit(solution)/shard_map/ppermute | solution.py:322
  9.4 3.3 %collective-permute-start.2 = (f32[3,5,8,128]{3,2,1,0:T(8,128)S(1)}, f32[3,5,8,128]{3,2,1,0:T(8,128)S(1)}, u32[]{:S(2)}, u32[]{:S(2)}) collective-permute-start(f32[3,5,8,128]{3,2,1,0:T(8,128)S(1)} %pad_maximum_fusion.1), channel_id=1, source_target_pairs={{0,96},{8,104},{16,112},{24,120},{32,128},{40,136},{48,144},{56,15... | collective-permute-start | bytes 184328 | tf_op jit(solution)/shard_map/ppermute | solution.py:322
  12.7 1.8 %collective-permute-start.3 = (f32[2,5,8,128]{3,2,1,0:T(8,128)S(1)}, f32[2,5,8,128]{3,2,1,0:T(8,128)S(1)}, u32[]{:S(2)}, u32[]{:S(2)}) collective-permute-start(f32[2,5,8,128]{3,2,1,0:T(8,128)S(1)} %slice.3), channel_id=1, source_target_pairs={{0,160},{8,168},{16,176},{24,184},{32,192},{40,200},{48,208},{56,2... | collective-permute-start | bytes 122888 | tf_op jit(solution)/shard_map/ppermute | solution.py:322
  14.5 2.7 %element.3.pad = f32[16,128]{1,0:T(8,128)S(1)} custom-call(f32[2,16,128]{2,1,0:T(8,128)} %bitcast.34, s32[2,256,128]{2,1,0:T(8,128)} %bitcast.31, f32[2,10,64,128]{3,2,1,0:T(8,128)} %bitcast.26), custom_call_target="tpu_custom_call" | custom-call | bytes 9000000 | tf_op jit(solution)/shard_map/element/pallas_call | solution.py:280
  17.2 0.0 copy-start
  17.2 3.4 %collective-permute-done.3 = f32[2,5,8,128]{3,2,1,0:T(8,128)S(1)} collective-permute-done((f32[2,5,8,128]{3,2,1,0:T(8,128)S(1)}, f32[2,5,8,128]{3,2,1,0:T(8,128)S(1)}, u32[]{:S(2)}, u32[]{:S(2)}) %collective-permute-start.3) | collective-permute-done | bytes 40992 | tf_op jit(solution)/shard_map/ppermute | solution.py:322
  20.6 0.0 collective-permute-done.2
  20.6 1.7 %collective-permute-start.4 = (f32[8,5,8,128]{3,2,1,0:T(8,128)S(1)}, f32[8,5,8,128]{3,2,1,0:T(8,128)S(1)}, u32[]{:S(2)}, u32[]{:S(2)}) collective-permute-start(f32[8,5,8,128]{3,2,1,0:T(8,128)S(1)} %constant_dynamic-update-slice_fusion.refs_0_), channel_id=1, source_target_pairs={{0,16},{8,24},{16,0},{24,8},{32,48},{40,56},{48,32},{56,40},{64,80... | collective-permute-start | bytes 491528 | tf_op jit(solution)/shard_map/ppermute | solution.py:325
  22.3 0.8 %rim.1 = f32[8,128]{1,0:T(8,128)S(1)} custom-call(f32[16,128]{1,0:T(8,128)S(1)} %element.2.disc, f32[16,128]{1,0:T(8,128)S(1)} %element.3.pad, s32[8,128]{1,0:T(8,128)} %bitcast.41), custom_call_target="tpu_custom_call" | custom-call | bytes 1800000 | tf_op jit(solution)/shard_map/rim/pallas_call | solution.py:280
  23.1 4.7 %collective-permute-start.5 = (f32[8,128]{1,0:T(8,128)S(1)}, f32[8,128]{1,0:T(8,128)S(1)}, u32[]{:S(2)}, u32[]{:S(2)}) collective-permute-start(f32[8,128]{1,0:T(8,128)S(1)} %rim.1), channel_id=1, source_target_pairs={{1,2},{2,1},{3,4},{4,3},{5,6},{6,5},{9,10},{10,9},{11,12},{12,11},... | collective-permute-start | bytes 12296 | tf_op jit(solution)/shard_map/ppermute | solution.py:357
  27.8 0.7 %pad_add_fusion.where = s32[2]{0:T(128)} fusion(s32[1]{0:T(128)} %bitcast.1, s32[1]{0:T(128)} %bitcast), kind=kLoop, calls=%fused_computation.5 | loop fusion | flops 2 | bytes 16 | tf_op jit(solution)/shard_map/stack | solution.py:318
  28.5 0.0 copy-done
  28.5 0.7 %copy.16 = s32[4,8,8,128]{3,2,1,0:T(8,128)} copy(s32[4,8,8,128]{3,1,2,0:T(8,128)S(1)} %bitcast.36) | data formatting | bytes 262144
  29.1 1.4 %first_packets.1 = (f32[8,128]{1,0:T(8,128)S(1)}, f32[8,128]{1,0:T(8,128)S(1)}, f32[32,64]{1,0:T(8,128)S(1)}) custom-call(s32[2]{0:T(128)} %pad_add_fusion.where, f32[8,5,8,128]{3,2,1,0:T(8,128)S(1)} %constant_dynamic-update-slice_fusion.refs_0_, s32[32,8,128]{2,1,0:T(8,128)} %bitcast.27, f32[1,5,8,128]{3,2,1,0:T(8,128)S(1)} %packet.1.refs_2_.own), custom_call_target="tpu_custom_call" | custom-call | bytes 3600000 | tf_op jit(solution)/shard_map/first_packets/pallas_call | solution.py:280
  30.6 1.6 %collective-permute-done.5.early = f32[8,128]{1,0:T(8,128)S(1)} collective-permute-done((f32[8,128]{1,0:T(8,128)S(1)}, f32[8,128]{1,0:T(8,128)S(1)}, u32[]{:S(2)}, u32[]{:S(2)}) %collective-permute-start.5) | collective-permute-done | bytes 4128 | tf_op jit(solution)/shard_map/ppermute | solution.py:357
  32.2 0.0 collective-permute-done.4.refs_0_
  32.2 0.1 collective-permute-start.6
  32.3 1.5 %second_packets.1 = (f32[8,128]{1,0:T(8,128)S(1)}, f32[8,128]{1,0:T(8,128)S(1)}, f32[32,64]{1,0:T(8,128)S(1)}) custom-call(s32[2]{0:T(128)} %pad_add_fusion.where, f32[8,5,8,128]{3,2,1,0:T(8,128)S(1)} %collective-permute-done.4.refs_0_, s32[32,8,128]{2,1,0:T(8,128)} %bitcast.28, f32[1,5,8,128]{3,2,1,0:T(8,128)S(1)} %packet.1.refs_2_.own, ...), custom_call_target="tpu_custom_call" | custom-call | bytes 3600000 | tf_op jit(solution)/shard_map/second_packets/pallas_call | solution.py:280
  33.8 0.2 collective-permute-done.6.packets
  33.9 2.5 %contact.1 = (f32[8,128]{1,0:T(8,128)S(1)}, f32[2,16,128]{2,1,0:T(8,128)S(1)}, f32[8,128]{1,0:T(8,128)S(1)}) custom-call(s32[2]{0:T(128)} %pad_add_fusion.where, f32[16,5,8,128]{3,2,1,0:T(8,128)S(1)} %collective-permute-done.6.packets, s32[32,8,128]{2,1,0:T(8,128)} %bitcast.29, f32[1,5,8,128]{3,2,1,0:T(8,128)S(1)} %packet.1.refs_2_.own, ...), custom_call_target="tpu_custom_call" | custom-call | bytes 3600000 | tf_op jit(solution)/shard_map/contact/pallas_call | solution.py:280
  36.5 0.1 collective-permute-start.7
  36.6 0.6 %copy.19 = f32[1,1024]{1,0:T(1,128)} copy(f32[1,1024]{1,0:T(1,128)S(1)} %bitcast.24) | data formatting | bytes 8192
  37.1 3.0 %collective-permute-done.7.late = f32[8,128]{1,0:T(8,128)S(1)} collective-permute-done((f32[8,128]{1,0:T(8,128)S(1)}, f32[8,128]{1,0:T(8,128)S(1)}, u32[]{:S(2)}, u32[]{:S(2)}) %collective-permute-start.7) | collective-permute-done | bytes 4128 | tf_op jit(solution)/shard_map/ppermute | solution.py:389
  40.2 1.7 %advance.1 = f32[2,16,128]{2,1,0:T(8,128)} custom-call(s32[2]{0:T(128)} %pad_add_fusion.where, f32[2,16,128]{2,1,0:T(8,128)} %bitcast.35, f32[2,16,128]{2,1,0:T(8,128)} %bitcast.44, f32[2,16,128]{2,1,0:T(8,128)S(1)} %get-tuple-element.52.nodal, s32[8,128]{1,0:T(8,128)} %bitcast.43, f32[8,128]{1,0:T(8,128)S(1)} %collective-permute-done.5.early, ...), custom_call_target="tpu_custom_call" | custom-call | bytes 3600000 | tf_op jit(solution)/shard_map/advance/pallas_call | solution.py:280
  (6 shorter events, 0.0 us)
Async XLA Ops:
  1.6 4.8 %collective-permute-start.1 = (f32[1,5,8,128]{3,2,1,0:T(8,128)S(1)}, f32[1,5,8,128]{3,2,1,0:T(8,128)S(1)}, u32[]{:S(2)}, u32[]{:S(2)}) collective-permute-start(f32[1,5,8,128]{3,2,1,0:T(8,128)S(1)} %packet.1.refs_2_.own), channel_id=1, source_target_pairs={{0,224},{8,232},{16,240},{24,248},{32,0},{40,8},{48,16},{56,24},{6... | collective-permute-start | bytes 61448 | tf_op jit(solution)/shard_map/ppermute | solution.py:322
  1.8 7.6 %collective-permute-start = (f32[1,5,8,128]{3,2,1,0:T(8,128)S(1)}, f32[1,5,8,128]{3,2,1,0:T(8,128)S(1)}, u32[]{:S(2)}, u32[]{:S(2)}) collective-permute-start(f32[1,5,8,128]{3,2,1,0:T(8,128)S(1)} %packet.1.refs_2_.own), channel_id=1, source_target_pairs={{0,32},{8,40},{16,48},{24,56},{32,64},{40,72},{48,80},{56,88},{64,... | collective-permute-start | bytes 61448 | tf_op jit(solution)/shard_map/ppermute | solution.py:322
  9.4 11.2 %collective-permute-start.2 = (f32[3,5,8,128]{3,2,1,0:T(8,128)S(1)}, f32[3,5,8,128]{3,2,1,0:T(8,128)S(1)}, u32[]{:S(2)}, u32[]{:S(2)}) collective-permute-start(f32[3,5,8,128]{3,2,1,0:T(8,128)S(1)} %pad_maximum_fusion.1), channel_id=1, source_target_pairs={{0,96},{8,104},{16,112},{24,120},{32,128},{40,136},{48,144},{56,15... | collective-permute-start | bytes 184328 | tf_op jit(solution)/shard_map/ppermute | solution.py:322
  12.7 7.9 %collective-permute-start.3 = (f32[2,5,8,128]{3,2,1,0:T(8,128)S(1)}, f32[2,5,8,128]{3,2,1,0:T(8,128)S(1)}, u32[]{:S(2)}, u32[]{:S(2)}) collective-permute-start(f32[2,5,8,128]{3,2,1,0:T(8,128)S(1)} %slice.3), channel_id=1, source_target_pairs={{0,160},{8,168},{16,176},{24,184},{32,192},{40,200},{48,208},{56,2... | collective-permute-start | bytes 122888 | tf_op jit(solution)/shard_map/ppermute | solution.py:322
  17.2 11.3 %copy-start = (s32[32,1024]{1,0:T(8,128)S(1)}, s32[32,1024]{1,0:T(8,128)}, u32[]{:S(2)}) copy-start(s32[32,1024]{1,0:T(8,128)} %param.17) | copy-start | bytes 393220
  20.6 11.6 %collective-permute-start.4 = (f32[8,5,8,128]{3,2,1,0:T(8,128)S(1)}, f32[8,5,8,128]{3,2,1,0:T(8,128)S(1)}, u32[]{:S(2)}, u32[]{:S(2)}) collective-permute-start(f32[8,5,8,128]{3,2,1,0:T(8,128)S(1)} %constant_dynamic-update-slice_fusion.refs_0_), channel_id=1, source_target_pairs={{0,16},{8,24},{16,0},{24,8},{32,48},{40,56},{48,32},{56,40},{64,80... | collective-permute-start | bytes 491528 | tf_op jit(solution)/shard_map/ppermute | solution.py:325
  23.1 9.1 %collective-permute-start.5 = (f32[8,128]{1,0:T(8,128)S(1)}, f32[8,128]{1,0:T(8,128)S(1)}, u32[]{:S(2)}, u32[]{:S(2)}) collective-permute-start(f32[8,128]{1,0:T(8,128)S(1)} %rim.1), channel_id=1, source_target_pairs={{1,2},{2,1},{3,4},{4,3},{5,6},{6,5},{9,10},{10,9},{11,12},{12,11},... | collective-permute-start | bytes 12296 | tf_op jit(solution)/shard_map/ppermute | solution.py:357
  32.2 1.7 %collective-permute-start.6 = (f32[16,5,8,128]{3,2,1,0:T(8,128)S(1)}, f32[16,5,8,128]{3,2,1,0:T(8,128)S(1)}, u32[]{:S(2)}, u32[]{:S(2)}) collective-permute-start(f32[16,5,8,128]{3,2,1,0:T(8,128)S(1)} %pad_maximum_fusion), channel_id=1, source_target_pairs={{0,8},{8,0},{16,24},{24,16},{32,40},{40,32},{48,56},{56,48},{64,72... | collective-permute-start | bytes 983048 | tf_op jit(solution)/shard_map/ppermute | solution.py:325
  36.5 3.7 %collective-permute-start.7 = (f32[8,128]{1,0:T(8,128)S(1)}, f32[8,128]{1,0:T(8,128)S(1)}, u32[]{:S(2)}, u32[]{:S(2)}) collective-permute-start(f32[8,128]{1,0:T(8,128)S(1)} %get-tuple-element.54), channel_id=1, source_target_pairs={{0,1},{1,0},{2,3},{3,2},{4,5},{5,4},{6,7},{7,6},{8,9},{9,8},{10,11... | collective-permute-start | bytes 12296 | tf_op jit(solution)/shard_map/ppermute | solution.py:389

commit v3 on v2

v3 whole, which is shorter than its diff:
```python
import functools

import jax
import jax.numpy as jnp
from jax import lax
from jax.experimental import pallas as pl
from jax.experimental.pallas import tpu as pltpu
from jax.sharding import PartitionSpec as P

increment_factor = 0.05
nitsche = 1.0
film_floor = 0.25

LANES = 128
ROWS = 8
LOW = 64
AHEAD = (-3, 0, 3, -4, -1, 2, -2, 1)


def lane_lookup(row_of, indices, row_total):
    lane = indices & (LANES - 1)
    row = indices >> 7
    level = [
        jnp.take_along_axis(row_of(r), lane, axis=1, mode="promise_in_bounds")
        for r in range(row_total)
    ]
    bit = 0
    while len(level) > 1:
        odd = ((row >> bit) & 1) == 1
        level = [jnp.where(odd, level[k + 1], level[k]) for k in range(0, len(level), 2)]
        bit += 1
    return level[0]


def wide(ref, row, *lead):
    return ref[(*lead, pl.ds(row, ROWS, stride=0), slice(None))]


def split(values):
    coarse = values.astype(jnp.bfloat16).astype(jnp.float32)
    fine = (values - coarse).astype(jnp.bfloat16).astype(jnp.float32)
    return coarse, fine


def double(tile):
    return jnp.concatenate([tile, tile], axis=0).astype(jnp.bfloat16)


def keys(total, interleaved=False):
    out = []
    for k in range(total // 16):
        halves = []
        for h in range(2):
            place = lax.broadcasted_iota(jnp.int32, (ROWS, LANES), 0) + (16 * k + ROWS * h)
            if interleaved:
                place = (place % (total // 2)) * 2 + place // (total // 2)
            halves.append(place.astype(jnp.float32))
        out.append(jnp.concatenate(halves, axis=0).astype(jnp.bfloat16))
    return out


def scatter_operands(index, coarse, fine, highs, lows):
    high = double((index >> 6).astype(jnp.float32))
    low = double((index & (LOW - 1)).astype(jnp.float32))
    coarse = double(coarse)
    fine = double(fine)
    zero = jnp.zeros((16, LANES), jnp.bfloat16)
    one = jnp.ones((16, LANES), jnp.bfloat16)
    hit = [high == key for key in highs]
    values = [jnp.where(h, coarse, zero) for h in hit] + [jnp.where(h, fine, zero) for h in hit]
    one_hot = [jnp.where(low == key, one, zero) for key in lows]
    return jnp.concatenate(values, axis=0), jnp.concatenate(one_hot, axis=0)


def contract(slices):
    values = jnp.concatenate([s[0] for s in slices], axis=1)
    one_hot = jnp.concatenate([s[1] for s in slices], axis=1)
    return lax.dot_general(
        values, one_hot, (((1,), (1,)), ((), ())), preferred_element_type=jnp.float32
    )


def store_nodal(ref, lead, total, sign=1.0):
    high_total = total.shape[0] // 2
    both = (total[:high_total] + total[high_total:]) * sign
    half = high_total // 2
    ref[(*lead, slice(0, half), slice(0, LOW))] = both[:half]
    ref[(*lead, slice(0, half), slice(LOW, LANES))] = both[half:]


def packet_kernel(field, corners, motion, engaged, gaps, factor, out, corners_out):
    trace = []
    for body in range(2):
        picked = [
            lane_lookup(lambda r: wide(field, r, body), corners[body, c], 16) for c in range(3)
        ]
        trace.append((picked[0] + picked[1] + picked[2]) / 3.0)
    out[0, 0] = motion[...]
    out[0, 1] = trace[1]
    out[0, 2] = trace[0]
    out[0, 3] = engaged[...].astype(jnp.float32) * factor[...]
    out[0, 4] = gaps[2] + nitsche * (gaps[0] - gaps[1])
    corners_out[...] = corners[...]


def element_sum(field, vertices, entries, out, coarse_at, fine_at):
    highs = keys(32, True)
    lows = keys(LOW)
    total = jnp.zeros((64, LOW), jnp.float32)
    order = ((0, 4, 5, 6), (4, 1, 7, 8), (5, 7, 2, 9), (6, 8, 9, 3))
    for j in range(8):
        here = slice(ROWS * j, ROWS * (j + 1))
        corner = [vertices[0, pl.ds(32 * j + c, ROWS, stride=4), :] for c in range(4)]
        picked = [lane_lookup(lambda r: wide(field, r, 0), i, 16) for i in corner]
        k = [entries[0, e, here, :] for e in range(10)]
        for c in range(4):
            o = order[c]
            row = (
                k[o[0]] * picked[0]
                + k[o[1]] * picked[1]
                + k[o[2]] * picked[2]
                + k[o[3]] * picked[3]
            )
            coarse, fine = split(row)
            coarse_at[c, here] = coarse
            fine_at[c, here] = fine
        slices = [
            scatter_operands(
                wide(vertices, 32 * j + 4 * s + c, 0),
                wide(coarse_at, ROWS * j + s, c),
                wide(fine_at, ROWS * j + s, c),
                highs,
                lows,
            )
            for c in range(4)
            for s in range(ROWS)
        ]
        total = total + contract(slices)
    store_nodal(out, (), total, -1.0)


def disc_kernel(field, vertices, entries, partners, out, lookup, coarse_at, fine_at):
    for g in range(4):
        for s in range(ROWS):
            lookup[pl.ds(64 * g + s, ROWS, stride=ROWS), :] = partners[
                ROWS * g : ROWS * (g + 1), LANES * s : LANES * (s + 1)
            ]
    element_sum(field, vertices, entries, out, coarse_at, fine_at)


def rim_lookup(first_row, second_row, index):
    first = lane_lookup(first_row, index, 16)
    second = lane_lookup(second_row, index, 16)
    place = lax.broadcasted_iota(jnp.int32, (ROWS, LANES), 0)
    return jnp.where(place < 4, first, second)


def pad_kernel(
    field, vertices, entries, rims, whole, storage, disc,
    out, rim_out, rims_out, slot_out, field_out, storage_out, coarse_at, fine_at,
):
    rims_out[...] = rims[...]
    field_out[...] = whole[...]
    storage_out[...] = storage[...]
    highs = keys(32, True)
    lows = keys(LOW)
    lane = lax.broadcasted_iota(jnp.int32, (ROWS, LANES), 1)
    for body in range(2):
        slices = []
        for s in range(4):
            coarse, fine = split((lane + (LANES * s + 1)).astype(jnp.float32))
            slices.append(scatter_operands(wide(rims, 4 * body + s), coarse, fine, highs, lows))
        store_nodal(slot_out, (body,), contract(slices))
    element_sum(field, vertices, entries, out, coarse_at, fine_at)
    rim_out[...] = rim_lookup(lambda r: wide(disc, r), lambda r: wide(out, r), rims[...])


def source_of(face, place):
    z = (face >> 2) + AHEAD[place % 8]
    near = (face & 3) ^ ((2 if place & 8 else 0) | (1 if place & 16 else 0))
    return ((z & 7) << 2) | near


def packet_work(face, packets, own, lookup, normal, trace, total, coarse_at, fine_at):
    highs = keys(16, True)
    lows = keys(LOW)
    mine = lookup[pl.ds(pl.multiple_of(face * ROWS, ROWS), ROWS), :]
    n = 0
    for ref, first in packets:
        for group in range(0, 8, 4):
            slices = []
            for at in range(group, group + 4):
                source = source_of(face, first + at)
                chosen = (mine >> 10) == source
                local = mine & 1023
                normal = jnp.where(chosen, lane_lookup(lambda r: wide(ref, r, at, 0), local, 8), normal)
                trace = jnp.where(chosen, lane_lookup(lambda r: wide(ref, r, at, 1), local, 8), trace)

                index = lookup[pl.ds(pl.multiple_of(source * ROWS, ROWS), ROWS), :]
                local = index & 1023
                pad_normal = lane_lookup(lambda r: wide(own, r, 0, 0), local, 8)
                pad_trace = lane_lookup(lambda r: wide(own, r, 0, 1), local, 8)
                rate = (
                    ref[at, 3]
                    * (film_floor + jnp.maximum(ref[at, 4] - nitsche * pad_normal, 0.0))
                    * (pad_trace - ref[at, 2])
                )
                coarse, fine = split(jnp.where((index >> 10) == face, rate, 0.0))
                coarse_at[n] = coarse
                fine_at[n] = fine
                slices += [
                    scatter_operands(
                        wide(lookup, source * ROWS + s) & 1023,
                        wide(coarse_at, s, n),
                        wide(fine_at, s, n),
                        highs,
                        lows,
                    )
                    for s in range(ROWS)
                ]
                n += 1
            total = total + contract(slices)
    return normal, trace, total


def first_kernel(eight, twin, lookup, own, normal_out, trace_out, total_out, coarse_at, fine_at):
    zero = jnp.zeros((ROWS, LANES), jnp.float32)
    normal_out[...], trace_out[...], total_out[...] = packet_work(
        lax.axis_index("face"), ((eight, 0), (twin, 16)), own, lookup,
        zero, zero, jnp.zeros((32, LOW), jnp.float32), coarse_at, fine_at,
    )


def second_kernel(
    other, lookup, own, normal, trace, total, normal_out, trace_out, total_out, coarse_at, fine_at
):
    normal_out[...], trace_out[...], total_out[...] = packet_work(
        lax.axis_index("face"), ((other, 8),), own, lookup,
        normal[...], trace[...], total[...], coarse_at, fine_at,
    )


def contact_kernel(
    last, lookup, own, normal, trace, total, corners, rims, disc, pad,
    pressure_out, nodal, rim_out, pads, coarse_at, fine_at,
):
    surface = (lax.axis_index("depth") == 0).astype(jnp.float32)
    pad_normal, pad_trace, total = packet_work(
        lax.axis_index("face"), ((last, 24),), own, lookup,
        normal[...], trace[...], total[...], coarse_at, fine_at,
    )
    weight = own[0, 3]
    pressure = jnp.where(
        weight != 0.0, jnp.maximum(own[0, 4] - nitsche * pad_normal, 0.0), 0.0
    )
    pressure_out[...] = pressure
    disc_rate = weight * (film_floor + pressure) * (pad_trace - own[0, 2])
    store_nodal(pads, (), total, -1.0)

    highs = keys(32, True)
    lows = keys(LOW)
    for body in range(2):
        rate = disc_rate if body == 0 else pads[...]
        coarse, fine = split(rate / 3.0 * surface)
        at = 8 + body
        coarse_at[at] = coarse
        fine_at[at] = fine
        slices = [
            scatter_operands(
                wide(corners, s, body, c), wide(coarse_at, s, at), wide(fine_at, s, at), highs, lows
            )
            for c in range(3)
            for s in range(ROWS)
        ]
        store_nodal(nodal, (body,), contract(slices))
        nodal[body] = nodal[body] + (disc if body == 0 else pad)[...]
    rim_out[...] = rim_lookup(lambda r: wide(nodal, r, 0), lambda r: wide(nodal, r, 1), rims[...])


def advance_kernel(field, storage, nodal, slots, early, late, out, gained):
    place = lax.broadcasted_iota(jnp.int32, (ROWS, LANES), 0)
    even = (lax.axis_index("depth") & 1) == 0
    above = jnp.where(even, late[...], early[...])
    below = jnp.where(even, early[...], late[...])
    gained[...] = jnp.where((place & 1) == 0, pltpu.roll(below, 7, 0), pltpu.roll(above, 1, 0))
    for body in range(2):
        for half in range(2):
            here = slice(ROWS * half, ROWS * (half + 1))
            slot = slots[body, here].astype(jnp.int32)
            found = lane_lookup(
                lambda r: wide(gained, 4 * body + r), jnp.maximum(slot - 1, 0), 4
            )
            total = nodal[body, here] + jnp.where(slot > 0, found, 0.0)
            out[body, here] = field[body, here] + increment_factor * total / storage[body, here]


def here(*shape, dtype=jnp.float32):
    return pltpu.VMEM(shape, dtype)


def near(array):
    return pltpu.with_memory_space_constraint(array, pltpu.VMEM)


def one_body(array, body):
    block = (1,) + array.shape[1:]
    return pl.BlockSpec(block, lambda i: (body,) + (0,) * (len(block) - 1), memory_space=pltpu.VMEM)


def call(body, out, arguments, scratch=(), specs=None, name=None, time=1.0):
    whole = pl.BlockSpec(memory_space=pltpu.VMEM)
    specs = specs or {}
    return pl.pallas_call(
        body,
        out_shape=out,
        in_specs=[specs.get(i, whole) for i in range(len(arguments))],
        out_specs=jax.tree.map(lambda _: whole, out),
        scratch_shapes=[pltpu.VMEM(s, jnp.float32) for s in scratch],
        grid=(1,) if specs else (),
        name=name,
        cost_estimate=pl.CostEstimate(
            flops=0, transcendentals=0, bytes_accessed=int(time * 3.6e6)
        ),
    )(*arguments)


def local(
    thermal_field,
    lumped_storage,
    simplex_vertices,
    stiffness_entries,
    interface_vertices,
    touching_triangle_vertices,
    partner_lookup,
    engaged_flags,
    rotor_gap_quantities,
    lining_orthogonal_motion,
    touching_transfer_factor,
):
    field = thermal_field.reshape(2, 16, LANES)
    storage = lumped_storage.reshape(2, 16, LANES)
    vertices = simplex_vertices.reshape(2, 4, 64, LANES).transpose(0, 2, 1, 3).reshape(2, 256, LANES)
    entries = stiffness_entries.reshape(2, 10, 64, LANES)
    rims = interface_vertices.reshape(2, 2, 2, LANES).transpose(0, 2, 1, 3).reshape(8, LANES)
    corners = touching_triangle_vertices.reshape(2, 3, ROWS, LANES)
    engaged = engaged_flags.reshape(ROWS, LANES)
    gaps = rotor_gap_quantities.reshape(3, ROWS, LANES)
    motion = lining_orthogonal_motion.reshape(ROWS, LANES)
    factor = touching_transfer_factor.reshape(ROWS, LANES)
    tile = here(ROWS, LANES)
    nodes = here(16, LANES)
    sums = (tile, tile, here(32, LOW))

    def along(cells, step):
        return lax.ppermute(cells, "face", [(i, (i + 4 * step) % 32) for i in range(32)])

    def across(cells, bit):
        return lax.ppermute(cells, "face", [(i, i ^ bit) for i in range(32)])

    def of_body(body):
        return {k: one_body(a, body) for k, a in enumerate((field, vertices, entries))}

    parts = ((4, 64, LANES), (4, 64, LANES))
    own, corners = call(
        packet_kernel,
        (here(1, 5, ROWS, LANES), here(2, 3, ROWS, LANES, dtype=jnp.int32)),
        (field, corners, motion, engaged, gaps, factor),
        name="packet",
    )
    behind = along(own, 3)
    ahead = along(own, -3)
    disc, lookup = call(
        disc_kernel,
        (nodes, here(256, LANES, dtype=jnp.int32)),
        (field, vertices, entries, partner_lookup),
        scratch=parts,
        specs=of_body(0),
        name="disc_element",
        time=2.2,
    )
    behind, ahead, disc, lookup = lax.optimization_barrier((behind, ahead, disc, lookup))
    three = jnp.concatenate([behind, own, ahead], axis=0)
    three, again = lax.optimization_barrier((three, field))
    near_behind = along(three, 1)
    near_ahead = along(three[:2], -1)
    pad, rim_element, rims, slots, field_near, storage_near = call(
        pad_kernel,
        (nodes, tile, here(ROWS, LANES, dtype=jnp.int32)) + (here(2, 16, LANES),) * 3,
        (again, vertices, entries, rims, field, storage, near(disc)),
        scratch=parts,
        specs=of_body(1),
        name="pad_element",
        time=2.5,
    )
    near_behind, near_ahead, pad, rim_element = lax.optimization_barrier(
        (near_behind, near_ahead, pad, rim_element)
    )
    eight = jnp.concatenate([three, near_behind, near_ahead], axis=0)

    other = across(eight, 2)
    twin = across(eight, 1)
    early = lax.ppermute(rim_element, "depth", [(1, 2), (2, 1), (3, 4), (4, 3), (5, 6), (6, 5)])
    done = call(
        first_kernel,
        sums,
        (near(eight), near(twin), near(lookup), near(own)),
        scratch=((16, ROWS, LANES), (16, ROWS, LANES)),
        name="first_packets",
        time=1.5,
    )
    other, done, early = lax.optimization_barrier((other, done, early))
    last = across(other, 1)
    done = call(
        second_kernel,
        sums,
        (near(other), near(lookup), near(own), *map(near, done)),
        scratch=((8, ROWS, LANES), (8, ROWS, LANES)),
        name="second_packets",
    )
    last, done = lax.optimization_barrier((last, done))
    pressure, nodal, rim_total = call(
        contact_kernel,
        (tile, here(2, 16, LANES), tile),
        tuple(map(near, (last, lookup, own, *done, corners, rims, disc, pad))),
        scratch=((ROWS, LANES), (10, ROWS, LANES), (10, ROWS, LANES)),
        name="contact",
        time=1.5,
    )
    late = lax.ppermute(rim_total, "depth", [(i, i ^ 1) for i in range(8)])
    advanced = call(
        advance_kernel,
        jax.ShapeDtypeStruct((2, 16, LANES), jnp.float32),
        tuple(map(near, (field_near, storage_near, nodal, slots, early, late))),
        scratch=((ROWS, LANES),),
        name="advance",
    )
    return advanced.reshape(thermal_field.shape), pressure.reshape(1, 1024)


def solution(mesh):
    placed = (
        P(None, "face", "depth", None),
        P(None, "face", "depth", None),
        P(None, "face", "depth", None, None),
        P(None, "face", "depth", None, None),
        P(None, "face", "depth", None, None),
        P(None, "face", None, None),
        P(),
        P("face", None),
        P(None, "face", None),
        P("face", None),
        P("face", None),
    )
    return jax.shard_map(
        local,
        mesh=mesh,
        in_specs=placed,
        out_specs=(P(None, "face", "depth", None), P("face", None)),
        check_vma=False,
    )
```

time: 42.2 us -> 39.5 us (0.936)
  the two profiles are of different devices: /device:TPU:38 before, /device:TPU:6 now
where the time goes in v3:
time: 39.5 us; the launch traced here: 39.3 us
  starting transfers between devices  16.7 us (42%)
  waiting for transfers between devices  11.5 us (29%)
  Pallas kernels  9.79 us (25%)
  between operations  0.75 us (2%)
  local copies, waits for them, and re-layouts  0.62 us (2%)
    ppermute x4, starting transfers between devices, along(): lax.ppermute(cells, 'face', [(i, (i + 4 * step) % 32) for i in range(32)])  10.1 us
    pallas_call x7, Pallas kernels, call(): pl.pallas_call(body, out_shape=out, in_specs=[specs.get(i, whole) for i i...  9.79 us
    ppermute x1, starting transfers between devices, local(): lax.ppermute(rim_element, 'depth', [(1, 2), (2, 1), (3, 4), (4, 3), (5, 6...  4.71 us
    ppermute x4, waiting for transfers between devices, along(): lax.ppermute(cells, 'face', [(i, (i + 4 * step) % 32) for i in range(32)])  4.2 us
    ppermute x1, waiting for transfers between devices, local(): lax.ppermute(rim_element, 'depth', [(1, 2), (2, 1), (3, 4), (4, 3), (5, 6...  3.41 us
    ppermute x1, waiting for transfers between devices, local(): late = lax.ppermute(rim_total, 'depth', [(i, i ^ 1) for i in range(8)])  3 us
    ppermute x3, starting transfers between devices, across(): return lax.ppermute(cells, 'face', [(i, i ^ bit) for i in range(32)])  1.76 us
    ppermute x3, waiting for transfers between devices, across(): return lax.ppermute(cells, 'face', [(i, i ^ bit) for i in range(32)])  0.85 us
  transfers between devices with their start and end apart: 9, of which 4 were waited for; matrix products, arithmetic and copies ran while one was open for 2% of the time, Pallas kernels for 17%

profile of v3, /device:TPU:6, one launch (start us, length us, event | category | flops | bytes accessed | tf_op | source)
XLA Modules:
  0.0 39.3 jit_solution(4772810258970432887)
XLA Ops:
  0.6 1.0 %packet.1 = (f32[1,5,8,128]{3,2,1,0:T(8,128)S(1)}, s32[2,3,8,128]{3,2,1,0:T(8,128)S(1)}) custom-call(f32[2,16,128]{2,1,0:T(8,128)} %bitcast.25, s32[2,3,8,128]{3,2,1,0:T(8,128)} %bitcast.29, f32[8,128]{1,0:T(8,128)} %bitcast.34, s32[8,128]{1,0:T(8,128)} %bitcast.35, f32[3,8,128]{2,1,0:T(8,128)} %bitcast.32, f32[8,128]{1,0:T(8,128)} %bitcast.36), custom_call_target="tpu_custom_call" | custom-call | bytes 3600000 | tf_op jit(solution)/shard_map/packet/pallas_call | solution.py:313
  1.6 6.8 %collective-permute-start.1 = (f32[1,5,8,128]{3,2,1,0:T(8,128)S(1)}, f32[1,5,8,128]{3,2,1,0:T(8,128)S(1)}, u32[]{:S(2)}, u32[]{:S(2)}) collective-permute-start(f32[1,5,8,128]{3,2,1,0:T(8,128)S(1)} %get-tuple-element.40.own), channel_id=1, source_target_pairs={{0,160},{8,168},{16,176},{24,184},{32,192},{40,200},{48,208},{56,2... | collective-permute-start | bytes 61448 | tf_op jit(solution)/shard_map/ppermute | solution.py:355
  8.4 0.0 collective-permute-start
  8.4 2.6 %disc_element.1 = (f32[16,128]{1,0:T(8,128)S(1)}, s32[256,128]{1,0:T(8,128)S(1)}) custom-call(f32[2,16,128]{2,1,0:T(8,128)} %bitcast.26, s32[2,256,128]{2,1,0:T(8,128)} %bitcast.23, f32[2,10,64,128]{3,2,1,0:T(8,128)} %bitcast.21, s32[32,1024]{1,0:T(8,128)} %partners.1), custom_call_target="tpu_custom_call" | custom-call | bytes 7920000 | tf_op jit(solution)/shard_map/disc_element/pallas_call | solution.py:313
  11.0 0.0 collective-permute-done.1
  11.0 4.2 %collective-permute-done = f32[1,5,8,128]{3,2,1,0:T(8,128)S(1)} collective-permute-done((f32[1,5,8,128]{3,2,1,0:T(8,128)S(1)}, f32[1,5,8,128]{3,2,1,0:T(8,128)S(1)}, u32[]{:S(2)}, u32[]{:S(2)}) %collective-permute-start) | collective-permute-done | bytes 20512 | tf_op jit(solution)/shard_map/ppermute | solution.py:355
  15.2 1.1 %collective-permute-start.2 = (f32[3,5,8,128]{3,2,1,0:T(8,128)S(1)}, f32[3,5,8,128]{3,2,1,0:T(8,128)S(1)}, u32[]{:S(2)}, u32[]{:S(2)}) collective-permute-start(f32[3,5,8,128]{3,2,1,0:T(8,128)S(1)} %pad_maximum_fusion), channel_id=1, source_target_pairs={{0,32},{8,40},{16,48},{24,56},{32,64},{40,72},{48,80},{56,88},{64,... | collective-permute-start | bytes 184328 | tf_op jit(solution)/shard_map/ppermute | solution.py:355
  16.3 2.2 %collective-permute-start.3 = (f32[2,5,8,128]{3,2,1,0:T(8,128)S(1)}, f32[2,5,8,128]{3,2,1,0:T(8,128)S(1)}, u32[]{:S(2)}, u32[]{:S(2)}) collective-permute-start(f32[2,5,8,128]{3,2,1,0:T(8,128)S(1)} %slice.3), channel_id=1, source_target_pairs={{0,224},{8,232},{16,240},{24,248},{32,0},{40,8},{48,16},{56,24},{6... | collective-permute-start | bytes 122888 | tf_op jit(solution)/shard_map/ppermute | solution.py:355
  18.6 2.8 %pad_element.1 = (f32[16,128]{1,0:T(8,128)S(1)}, f32[8,128]{1,0:T(8,128)S(1)}, s32[8,128]{1,0:T(8,128)S(1)}, f32[2,16,128]{2,1,0:T(8,128)S(1)}, f32[2,16,128]{2,1,0:T(8,128)S(1)}, /*index=5*/f32[2,16,128]{2,1,0:T(8,128)S(1)}) custom-call(f32[2,16,128]{2,1,0:T(8,128)} %bitcast.27, s32[2,256,128]{2,1,0:T(8,128)} %bitcast.24, f32[2,10,64,128]{3,2,1,0:T(8,128)} %bitcast.22, ...), custom_call_target="tpu_custom_call" | custom-call | bytes 9000000 | tf_op jit(solution)/shard_map/pad_element/pallas_call | solution.py:313
  21.3 0.0 collective-permute-done.3
  21.3 0.0 collective-permute-done.2
  21.4 0.1 collective-permute-start.5
  21.5 1.7 %collective-permute-start.4 = (f32[8,5,8,128]{3,2,1,0:T(8,128)S(1)}, f32[8,5,8,128]{3,2,1,0:T(8,128)S(1)}, u32[]{:S(2)}, u32[]{:S(2)}) collective-permute-start(f32[8,5,8,128]{3,2,1,0:T(8,128)S(1)} %constant_dynamic-update-slice_fusion.eight), channel_id=1, source_target_pairs={{0,16},{8,24},{16,0},{24,8},{32,48},{40,56},{48,32},{56,40},{64,80... | collective-permute-start | bytes 491528 | tf_op jit(solution)/shard_map/ppermute | solution.py:358
  23.1 4.7 %collective-permute-start.6 = (f32[8,128]{1,0:T(8,128)S(1)}, f32[8,128]{1,0:T(8,128)S(1)}, u32[]{:S(2)}, u32[]{:S(2)}) collective-permute-start(f32[8,128]{1,0:T(8,128)S(1)} %get-tuple-element.58), channel_id=1, source_target_pairs={{1,2},{2,1},{3,4},{4,3},{5,6},{6,5},{9,10},{10,9},{11,12},{12,11},... | collective-permute-start | bytes 12296 | tf_op jit(solution)/shard_map/ppermute | solution.py:402
  27.9 0.0 collective-permute-done.5.twin
  27.9 0.9 %first_packets.1 = (f32[8,128]{1,0:T(8,128)S(1)}, f32[8,128]{1,0:T(8,128)S(1)}, f32[32,64]{1,0:T(8,128)S(1)}) custom-call(f32[8,5,8,128]{3,2,1,0:T(8,128)S(1)} %constant_dynamic-update-slice_fusion.eight, f32[8,5,8,128]{3,2,1,0:T(8,128)S(1)} %collective-permute-done.5.twin, s32[256,128]{1,0:T(8,128)S(1)} %get-tuple-element.54.lookup, ...), custom_call_target="tpu_custom_call" | custom-call | bytes 5400000 | tf_op jit(solution)/shard_map/first_packets/pallas_call | solution.py:313
  28.8 3.4 %collective-permute-done.6.early = f32[8,128]{1,0:T(8,128)S(1)} collective-permute-done((f32[8,128]{1,0:T(8,128)S(1)}, f32[8,128]{1,0:T(8,128)S(1)}, u32[]{:S(2)}, u32[]{:S(2)}) %collective-permute-start.6) | collective-permute-done | bytes 4128 | tf_op jit(solution)/shard_map/ppermute | solution.py:402
  32.2 0.0 collective-permute-done.4.other
  32.2 0.0 collective-permute-start.7
  32.2 0.5 %second_packets.1 = (f32[8,128]{1,0:T(8,128)S(1)}, f32[8,128]{1,0:T(8,128)S(1)}, f32[32,64]{1,0:T(8,128)S(1)}) custom-call(f32[8,5,8,128]{3,2,1,0:T(8,128)S(1)} %collective-permute-done.4.other, s32[256,128]{1,0:T(8,128)S(1)} %get-tuple-element.54.lookup, f32[1,5,8,128]{3,2,1,0:T(8,128)S(1)} %get-tuple-element.40.own, ...), custom_call_target="tpu_custom_call" | custom-call | bytes 3600000 | tf_op jit(solution)/shard_map/second_packets/pallas_call | solution.py:313
  32.8 0.8 %collective-permute-done.7.last = f32[8,5,8,128]{3,2,1,0:T(8,128)S(1)} collective-permute-done((f32[8,5,8,128]{3,2,1,0:T(8,128)S(1)}, f32[8,5,8,128]{3,2,1,0:T(8,128)S(1)}, u32[]{:S(2)}, u32[]{:S(2)}) %collective-permute-start.7) | collective-permute-done | bytes 163872 | tf_op jit(solution)/shard_map/ppermute | solution.py:358
  33.6 1.3 %contact.1 = (f32[8,128]{1,0:T(8,128)S(1)}, f32[2,16,128]{2,1,0:T(8,128)S(1)}, f32[8,128]{1,0:T(8,128)S(1)}) custom-call(f32[8,5,8,128]{3,2,1,0:T(8,128)S(1)} %collective-permute-done.7.last, s32[256,128]{1,0:T(8,128)S(1)} %get-tuple-element.54.lookup, f32[1,5,8,128]{3,2,1,0:T(8,128)S(1)} %get-tuple-element.40.own, f32[8,128]{1,0:T(8,128)S(1)} %get-tuple-element.67.normal, ...), custom_call_target="tpu_custom_call" | custom-call | bytes 5400000 | tf_op jit(solution)/shard_map/contact/pallas_call | solution.py:313
  34.9 0.1 collective-permute-start.8
  35.0 0.6 %copy.18 = f32[1,1024]{1,0:T(1,128)} copy(f32[1,1024]{1,0:T(1,128)S(1)} %bitcast.20) | data formatting | bytes 8192
  35.6 3.0 %collective-permute-done.8.late = f32[8,128]{1,0:T(8,128)S(1)} collective-permute-done((f32[8,128]{1,0:T(8,128)S(1)}, f32[8,128]{1,0:T(8,128)S(1)}, u32[]{:S(2)}, u32[]{:S(2)}) %collective-permute-start.8) | collective-permute-done | bytes 4128 | tf_op jit(solution)/shard_map/ppermute | solution.py:429
  38.6 0.7 %advance.1 = f32[2,16,128]{2,1,0:T(8,128)} custom-call(f32[2,16,128]{2,1,0:T(8,128)S(1)} %get-tuple-element.47.field, f32[2,16,128]{2,1,0:T(8,128)S(1)} %get-tuple-element.48.storage, f32[2,16,128]{2,1,0:T(8,128)S(1)} %get-tuple-element.73.nodal, f32[2,16,128]{2,1,0:T(8,128)S(1)} %get-tuple-element.74.slots, f32[8,128]{1,0:T(8,128)S(1)} %collective-permute-done.6.early, ...), custom_call_target="tpu_custom_call" | custom-call | bytes 3600000 | tf_op jit(solution)/shard_map/advance/pallas_call | solution.py:313
  (5 shorter events, 0.0 us)
Async XLA Ops:
  1.6 9.4 %collective-permute-start.1 = (f32[1,5,8,128]{3,2,1,0:T(8,128)S(1)}, f32[1,5,8,128]{3,2,1,0:T(8,128)S(1)}, u32[]{:S(2)}, u32[]{:S(2)}) collective-permute-start(f32[1,5,8,128]{3,2,1,0:T(8,128)S(1)} %get-tuple-element.40.own), channel_id=1, source_target_pairs={{0,160},{8,168},{16,176},{24,184},{32,192},{40,200},{48,208},{56,2... | collective-permute-start | bytes 61448 | tf_op jit(solution)/shard_map/ppermute | solution.py:355
  8.4 6.8 %collective-permute-start = (f32[1,5,8,128]{3,2,1,0:T(8,128)S(1)}, f32[1,5,8,128]{3,2,1,0:T(8,128)S(1)}, u32[]{:S(2)}, u32[]{:S(2)}) collective-permute-start(f32[1,5,8,128]{3,2,1,0:T(8,128)S(1)} %get-tuple-element.40.own), channel_id=1, source_target_pairs={{0,96},{8,104},{16,112},{24,120},{32,128},{40,136},{48,144},{56,15... | collective-permute-start | bytes 61448 | tf_op jit(solution)/shard_map/ppermute | solution.py:355
  15.2 6.1 %collective-permute-start.2 = (f32[3,5,8,128]{3,2,1,0:T(8,128)S(1)}, f32[3,5,8,128]{3,2,1,0:T(8,128)S(1)}, u32[]{:S(2)}, u32[]{:S(2)}) collective-permute-start(f32[3,5,8,128]{3,2,1,0:T(8,128)S(1)} %pad_maximum_fusion), channel_id=1, source_target_pairs={{0,32},{8,40},{16,48},{24,56},{32,64},{40,72},{48,80},{56,88},{64,... | collective-permute-start | bytes 184328 | tf_op jit(solution)/shard_map/ppermute | solution.py:355
  16.3 5.0 %collective-permute-start.3 = (f32[2,5,8,128]{3,2,1,0:T(8,128)S(1)}, f32[2,5,8,128]{3,2,1,0:T(8,128)S(1)}, u32[]{:S(2)}, u32[]{:S(2)}) collective-permute-start(f32[2,5,8,128]{3,2,1,0:T(8,128)S(1)} %slice.3), channel_id=1, source_target_pairs={{0,224},{8,232},{16,240},{24,248},{32,0},{40,8},{48,16},{56,24},{6... | collective-permute-start | bytes 122888 | tf_op jit(solution)/shard_map/ppermute | solution.py:355
  21.4 6.5 %collective-permute-start.5 = (f32[8,5,8,128]{3,2,1,0:T(8,128)S(1)}, f32[8,5,8,128]{3,2,1,0:T(8,128)S(1)}, u32[]{:S(2)}, u32[]{:S(2)}) collective-permute-start(f32[8,5,8,128]{3,2,1,0:T(8,128)S(1)} %constant_dynamic-update-slice_fusion.eight), channel_id=1, source_target_pairs={{0,8},{8,0},{16,24},{24,16},{32,40},{40,32},{48,56},{56,48},{64,72... | collective-permute-start | bytes 491528 | tf_op jit(solution)/shard_map/ppermute | solution.py:358
  21.5 10.8 %collective-permute-start.4 = (f32[8,5,8,128]{3,2,1,0:T(8,128)S(1)}, f32[8,5,8,128]{3,2,1,0:T(8,128)S(1)}, u32[]{:S(2)}, u32[]{:S(2)}) collective-permute-start(f32[8,5,8,128]{3,2,1,0:T(8,128)S(1)} %constant_dynamic-update-slice_fusion.eight), channel_id=1, source_target_pairs={{0,16},{8,24},{16,0},{24,8},{32,48},{40,56},{48,32},{56,40},{64,80... | collective-permute-start | bytes 491528 | tf_op jit(solution)/shard_map/ppermute | solution.py:358
  23.1 9.1 %collective-permute-start.6 = (f32[8,128]{1,0:T(8,128)S(1)}, f32[8,128]{1,0:T(8,128)S(1)}, u32[]{:S(2)}, u32[]{:S(2)}) collective-permute-start(f32[8,128]{1,0:T(8,128)S(1)} %get-tuple-element.58), channel_id=1, source_target_pairs={{1,2},{2,1},{3,4},{4,3},{5,6},{6,5},{9,10},{10,9},{11,12},{12,11},... | collective-permute-start | bytes 12296 | tf_op jit(solution)/shard_map/ppermute | solution.py:402
  32.2 1.4 %collective-permute-start.7 = (f32[8,5,8,128]{3,2,1,0:T(8,128)S(1)}, f32[8,5,8,128]{3,2,1,0:T(8,128)S(1)}, u32[]{:S(2)}, u32[]{:S(2)}) collective-permute-start(f32[8,5,8,128]{3,2,1,0:T(8,128)S(1)} %collective-permute-done.4.other), channel_id=1, source_target_pairs={{0,8},{8,0},{16,24},{24,16},{32,40},{40,32},{48,56},{56,48},{64,72... | collective-permute-start | bytes 491528 | tf_op jit(solution)/shard_map/ppermute | solution.py:358
  34.9 3.7 %collective-permute-start.8 = (f32[8,128]{1,0:T(8,128)S(1)}, f32[8,128]{1,0:T(8,128)S(1)}, u32[]{:S(2)}, u32[]{:S(2)}) collective-permute-start(f32[8,128]{1,0:T(8,128)S(1)} %get-tuple-element.76), channel_id=1, source_target_pairs={{0,1},{1,0},{2,3},{3,2},{4,5},{5,4},{6,7},{7,6},{8,9},{9,8},{10,11... | collective-permute-start | bytes 12296 | tf_op jit(solution)/shard_map/ppermute | solution.py:429

commit v4 on v3

--- a/solution.py
+++ b/solution.py
@@ -14,7 +14,7 @@
 LANES = 128
 ROWS = 8
 LOW = 64
-AHEAD = (-3, 0, 3, -4, -1, 2, -2, 1)
+AHEAD = (-1, 0, 1, -4, -3, -2, 2, 3)
 
 
 def lane_lookup(row_of, indices, row_total):
@@ -103,16 +103,16 @@
     corners_out[...] = corners[...]
 
 
-def element_sum(field, vertices, entries, out, coarse_at, fine_at):
+def element_sum(field, vertices, entries, out, coarse_at, fine_at, body=0):
     highs = keys(32, True)
     lows = keys(LOW)
     total = jnp.zeros((64, LOW), jnp.float32)
     order = ((0, 4, 5, 6), (4, 1, 7, 8), (5, 7, 2, 9), (6, 8, 9, 3))
     for j in range(8):
         here = slice(ROWS * j, ROWS * (j + 1))
-        corner = [vertices[0, pl.ds(32 * j + c, ROWS, stride=4), :] for c in range(4)]
-        picked = [lane_lookup(lambda r: wide(field, r, 0), i, 16) for i in corner]
-        k = [entries[0, e, here, :] for e in range(10)]
+        corner = [vertices[body, pl.ds(32 * j + c, ROWS, stride=4), :] for c in range(4)]
+        picked = [lane_lookup(lambda r: wide(field, r, body), i, 16) for i in corner]
+        k = [entries[body, e, here, :] for e in range(10)]
         for c in range(4):
             o = order[c]
             row = (
@@ -122,13 +122,13 @@
                 + k[o[3]] * picked[3]
             )
             coarse, fine = split(row)
-            coarse_at[c, here] = coarse
-            fine_at[c, here] = fine
+            coarse_at[body, c, here] = coarse
+            fine_at[body, c, here] = fine
         slices = [
             scatter_operands(
-                wide(vertices, 32 * j + 4 * s + c, 0),
-                wide(coarse_at, ROWS * j + s, c),
-                wide(fine_at, ROWS * j + s, c),
+                wide(vertices, 32 * j + 4 * s + c, body),
+                wide(coarse_at, ROWS * j + s, body, c),
+                wide(fine_at, ROWS * j + s, body, c),
                 highs,
                 lows,
             )
@@ -155,13 +155,7 @@
     return jnp.where(place < 4, first, second)
 
 
-def pad_kernel(
-    field, vertices, entries, rims, whole, storage, disc,
-    out, rim_out, rims_out, slot_out, field_out, storage_out, coarse_at, fine_at,
-):
-    rims_out[...] = rims[...]
-    field_out[...] = whole[...]
-    storage_out[...] = storage[...]
+def rim_slots(rims, slot_out):
     highs = keys(32, True)
     lows = keys(LOW)
     lane = lax.broadcasted_iota(jnp.int32, (ROWS, LANES), 1)
@@ -171,8 +165,19 @@
             coarse, fine = split((lane + (LANES * s + 1)).astype(jnp.float32))
             slices.append(scatter_operands(wide(rims, 4 * body + s), coarse, fine, highs, lows))
         store_nodal(slot_out, (body,), contract(slices))
-    element_sum(field, vertices, entries, out, coarse_at, fine_at)
-    rim_out[...] = rim_lookup(lambda r: wide(disc, r), lambda r: wide(out, r), rims[...])
+
+
+def pad_kernel(
+    field, vertices, entries, rims, whole, storage, disc,
+    out, rim_out, rims_out, slot_out, field_out, storage_out, coarse_at, fine_at,
+):
+    rims_out[...] = rims[...]
+    field_out[...] = whole[...]
+    storage_out[...] = storage[...]
+    rim_slots(rims, slot_out)
+    element_sum(field, vertices, entries, out.at[1], coarse_at, fine_at)
+    out[0] = disc[...]
+    rim_out[...] = rim_lookup(lambda r: wide(out, r, 0), lambda r: wide(out, r, 1), rims[...])
 
 
 def source_of(face, place):
@@ -241,10 +246,9 @@
 
 
 def contact_kernel(
-    last, lookup, own, normal, trace, total, corners, rims, disc, pad,
+    last, lookup, own, normal, trace, total, corners, rims, element,
     pressure_out, nodal, rim_out, pads, coarse_at, fine_at,
 ):
-    surface = (lax.axis_index("depth") == 0).astype(jnp.float32)
     pad_normal, pad_trace, total = packet_work(
         lax.axis_index("face"), ((last, 24),), own, lookup,
         normal[...], trace[...], total[...], coarse_at, fine_at,
@@ -261,7 +265,7 @@
     lows = keys(LOW)
     for body in range(2):
         rate = disc_rate if body == 0 else pads[...]
-        coarse, fine = split(rate / 3.0 * surface)
+        coarse, fine = split(rate / 3.0)
         at = 8 + body
         coarse_at[at] = coarse
         fine_at[at] = fine
@@ -273,15 +277,53 @@
             for s in range(ROWS)
         ]
         store_nodal(nodal, (body,), contract(slices))
-        nodal[body] = nodal[body] + (disc if body == 0 else pad)[...]
+        nodal[body] = nodal[body] + element[body]
     rim_out[...] = rim_lookup(lambda r: wide(nodal, r, 0), lambda r: wide(nodal, r, 1), rims[...])
+
+
+def inner_kernel(
+    field, vertices, entries, rims, storage, partners, engaged, gaps, motion,
+    out, rim_out, slot_out, field_out, storage_out, mine, active, gaps_out, normals, coarse_at, fine_at,
+):
+    field_out[...] = field[...]
+    storage_out[...] = storage[...]
+    active[...] = engaged[...].astype(jnp.float32)
+    gaps_out[...] = gaps[...]
+    for patch in range(32):
+        normals[patch] = motion[...]
+    face = lax.axis_index("face")
+    place = lax.broadcasted_iota(jnp.int32, (ROWS, LANES), 0)
+    faces = jnp.zeros((ROWS, LANES), jnp.int32)
+    for s in range(ROWS):
+        block = partners[
+            pl.ds(pl.multiple_of(face & -ROWS, ROWS), ROWS), LANES * s : LANES * (s + 1)
+        ]
+        row = jnp.sum(jnp.where(place == (face & (ROWS - 1)), block, 0), axis=0, keepdims=True)
+        faces = jnp.where(place == s, row, faces)
+    mine[...] = faces
+    rim_slots(rims, slot_out)
+    for body in range(2):
+        element_sum(field, vertices, entries, out.at[body], coarse_at, fine_at, body)
+    rim_out[...] = rim_lookup(lambda r: wide(out, r, 0), lambda r: wide(out, r, 1), rims[...])
+
+
+def pressure_kernel(normals, mine, active, gaps, out):
+    patch = mine[...] >> 10
+    local = mine[...] & 1023
+    normal = jnp.zeros((ROWS, LANES), jnp.float32)
+    for source in range(32):
+        found = lane_lookup(lambda r: wide(normals, r, source), local, 8)
+        normal = jnp.where(patch == source, found, normal)
+    out[...] = active[...] * jnp.maximum(gaps[2] + nitsche * (gaps[0] - normal - gaps[1]), 0.0)
 
 
 def advance_kernel(field, storage, nodal, slots, early, late, out, gained):
     place = lax.broadcasted_iota(jnp.int32, (ROWS, LANES), 0)
-    even = (lax.axis_index("depth") & 1) == 0
-    above = jnp.where(even, late[...], early[...])
-    below = jnp.where(even, early[...], late[...])
+    depth = lax.axis_index("depth")
+    even = (depth & 1) == 0
+    other = jnp.where((depth > 0) & (depth < 7), early[...], 0.0)
+    above = jnp.where(even, late[...], other)
+    below = jnp.where(even, other, late[...])
     gained[...] = jnp.where((place & 1) == 0, pltpu.roll(below, 7, 0), pltpu.roll(above, 1, 0))
     for body in range(2):
         for half in range(2):
@@ -298,8 +340,17 @@
     return pltpu.VMEM(shape, dtype)
 
 
+class Placed:
+    def __init__(self, array, near):
+        self.array, self.near = array, near
+
+    @staticmethod
+    def of(argument):
+        return argument if isinstance(argument, Placed) else Placed(argument, False)
+
+
 def near(array):
-    return pltpu.with_memory_space_constraint(array, pltpu.VMEM)
+    return Placed(array, True)
 
 
 def one_body(array, body):
@@ -310,6 +361,10 @@
 def call(body, out, arguments, scratch=(), specs=None, name=None, time=1.0):
     whole = pl.BlockSpec(memory_space=pltpu.VMEM)
     specs = specs or {}
+    arguments = tuple(
+        pltpu.with_memory_space_constraint(a.array, pltpu.VMEM if a.near else pltpu.HBM)
+        for a in map(Placed.of, arguments)
+    )
     return pl.pallas_call(
         body,
         out_shape=out,
@@ -360,71 +415,102 @@
     def of_body(body):
         return {k: one_body(a, body) for k, a in enumerate((field, vertices, entries))}
 
-    parts = ((4, 64, LANES), (4, 64, LANES))
-    own, corners = call(
-        packet_kernel,
-        (here(1, 5, ROWS, LANES), here(2, 3, ROWS, LANES, dtype=jnp.int32)),
-        (field, corners, motion, engaged, gaps, factor),
-        name="packet",
-    )
-    behind = along(own, 3)
-    ahead = along(own, -3)
-    disc, lookup = call(
-        disc_kernel,
-        (nodes, here(256, LANES, dtype=jnp.int32)),
-        (field, vertices, entries, partner_lookup),
-        scratch=parts,
-        specs=of_body(0),
-        name="disc_element",
-        time=2.2,
-    )
-    behind, ahead, disc, lookup = lax.optimization_barrier((behind, ahead, disc, lookup))
-    three = jnp.concatenate([behind, own, ahead], axis=0)
-    three, again = lax.optimization_barrier((three, field))
-    near_behind = along(three, 1)
-    near_ahead = along(three[:2], -1)
-    pad, rim_element, rims, slots, field_near, storage_near = call(
-        pad_kernel,
-        (nodes, tile, here(ROWS, LANES, dtype=jnp.int32)) + (here(2, 16, LANES),) * 3,
-        (again, vertices, entries, rims, field, storage, near(disc)),
-        scratch=parts,
-        specs=of_body(1),
-        name="pad_element",
-        time=2.5,
-    )
-    near_behind, near_ahead, pad, rim_element = lax.optimization_barrier(
-        (near_behind, near_ahead, pad, rim_element)
-    )
-    eight = jnp.concatenate([three, near_behind, near_ahead], axis=0)
-
-    other = across(eight, 2)
-    twin = across(eight, 1)
-    early = lax.ppermute(rim_element, "depth", [(1, 2), (2, 1), (3, 4), (4, 3), (5, 6), (6, 5)])
-    done = call(
-        first_kernel,
-        sums,
-        (near(eight), near(twin), near(lookup), near(own)),
-        scratch=((16, ROWS, LANES), (16, ROWS, LANES)),
-        name="first_packets",
-        time=1.5,
-    )
-    other, done, early = lax.optimization_barrier((other, done, early))
-    last = across(other, 1)
-    done = call(
-        second_kernel,
-        sums,
-        (near(other), near(lookup), near(own), *map(near, done)),
-        scratch=((8, ROWS, LANES), (8, ROWS, LANES)),
-        name="second_packets",
-    )
-    last, done = lax.optimization_barrier((last, done))
-    pressure, nodal, rim_total = call(
-        contact_kernel,
-        (tile, here(2, 16, LANES), tile),
-        tuple(map(near, (last, lookup, own, *done, corners, rims, disc, pad))),
-        scratch=((ROWS, LANES), (10, ROWS, LANES), (10, ROWS, LANES)),
-        name="contact",
-        time=1.5,
+    parts = ((1, 4, 64, LANES),) * 2
+
+    def elements_and_eight(own):
+        behind = along(own, 1)
+        ahead = along(own, -1)
+        disc, lookup = call(
+            disc_kernel,
+            (nodes, here(256, LANES, dtype=jnp.int32)),
+            (field, vertices, entries, partner_lookup),
+            scratch=parts,
+            specs=of_body(0),
+            name="disc_element",
+            time=2.2,
+        )
+        behind, ahead, disc, lookup = lax.optimization_barrier((behind, ahead, disc, lookup))
+        three = jnp.concatenate([behind, own, ahead], axis=0)
+        three, again = lax.optimization_barrier((three, field))
+        far_behind = along(three, 3)
+        far_ahead = along(three[:2], -3)
+        element, rim_element, rims_near, *kept = call(
+            pad_kernel,
+            (here(2, 16, LANES), tile, here(ROWS, LANES, dtype=jnp.int32))
+            + (here(2, 16, LANES),) * 3,
+            (again, vertices, entries, rims, field, storage, near(disc)),
+            scratch=parts,
+            specs=of_body(1),
+            name="pad_element",
+            time=2.5,
+        )
+        far_behind, far_ahead, element, rim_element = lax.optimization_barrier(
+            (far_behind, far_ahead, element, rim_element)
+        )
+        eight = jnp.concatenate([three, far_behind, far_ahead], axis=0)
+        return eight, lookup, element, rim_element, rims_near, kept
+
+    def surface_block():
+        own, own_corners = call(
+            packet_kernel,
+            (here(1, 5, ROWS, LANES), here(2, 3, ROWS, LANES, dtype=jnp.int32)),
+            (field, corners, motion, engaged, gaps, factor),
+            name="packet",
+        )
+        eight, lookup, element, rim_element, rims_near, kept = elements_and_eight(own)
+        other = across(eight, 2)
+        twin = across(eight, 1)
+        done = call(
+            first_kernel,
+            sums,
+            (near(eight), near(twin), near(lookup), near(own)),
+            scratch=((16, ROWS, LANES), (16, ROWS, LANES)),
+            name="first_packets",
+            time=1.5,
+        )
+        other, done = lax.optimization_barrier((other, done))
+        last = across(other, 1)
+        done = call(
+            second_kernel,
+            sums,
+            (near(other), near(lookup), near(own), *map(near, done)),
+            scratch=((8, ROWS, LANES), (8, ROWS, LANES)),
+            name="second_packets",
+        )
+        last, done = lax.optimization_barrier((last, done))
+        pressure, nodal, rim_total = call(
+            contact_kernel,
+            (tile, here(2, 16, LANES), tile),
+            tuple(map(near, (last, lookup, own, *done, own_corners, rims_near, element))),
+            scratch=((ROWS, LANES), (10, ROWS, LANES), (10, ROWS, LANES)),
+            name="contact",
+            time=1.5,
+        )
+        return pressure, nodal, rim_total, rim_element, *kept
+
+    def inner_block():
+        element, rim_element, *kept, mine, active, gaps_near, normals = call(
+            inner_kernel,
+            (here(2, 16, LANES), tile)
+            + (here(2, 16, LANES),) * 3
+            + (here(ROWS, LANES, dtype=jnp.int32), tile, here(3, ROWS, LANES), here(32, ROWS, LANES)),
+            (field, vertices, entries, rims, storage, partner_lookup, engaged, gaps, motion),
+            scratch=((2, 4, 64, LANES),) * 2,
+            name="inner_elements",
+            time=4.5,
+        )
+        early = lax.ppermute(rim_element, "depth", [(1, 2), (2, 1), (3, 4), (4, 3), (5, 6), (6, 5)])
+        normals = lax.all_to_all(normals, "face", 0, 0, tiled=True)
+        pressure = call(
+            pressure_kernel,
+            tile,
+            tuple(map(near, (normals, mine, active, gaps_near))),
+            name="pressure",
+        )
+        return pressure, element, rim_element, early, *kept
+
+    pressure, nodal, rim_total, early, slots, field_near, storage_near = lax.cond(
+        lax.axis_index("depth") == 0, surface_block, inner_block
     )
     late = lax.ppermute(rim_total, "depth", [(i, i ^ 1) for i in range(8)])
     advanced = call(

time: 39.5 us -> 34.7 us (0.88)
  the two profiles are of different devices: /device:TPU:6 before, /device:TPU:8 now
where the time goes in v4:
time: 34.7 us; the launch traced here: 34.4 us
  starting transfers between devices  11.8 us (34%)
  waiting for transfers between devices  11.4 us (33%)
  Pallas kernels  9.79 us (28%)
  between operations  0.65 us (2%)
  local copies, waits for them, and re-layouts  0.62 us (2%)
    ppermute x4, starting transfers between devices, along(): lax.ppermute(cells, 'face', [(i, (i + 4 * step) % 32) for i in range(32)])  11 us
    pallas_call x7, Pallas kernels, call(): pl.pallas_call(body, out_shape=out, in_specs=[specs.get(i, whole) for i i...  9.79 us
    ppermute x3, waiting for transfers between devices, across(): return lax.ppermute(cells, 'face', [(i, i ^ bit) for i in range(32)])  6.03 us
    ppermute x1, waiting for transfers between devices, local(): late = lax.ppermute(rim_total, 'depth', [(i, i ^ 1) for i in range(8)])  3 us
    ppermute x4, waiting for transfers between devices, along(): lax.ppermute(cells, 'face', [(i, (i + 4 * step) % 32) for i in range(32)])  2.39 us
  transfers between devices with their start and end apart: 8, of which 5 were waited for; matrix products, arithmetic and copies ran while one was open for 2% of the time, Pallas kernels for 20%

profile of v4, /device:TPU:8, one launch (start us, length us, event | category | flops | bytes accessed | tf_op | source)
XLA Modules:
  0.0 34.4 jit_solution(2857284572469527048)
XLA Ops:
  0.6 29.3 %conditional.1 = (f32[2,16,128]{2,1,0:T(8,128)S(1)}, f32[8,128]{1,0:T(8,128)S(1)}, f32[8,128]{1,0:T(8,128)S(1)}, f32[2,16,128]{2,1,0:T(8,128)S(1)}, f32[2,16,128...) conditional(s32[]{:T(128)} %convert_element_type.3, (f32[2,16,128]{2,1,0:T(8,128)}, ...), branch_computations={%region_0.0_spmd, %region_1.0_spmd} | conditional | flops 30720 | bytes 37992336 | solution.py:512
  0.7 1.0 %packet.1 = (f32[1,5,8,128]{3,2,1,0:T(8,128)S(1)}, s32[2,3,8,128]{3,2,1,0:T(8,128)S(1)}) custom-call(f32[2,16,128]{2,1,0:T(8,128)} %get-tuple-element.76.field.whole, s32[2,3,8,128]{3,2,1,0:T(8,128)} %bitcast.33, f32[8,128]{1,0:T(8,128)} %get-tuple-element.63.motion, s32[8,128]{1,0:T(8,128)} %get-tuple-element.64.engaged, ...), custom_call_target="tpu_custom_call" | custom-call | bytes 3600000 | tf_op jit(solution)/shard_map/cond/branch_1_fun/packet/pallas_call | solution.py:368
  1.6 5.9 %collective-permute-start.2 = (f32[1,5,8,128]{3,2,1,0:T(8,128)S(1)}, f32[1,5,8,128]{3,2,1,0:T(8,128)S(1)}, u32[]{:S(2)}, u32[]{:S(2)}) collective-permute-start(f32[1,5,8,128]{3,2,1,0:T(8,128)S(1)} %get-tuple-element.67.own), channel_id=1, source_target_pairs={{0,224},{8,232},{16,240},{24,248},{32,0},{40,8},{48,16},{56,24},{6... | collective-permute-start | bytes 61448 | tf_op jit(solution)/shard_map/cond/branch_1_fun/ppermute | solution.py:410
  7.6 0.0 collective-permute-start.1
  7.6 2.6 %disc_element.1 = (f32[16,128]{1,0:T(8,128)S(1)}, s32[256,128]{1,0:T(8,128)S(1)}) custom-call(f32[2,16,128]{2,1,0:T(8,128)} %get-tuple-element.76.field.whole, s32[2,256,128]{2,1,0:T(8,128)} %get-tuple-element.68.vertices, f32[2,10,64,128]{3,2,1,0:T(8,128)} %get-tuple-element.69.entries, s32[32,1024]{1,0:T(8,128)} %get-tuple-element.70.partners), custom_call_target="tpu_custom_call" | custom-call | bytes 7920000 | tf_op jit(solution)/shard_map/cond/branch_1_fun/disc_element/pallas_call | solution.py:368
  10.2 0.0 collective-permute-done.2
  10.2 2.4 %collective-permute-done.1 = f32[1,5,8,128]{3,2,1,0:T(8,128)S(1)} collective-permute-done((f32[1,5,8,128]{3,2,1,0:T(8,128)S(1)}, f32[1,5,8,128]{3,2,1,0:T(8,128)S(1)}, u32[]{:S(2)}, u32[]{:S(2)}) %collective-permute-start.1) | collective-permute-done | bytes 20512 | tf_op jit(solution)/shard_map/cond/branch_1_fun/ppermute | solution.py:410
  12.6 0.1 collective-permute-start.3
  12.7 5.0 %collective-permute-start.4 = (f32[2,5,8,128]{3,2,1,0:T(8,128)S(1)}, f32[2,5,8,128]{3,2,1,0:T(8,128)S(1)}, u32[]{:S(2)}, u32[]{:S(2)}) collective-permute-start(f32[2,5,8,128]{3,2,1,0:T(8,128)S(1)} %slice.2), channel_id=1, source_target_pairs={{0,160},{8,168},{16,176},{24,184},{32,192},{40,200},{48,208},{56,2... | collective-permute-start | bytes 122888 | tf_op jit(solution)/shard_map/cond/branch_1_fun/ppermute | solution.py:410
  17.7 2.8 %pad_element.1 = (f32[2,16,128]{2,1,0:T(8,128)S(1)}, f32[8,128]{1,0:T(8,128)S(1)}, s32[8,128]{1,0:T(8,128)S(1)}, f32[2,16,128]{2,1,0:T(8,128)S(1)}, f32[2,16,128...) custom-call(f32[2,16,128]{2,1,0:T(8,128)} %get-tuple-element.76.field.whole, s32[2,256,128]{2,1,0:T(8,128)} %get-tuple-element.68.vertices, ...), custom_call_target="tpu_custom_call" | custom-call | bytes 9000000 | tf_op jit(solution)/shard_map/cond/branch_1_fun/pad_element/pallas_call | solution.py:368
  20.4 0.0 collective-permute-done.4
  20.5 0.0 collective-permute-done.3
  20.5 0.1 collective-permute-start.6
  20.6 0.5 %collective-permute-start.5 = (f32[8,5,8,128]{3,2,1,0:T(8,128)S(1)}, f32[8,5,8,128]{3,2,1,0:T(8,128)S(1)}, u32[]{:S(2)}, u32[]{:S(2)}) collective-permute-start(f32[8,5,8,128]{3,2,1,0:T(8,128)S(1)} %constant_dynamic-update-slice_fusion.eight), channel_id=1, source_target_pairs={{0,16},{8,24},{16,0},{24,8},{32,48},{40,56},{48,32},{56,40},{64,80... | collective-permute-start | bytes 491528 | tf_op jit(solution)/shard_map/cond/branch_1_fun/ppermute | solution.py:413
  21.1 0.8 %collective-permute-done.6.twin = f32[8,5,8,128]{3,2,1,0:T(8,128)S(1)} collective-permute-done((f32[8,5,8,128]{3,2,1,0:T(8,128)S(1)}, f32[8,5,8,128]{3,2,1,0:T(8,128)S(1)}, u32[]{:S(2)}, u32[]{:S(2)}) %collective-permute-start.6) | collective-permute-done | bytes 163872 | tf_op jit(solution)/shard_map/cond/branch_1_fun/ppermute | solution.py:413
  22.0 0.9 %first_packets.1 = (f32[8,128]{1,0:T(8,128)S(1)}, f32[8,128]{1,0:T(8,128)S(1)}, f32[32,64]{1,0:T(8,128)S(1)}) custom-call(f32[8,5,8,128]{3,2,1,0:T(8,128)S(1)} %constant_dynamic-update-slice_fusion.eight, f32[8,5,8,128]{3,2,1,0:T(8,128)S(1)} %collective-permute-done.6.twin, s32[256,128]{1,0:T(8,128)S(1)} %get-tuple-element.84.lookup, ...), custom_call_target="tpu_custom_call" | custom-call | bytes 5400000 | tf_op jit(solution)/shard_map/cond/branch_1_fun/first_packets/pallas_call | solution.py:368
  22.9 4.3 %collective-permute-done.5.other = f32[8,5,8,128]{3,2,1,0:T(8,128)S(1)} collective-permute-done((f32[8,5,8,128]{3,2,1,0:T(8,128)S(1)}, f32[8,5,8,128]{3,2,1,0:T(8,128)S(1)}, u32[]{:S(2)}, u32[]{:S(2)}) %collective-permute-start.5) | collective-permute-done | bytes 163872 | tf_op jit(solution)/shard_map/cond/branch_1_fun/ppermute | solution.py:413
  27.3 0.0 collective-permute-start.7
  27.3 0.5 %second_packets.1 = (f32[8,128]{1,0:T(8,128)S(1)}, f32[8,128]{1,0:T(8,128)S(1)}, f32[32,64]{1,0:T(8,128)S(1)}) custom-call(f32[8,5,8,128]{3,2,1,0:T(8,128)S(1)} %collective-permute-done.5.other, s32[256,128]{1,0:T(8,128)S(1)} %get-tuple-element.84.lookup, f32[1,5,8,128]{3,2,1,0:T(8,128)S(1)} %get-tuple-element.67.own, ...), custom_call_target="tpu_custom_call" | custom-call | bytes 3600000 | tf_op jit(solution)/shard_map/cond/branch_1_fun/second_packets/pallas_call | solution.py:368
  27.8 0.9 %collective-permute-done.7.last = f32[8,5,8,128]{3,2,1,0:T(8,128)S(1)} collective-permute-done((f32[8,5,8,128]{3,2,1,0:T(8,128)S(1)}, f32[8,5,8,128]{3,2,1,0:T(8,128)S(1)}, u32[]{:S(2)}, u32[]{:S(2)}) %collective-permute-start.7) | collective-permute-done | bytes 163872 | tf_op jit(solution)/shard_map/cond/branch_1_fun/ppermute | solution.py:413
  28.7 1.3 %contact.1 = (f32[8,128]{1,0:T(8,128)S(1)}, f32[2,16,128]{2,1,0:T(8,128)S(1)}, f32[8,128]{1,0:T(8,128)S(1)}) custom-call(f32[8,5,8,128]{3,2,1,0:T(8,128)S(1)} %collective-permute-done.7.last, s32[256,128]{1,0:T(8,128)S(1)} %get-tuple-element.84.lookup, f32[1,5,8,128]{3,2,1,0:T(8,128)S(1)} %get-tuple-element.67.own, f32[8,128]{1,0:T(8,128)S(1)} %get-tuple-element.96.normal, ...), custom_call_target="tpu_custom_call" | custom-call | bytes 5400000 | tf_op jit(solution)/shard_map/cond/branch_1_fun/contact/pallas_call | solution.py:368
  29.9 0.1 collective-permute-start.8
  30.0 0.6 %copy.41 = f32[1,1024]{1,0:T(1,128)} copy(f32[1,1024]{1,0:T(1,128)S(1)} %get-tuple-element.170) | data formatting | bytes 8192
  30.6 3.0 %collective-permute-done.8.late = f32[8,128]{1,0:T(8,128)S(1)} collective-permute-done((f32[8,128]{1,0:T(8,128)S(1)}, f32[8,128]{1,0:T(8,128)S(1)}, u32[]{:S(2)}, u32[]{:S(2)}) %collective-permute-start.8) | collective-permute-done | bytes 4128 | tf_op jit(solution)/shard_map/ppermute | solution.py:515
  33.6 0.7 %advance.1 = f32[2,16,128]{2,1,0:T(8,128)} custom-call(f32[2,16,128]{2,1,0:T(8,128)S(1)} %get-tuple-element.118.field, f32[2,16,128]{2,1,0:T(8,128)S(1)} %get-tuple-element.119.storage, f32[2,16,128]{2,1,0:T(8,128)S(1)} %get-tuple-element.120.nodal, f32[2,16,128]{2,1,0:T(8,128)S(1)} %get-tuple-element.121.slots, f32[8,128]{1,0:T(8,128)S(1)} %get-tuple-element.122.early, ...), custom_call_target="tpu_custom_call" | custom-call | bytes 3600000 | tf_op jit(solution)/shard_map/advance/pallas_call | solution.py:368
  (5 shorter events, 0.0 us)
Async XLA Ops:
  1.6 8.5 %collective-permute-start.2 = (f32[1,5,8,128]{3,2,1,0:T(8,128)S(1)}, f32[1,5,8,128]{3,2,1,0:T(8,128)S(1)}, u32[]{:S(2)}, u32[]{:S(2)}) collective-permute-start(f32[1,5,8,128]{3,2,1,0:T(8,128)S(1)} %get-tuple-element.67.own), channel_id=1, source_target_pairs={{0,224},{8,232},{16,240},{24,248},{32,0},{40,8},{48,16},{56,24},{6... | collective-permute-start | bytes 61448 | tf_op jit(solution)/shard_map/cond/branch_1_fun/ppermute | solution.py:410
  7.6 5.0 %collective-permute-start.1 = (f32[1,5,8,128]{3,2,1,0:T(8,128)S(1)}, f32[1,5,8,128]{3,2,1,0:T(8,128)S(1)}, u32[]{:S(2)}, u32[]{:S(2)}) collective-permute-start(f32[1,5,8,128]{3,2,1,0:T(8,128)S(1)} %get-tuple-element.67.own), channel_id=1, source_target_pairs={{0,32},{8,40},{16,48},{24,56},{32,64},{40,72},{48,80},{56,88},{64,... | collective-permute-start | bytes 61448 | tf_op jit(solution)/shard_map/cond/branch_1_fun/ppermute | solution.py:410
  12.6 7.9 %collective-permute-start.3 = (f32[3,5,8,128]{3,2,1,0:T(8,128)S(1)}, f32[3,5,8,128]{3,2,1,0:T(8,128)S(1)}, u32[]{:S(2)}, u32[]{:S(2)}) collective-permute-start(f32[3,5,8,128]{3,2,1,0:T(8,128)S(1)} %pad_maximum_fusion), channel_id=1, source_target_pairs={{0,96},{8,104},{16,112},{24,120},{32,128},{40,136},{48,144},{56,15... | collective-permute-start | bytes 184328 | tf_op jit(solution)/shard_map/cond/branch_1_fun/ppermute | solution.py:410
  12.7 7.8 %collective-permute-start.4 = (f32[2,5,8,128]{3,2,1,0:T(8,128)S(1)}, f32[2,5,8,128]{3,2,1,0:T(8,128)S(1)}, u32[]{:S(2)}, u32[]{:S(2)}) collective-permute-start(f32[2,5,8,128]{3,2,1,0:T(8,128)S(1)} %slice.2), channel_id=1, source_target_pairs={{0,160},{8,168},{16,176},{24,184},{32,192},{40,200},{48,208},{56,2... | collective-permute-start | bytes 122888 | tf_op jit(solution)/shard_map/cond/branch_1_fun/ppermute | solution.py:410
  20.5 1.5 %collective-permute-start.6 = (f32[8,5,8,128]{3,2,1,0:T(8,128)S(1)}, f32[8,5,8,128]{3,2,1,0:T(8,128)S(1)}, u32[]{:S(2)}, u32[]{:S(2)}) collective-permute-start(f32[8,5,8,128]{3,2,1,0:T(8,128)S(1)} %constant_dynamic-update-slice_fusion.eight), channel_id=1, source_target_pairs={{0,8},{8,0},{16,24},{24,16},{32,40},{40,32},{48,56},{56,48},{64,72... | collective-permute-start | bytes 491528 | tf_op jit(solution)/shard_map/cond/branch_1_fun/ppermute | solution.py:413
  20.6 6.7 %collective-permute-start.5 = (f32[8,5,8,128]{3,2,1,0:T(8,128)S(1)}, f32[8,5,8,128]{3,2,1,0:T(8,128)S(1)}, u32[]{:S(2)}, u32[]{:S(2)}) collective-permute-start(f32[8,5,8,128]{3,2,1,0:T(8,128)S(1)} %constant_dynamic-update-slice_fusion.eight), channel_id=1, source_target_pairs={{0,16},{8,24},{16,0},{24,8},{32,48},{40,56},{48,32},{56,40},{64,80... | collective-permute-start | bytes 491528 | tf_op jit(solution)/shard_map/cond/branch_1_fun/ppermute | solution.py:413
  27.3 1.4 %collective-permute-start.7 = (f32[8,5,8,128]{3,2,1,0:T(8,128)S(1)}, f32[8,5,8,128]{3,2,1,0:T(8,128)S(1)}, u32[]{:S(2)}, u32[]{:S(2)}) collective-permute-start(f32[8,5,8,128]{3,2,1,0:T(8,128)S(1)} %collective-permute-done.5.other), channel_id=1, source_target_pairs={{0,8},{8,0},{16,24},{24,16},{32,40},{40,32},{48,56},{56,48},{64,72... | collective-permute-start | bytes 491528 | tf_op jit(solution)/shard_map/cond/branch_1_fun/ppermute | solution.py:413
  29.9 3.7 %collective-permute-start.8 = (f32[8,128]{1,0:T(8,128)S(1)}, f32[8,128]{1,0:T(8,128)S(1)}, u32[]{:S(2)}, u32[]{:S(2)}) collective-permute-start(f32[8,128]{1,0:T(8,128)S(1)} %get-tuple-element.123), channel_id=1, source_target_pairs={{0,1},{1,0},{2,3},{3,2},{4,5},{5,4},{6,7},{7,6},{8,9},{9,8},{10,11... | collective-permute-start | bytes 12296 | tf_op jit(solution)/shard_map/ppermute | solution.py:515

commit v5 on v4

--- a/solution.py
+++ b/solution.py
@@ -14,7 +14,7 @@
 LANES = 128
 ROWS = 8
 LOW = 64
-AHEAD = (-1, 0, 1, -4, -3, -2, 2, 3)
+AHEAD = (-1, 0, 1, 2, 3, 4, -3, -2)
 
 
 def lane_lookup(row_of, indices, row_total):
@@ -191,10 +191,10 @@
     lows = keys(LOW)
     mine = lookup[pl.ds(pl.multiple_of(face * ROWS, ROWS), ROWS), :]
     n = 0
-    for ref, first in packets:
-        for group in range(0, 8, 4):
+    for ref, first, count in packets:
+        for group in range(0, count, 4):
             slices = []
-            for at in range(group, group + 4):
+            for at in range(group, min(group + 4, count)):
                 source = source_of(face, first + at)
                 chosen = (mine >> 10) == source
                 local = mine & 1023
@@ -228,19 +228,19 @@
     return normal, trace, total
 
 
-def first_kernel(eight, twin, lookup, own, normal_out, trace_out, total_out, coarse_at, fine_at):
+def first_kernel(eight, twin, three, lookup, own, normal_out, trace_out, total_out, coarse_at, fine_at):
     zero = jnp.zeros((ROWS, LANES), jnp.float32)
     normal_out[...], trace_out[...], total_out[...] = packet_work(
-        lax.axis_index("face"), ((eight, 0), (twin, 16)), own, lookup,
+        lax.axis_index("face"), ((eight, 0, 8), (twin, 16, 8), (three, 8, 3)), own, lookup,
         zero, zero, jnp.zeros((32, LOW), jnp.float32), coarse_at, fine_at,
     )
 
 
 def second_kernel(
-    other, lookup, own, normal, trace, total, normal_out, trace_out, total_out, coarse_at, fine_at
+    three, five, lookup, own, normal, trace, total, normal_out, trace_out, total_out, coarse_at, fine_at
 ):
     normal_out[...], trace_out[...], total_out[...] = packet_work(
-        lax.axis_index("face"), ((other, 8),), own, lookup,
+        lax.axis_index("face"), ((three, 24, 3), (five, 11, 5)), own, lookup,
         normal[...], trace[...], total[...], coarse_at, fine_at,
     )
 
@@ -250,7 +250,7 @@
     pressure_out, nodal, rim_out, pads, coarse_at, fine_at,
 ):
     pad_normal, pad_trace, total = packet_work(
-        lax.axis_index("face"), ((last, 24),), own, lookup,
+        lax.axis_index("face"), ((last, 27, 5),), own, lookup,
         normal[...], trace[...], total[...], coarse_at, fine_at,
     )
     weight = own[0, 3]
@@ -432,8 +432,9 @@
         behind, ahead, disc, lookup = lax.optimization_barrier((behind, ahead, disc, lookup))
         three = jnp.concatenate([behind, own, ahead], axis=0)
         three, again = lax.optimization_barrier((three, field))
-        far_behind = along(three, 3)
-        far_ahead = along(three[:2], -3)
+        far_ahead = along(three, -3)
+        far_behind = along(three[:2], 2)
+        other_three = across(three, 2)
         element, rim_element, rims_near, *kept = call(
             pad_kernel,
             (here(2, 16, LANES), tile, here(ROWS, LANES, dtype=jnp.int32))
@@ -447,8 +448,9 @@
         far_behind, far_ahead, element, rim_element = lax.optimization_barrier(
             (far_behind, far_ahead, element, rim_element)
         )
-        eight = jnp.concatenate([three, far_behind, far_ahead], axis=0)
-        return eight, lookup, element, rim_element, rims_near, kept
+        five = jnp.concatenate([far_ahead, far_behind], axis=0)
+        eight = jnp.concatenate([three, five], axis=0)
+        return eight, five, other_three, lookup, element, rim_element, rims_near, kept
 
     def surface_block():
         own, own_corners = call(
@@ -457,24 +459,27 @@
             (field, corners, motion, engaged, gaps, factor),
             name="packet",
         )
-        eight, lookup, element, rim_element, rims_near, kept = elements_and_eight(own)
-        other = across(eight, 2)
+        eight, five, other_three, lookup, element, rim_element, rims_near, kept = (
+            elements_and_eight(own)
+        )
+        other_five = across(five, 2)
         twin = across(eight, 1)
+        last_three = across(other_three, 1)
         done = call(
             first_kernel,
             sums,
-            (near(eight), near(twin), near(lookup), near(own)),
-            scratch=((16, ROWS, LANES), (16, ROWS, LANES)),
+            (near(eight), near(twin), near(other_three), near(lookup), near(own)),
+            scratch=((19, ROWS, LANES),) * 2,
             name="first_packets",
             time=1.5,
         )
-        other, done = lax.optimization_barrier((other, done))
-        last = across(other, 1)
+        other_five, last_three, done = lax.optimization_barrier((other_five, last_three, done))
+        last = across(other_five, 1)
         done = call(
             second_kernel,
             sums,
-            (near(other), near(lookup), near(own), *map(near, done)),
-            scratch=((8, ROWS, LANES), (8, ROWS, LANES)),
+            (near(last_three), near(other_five), near(lookup), near(own), *map(near, done)),
+            scratch=((8, ROWS, LANES),) * 2,
             name="second_packets",
         )
         last, done = lax.optimization_barrier((last, done))

time: 34.7 us -> 32.8 us (0.945)
  waiting for transfers between devices: 11.4 us -> 8.8 us
  starting transfers between devices: 11.8 us -> 12.3 us
    ppermute x3 -> x5, waiting for transfers between devices: 6.03 us -> 4.2 us  [across(): return lax.ppermute(cells, 'face', [(i, i ^ bit) for i in range(32)])]
    ppermute x4, waiting for transfers between devices: 2.39 us -> 1.61 us  [along(): lax.ppermute(cells, 'face', [(i, (i + 4 * step) % 32) for i in range(32)])]
    ppermute x3 -> x5, starting transfers between devices: 0.63 us -> 1.41 us  [across(): return lax.ppermute(cells, 'face', [(i, i ^ bit) for i in range(32)])]
  transfers between devices with their start and end apart: 8 -> 10, of which waited for: 5 -> 5; matrix products, arithmetic and copies ran while one was open for 2% -> 2% of each run, Pallas kernels for 20% -> 22%
where the time goes in v5:
time: 32.8 us; the launch traced here: 32.6 us
  starting transfers between devices  12.3 us (38%)
  Pallas kernels  9.87 us (30%)
  waiting for transfers between devices  8.8 us (27%)
  between operations  0.65 us (2%)
  local copies, waits for them, and re-layouts  0.62 us (2%)
    ppermute x4, starting transfers between devices, along(): lax.ppermute(cells, 'face', [(i, (i + 4 * step) % 32) for i in range(32)])  10.8 us
    pallas_call x7, Pallas kernels, call(): pl.pallas_call(body, out_shape=out, in_specs=[specs.get(i, whole) for i i...  9.87 us
    ppermute x5, waiting for transfers between devices, across(): return lax.ppermute(cells, 'face', [(i, i ^ bit) for i in range(32)])  4.2 us
    ppermute x1, waiting for transfers between devices, local(): late = lax.ppermute(rim_total, 'depth', [(i, i ^ 1) for i in range(8)])  3 us
    ppermute x4, waiting for transfers between devices, along(): lax.ppermute(cells, 'face', [(i, (i + 4 * step) % 32) for i in range(32)])  1.61 us
    ppermute x5, starting transfers between devices, across(): return lax.ppermute(cells, 'face', [(i, i ^ bit) for i in range(32)])  1.41 us
  transfers between devices with their start and end apart: 10, of which 5 were waited for; matrix products, arithmetic and copies ran while one was open for 2% of the time, Pallas kernels for 22%

profile of v5, /device:TPU:8, one launch (start us, length us, event | category | flops | bytes accessed | tf_op | source)
XLA Modules:
  0.0 32.6 jit_solution(8722899188673260285)
XLA Ops:
  0.6 27.5 %conditional.1 = (f32[2,16,128]{2,1,0:T(8,128)S(1)}, f32[8,128]{1,0:T(8,128)S(1)}, f32[8,128]{1,0:T(8,128)S(1)}, f32[2,16,128]{2,1,0:T(8,128)S(1)}, f32[2,16,128...) conditional(s32[]{:T(128)} %convert_element_type.3, (f32[2,16,128]{2,1,0:T(8,128)}, ...), branch_computations={%region_0.0_spmd, %region_1.0_spmd} | conditional | flops 56320 | bytes 38197216 | solution.py:517
  0.7 1.0 %packet.1 = (f32[1,5,8,128]{3,2,1,0:T(8,128)S(1)}, s32[2,3,8,128]{3,2,1,0:T(8,128)S(1)}) custom-call(f32[2,16,128]{2,1,0:T(8,128)} %get-tuple-element.76.field.whole, s32[2,3,8,128]{3,2,1,0:T(8,128)} %bitcast.33, f32[8,128]{1,0:T(8,128)} %get-tuple-element.63.motion, s32[8,128]{1,0:T(8,128)} %get-tuple-element.64.engaged, ...), custom_call_target="tpu_custom_call" | custom-call | bytes 3600000 | tf_op jit(solution)/shard_map/cond/branch_1_fun/packet/pallas_call | solution.py:368
  1.6 2.0 %collective-permute-start.1 = (f32[1,5,8,128]{3,2,1,0:T(8,128)S(1)}, f32[1,5,8,128]{3,2,1,0:T(8,128)S(1)}, u32[]{:S(2)}, u32[]{:S(2)}) collective-permute-start(f32[1,5,8,128]{3,2,1,0:T(8,128)S(1)} %get-tuple-element.67.own), channel_id=1, source_target_pairs={{0,32},{8,40},{16,48},{24,56},{32,64},{40,72},{48,80},{56,88},{64,... | collective-permute-start | bytes 61448 | tf_op jit(solution)/shard_map/cond/branch_1_fun/ppermute | solution.py:410
  3.6 4.0 %collective-permute-start.2 = (f32[1,5,8,128]{3,2,1,0:T(8,128)S(1)}, f32[1,5,8,128]{3,2,1,0:T(8,128)S(1)}, u32[]{:S(2)}, u32[]{:S(2)}) collective-permute-start(f32[1,5,8,128]{3,2,1,0:T(8,128)S(1)} %get-tuple-element.67.own), channel_id=1, source_target_pairs={{0,224},{8,232},{16,240},{24,248},{32,0},{40,8},{48,16},{56,24},{6... | collective-permute-start | bytes 61448 | tf_op jit(solution)/shard_map/cond/branch_1_fun/ppermute | solution.py:410
  7.7 2.6 %disc_element.1 = (f32[16,128]{1,0:T(8,128)S(1)}, s32[256,128]{1,0:T(8,128)S(1)}) custom-call(f32[2,16,128]{2,1,0:T(8,128)} %get-tuple-element.76.field.whole, s32[2,256,128]{2,1,0:T(8,128)} %get-tuple-element.68.vertices, f32[2,10,64,128]{3,2,1,0:T(8,128)} %get-tuple-element.69.entries, s32[32,1024]{1,0:T(8,128)} %get-tuple-element.70.partners), custom_call_target="tpu_custom_call" | custom-call | bytes 7920000 | tf_op jit(solution)/shard_map/cond/branch_1_fun/disc_element/pallas_call | solution.py:368
  10.2 0.0 collective-permute-done.1
  10.3 0.0 collective-permute-done.2
  10.3 3.0 %collective-permute-start.4 = (f32[3,5,8,128]{3,2,1,0:T(8,128)S(1)}, f32[3,5,8,128]{3,2,1,0:T(8,128)S(1)}, u32[]{:S(2)}, u32[]{:S(2)}) collective-permute-start(f32[3,5,8,128]{3,2,1,0:T(8,128)S(1)} %pad_maximum_fusion.1), channel_id=1, source_target_pairs={{0,160},{8,168},{16,176},{24,184},{32,192},{40,200},{48,208},{56,2... | collective-permute-start | bytes 184328 | tf_op jit(solution)/shard_map/cond/branch_1_fun/ppermute | solution.py:410
  13.3 1.8 %collective-permute-start.3 = (f32[2,5,8,128]{3,2,1,0:T(8,128)S(1)}, f32[2,5,8,128]{3,2,1,0:T(8,128)S(1)}, u32[]{:S(2)}, u32[]{:S(2)}) collective-permute-start(f32[2,5,8,128]{3,2,1,0:T(8,128)S(1)} %slice.2), channel_id=1, source_target_pairs={{0,64},{8,72},{16,80},{24,88},{32,96},{40,104},{48,112},{56,120},{... | collective-permute-start | bytes 122888 | tf_op jit(solution)/shard_map/cond/branch_1_fun/ppermute | solution.py:410
  15.1 0.4 %collective-permute-start.6 = (f32[3,5,8,128]{3,2,1,0:T(8,128)S(1)}, f32[3,5,8,128]{3,2,1,0:T(8,128)S(1)}, u32[]{:S(2)}, u32[]{:S(2)}) collective-permute-start(f32[3,5,8,128]{3,2,1,0:T(8,128)S(1)} %pad_maximum_fusion.1), channel_id=1, source_target_pairs={{0,16},{8,24},{16,0},{24,8},{32,48},{40,56},{48,32},{56,40},{64,80... | collective-permute-start | bytes 184328 | tf_op jit(solution)/shard_map/cond/branch_1_fun/ppermute | solution.py:413
  15.6 2.8 %pad_element.1 = (f32[2,16,128]{2,1,0:T(8,128)S(1)}, f32[8,128]{1,0:T(8,128)S(1)}, s32[8,128]{1,0:T(8,128)S(1)}, f32[2,16,128]{2,1,0:T(8,128)S(1)}, f32[2,16,128...) custom-call(f32[2,16,128]{2,1,0:T(8,128)} %get-tuple-element.76.field.whole, s32[2,256,128]{2,1,0:T(8,128)} %get-tuple-element.68.vertices, ...), custom_call_target="tpu_custom_call" | custom-call | bytes 9000000 | tf_op jit(solution)/shard_map/cond/branch_1_fun/pad_element/pallas_call | solution.py:368
  18.3 1.6 %collective-permute-done.3 = f32[2,5,8,128]{3,2,1,0:T(8,128)S(1)} collective-permute-done((f32[2,5,8,128]{3,2,1,0:T(8,128)S(1)}, f32[2,5,8,128]{3,2,1,0:T(8,128)S(1)}, u32[]{:S(2)}, u32[]{:S(2)}) %collective-permute-start.3) | collective-permute-done | bytes 40992 | tf_op jit(solution)/shard_map/cond/branch_1_fun/ppermute | solution.py:410
  19.9 0.0 collective-permute-done.4
  19.9 0.1 collective-permute-start.8
  20.0 0.5 %collective-permute-start.5 = (f32[5,5,8,128]{3,2,1,0:T(8,128)S(1)}, f32[5,5,8,128]{3,2,1,0:T(8,128)S(1)}, u32[]{:S(2)}, u32[]{:S(2)}) collective-permute-start(f32[5,5,8,128]{3,2,1,0:T(8,128)S(1)} %pad_maximum_fusion), channel_id=1, source_target_pairs={{0,16},{8,24},{16,0},{24,8},{32,48},{40,56},{48,32},{56,40},{64,80... | collective-permute-start | bytes 307208 | tf_op jit(solution)/shard_map/cond/branch_1_fun/ppermute | solution.py:413
  20.6 0.0 collective-permute-done.6.three
  20.6 0.3 %collective-permute-start.7 = (f32[3,5,8,128]{3,2,1,0:T(8,128)S(1)}, f32[3,5,8,128]{3,2,1,0:T(8,128)S(1)}, u32[]{:S(2)}, u32[]{:S(2)}) collective-permute-start(f32[3,5,8,128]{3,2,1,0:T(8,128)S(1)} %collective-permute-done.6.three), channel_id=1, source_target_pairs={{0,8},{8,0},{16,24},{24,16},{32,40},{40,32},{48,56},{56,48},{64,72... | collective-permute-start | bytes 184328 | tf_op jit(solution)/shard_map/cond/branch_1_fun/ppermute | solution.py:413
  20.9 0.5 %collective-permute-done.8.twin = f32[8,5,8,128]{3,2,1,0:T(8,128)S(1)} collective-permute-done((f32[8,5,8,128]{3,2,1,0:T(8,128)S(1)}, f32[8,5,8,128]{3,2,1,0:T(8,128)S(1)}, u32[]{:S(2)}, u32[]{:S(2)}) %collective-permute-start.8) | collective-permute-done | bytes 163872 | tf_op jit(solution)/shard_map/cond/branch_1_fun/ppermute | solution.py:413
  21.4 1.2 %first_packets.1 = (f32[8,128]{1,0:T(8,128)S(1)}, f32[8,128]{1,0:T(8,128)S(1)}, f32[32,64]{1,0:T(8,128)S(1)}) custom-call(f32[8,5,8,128]{3,2,1,0:T(8,128)S(1)} %constant_dynamic-update-slice_fusion.eight, f32[8,5,8,128]{3,2,1,0:T(8,128)S(1)} %collective-permute-done.8.twin, f32[3,5,8,128]{3,2,1,0:T(8,128)S(1)} %collective-permute-done.6.three, ...), custom_call_target="tpu_custom_call" | custom-call | bytes 5400000 | tf_op jit(solution)/shard_map/cond/branch_1_fun/first_packets/pallas_call | solution.py:368
  22.6 0.0 collective-permute-done.7.three
  22.6 2.9 %collective-permute-done.5.five = f32[5,5,8,128]{3,2,1,0:T(8,128)S(1)} collective-permute-done((f32[5,5,8,128]{3,2,1,0:T(8,128)S(1)}, f32[5,5,8,128]{3,2,1,0:T(8,128)S(1)}, u32[]{:S(2)}, u32[]{:S(2)}) %collective-permute-start.5) | collective-permute-done | bytes 102432 | tf_op jit(solution)/shard_map/cond/branch_1_fun/ppermute | solution.py:413
  25.5 0.0 collective-permute-start.9
  25.5 0.5 %second_packets.1 = (f32[8,128]{1,0:T(8,128)S(1)}, f32[8,128]{1,0:T(8,128)S(1)}, f32[32,64]{1,0:T(8,128)S(1)}) custom-call(f32[3,5,8,128]{3,2,1,0:T(8,128)S(1)} %collective-permute-done.7.three, f32[5,5,8,128]{3,2,1,0:T(8,128)S(1)} %collective-permute-done.5.five, s32[256,128]{1,0:T(8,128)S(1)} %get-tuple-element.84.lookup, ...), custom_call_target="tpu_custom_call" | custom-call | bytes 3600000 | tf_op jit(solution)/shard_map/cond/branch_1_fun/second_packets/pallas_call | solution.py:368
  26.0 0.8 %collective-permute-done.9.last = f32[5,5,8,128]{3,2,1,0:T(8,128)S(1)} collective-permute-done((f32[5,5,8,128]{3,2,1,0:T(8,128)S(1)}, f32[5,5,8,128]{3,2,1,0:T(8,128)S(1)}, u32[]{:S(2)}, u32[]{:S(2)}) %collective-permute-start.9) | collective-permute-done | bytes 102432 | tf_op jit(solution)/shard_map/cond/branch_1_fun/ppermute | solution.py:413
  26.8 1.1 %contact.1 = (f32[8,128]{1,0:T(8,128)S(1)}, f32[2,16,128]{2,1,0:T(8,128)S(1)}, f32[8,128]{1,0:T(8,128)S(1)}) custom-call(f32[5,5,8,128]{3,2,1,0:T(8,128)S(1)} %collective-permute-done.9.last, s32[256,128]{1,0:T(8,128)S(1)} %get-tuple-element.84.lookup, f32[1,5,8,128]{3,2,1,0:T(8,128)S(1)} %get-tuple-element.67.own, f32[8,128]{1,0:T(8,128)S(1)} %get-tuple-element.97.normal, ...), custom_call_target="tpu_custom_call" | custom-call | bytes 5400000 | tf_op jit(solution)/shard_map/cond/branch_1_fun/contact/pallas_call | solution.py:368
  28.2 0.1 collective-permute-start.10
  28.3 0.6 %copy.41 = f32[1,1024]{1,0:T(1,128)} copy(f32[1,1024]{1,0:T(1,128)S(1)} %get-tuple-element.171) | data formatting | bytes 8192
  28.9 3.0 %collective-permute-done.10.late = f32[8,128]{1,0:T(8,128)S(1)} collective-permute-done((f32[8,128]{1,0:T(8,128)S(1)}, f32[8,128]{1,0:T(8,128)S(1)}, u32[]{:S(2)}, u32[]{:S(2)}) %collective-permute-start.10) | collective-permute-done | bytes 4128 | tf_op jit(solution)/shard_map/ppermute | solution.py:520
  31.9 0.7 %advance.1 = f32[2,16,128]{2,1,0:T(8,128)} custom-call(f32[2,16,128]{2,1,0:T(8,128)S(1)} %get-tuple-element.119.field, f32[2,16,128]{2,1,0:T(8,128)S(1)} %get-tuple-element.120.storage, f32[2,16,128]{2,1,0:T(8,128)S(1)} %get-tuple-element.121.nodal, f32[2,16,128]{2,1,0:T(8,128)S(1)} %get-tuple-element.122.slots, f32[8,128]{1,0:T(8,128)S(1)} %get-tuple-element.123.early, ...), custom_call_target="tpu_custom_call" | custom-call | bytes 3600000 | tf_op jit(solution)/shard_map/advance/pallas_call | solution.py:368
  (6 shorter events, 0.0 us)
Async XLA Ops:
  1.6 8.6 %collective-permute-start.1 = (f32[1,5,8,128]{3,2,1,0:T(8,128)S(1)}, f32[1,5,8,128]{3,2,1,0:T(8,128)S(1)}, u32[]{:S(2)}, u32[]{:S(2)}) collective-permute-start(f32[1,5,8,128]{3,2,1,0:T(8,128)S(1)} %get-tuple-element.67.own), channel_id=1, source_target_pairs={{0,32},{8,40},{16,48},{24,56},{32,64},{40,72},{48,80},{56,88},{64,... | collective-permute-start | bytes 61448 | tf_op jit(solution)/shard_map/cond/branch_1_fun/ppermute | solution.py:410
  3.6 6.7 %collective-permute-start.2 = (f32[1,5,8,128]{3,2,1,0:T(8,128)S(1)}, f32[1,5,8,128]{3,2,1,0:T(8,128)S(1)}, u32[]{:S(2)}, u32[]{:S(2)}) collective-permute-start(f32[1,5,8,128]{3,2,1,0:T(8,128)S(1)} %get-tuple-element.67.own), channel_id=1, source_target_pairs={{0,224},{8,232},{16,240},{24,248},{32,0},{40,8},{48,16},{56,24},{6... | collective-permute-start | bytes 61448 | tf_op jit(solution)/shard_map/cond/branch_1_fun/ppermute | solution.py:410
  10.3 9.6 %collective-permute-start.4 = (f32[3,5,8,128]{3,2,1,0:T(8,128)S(1)}, f32[3,5,8,128]{3,2,1,0:T(8,128)S(1)}, u32[]{:S(2)}, u32[]{:S(2)}) collective-permute-start(f32[3,5,8,128]{3,2,1,0:T(8,128)S(1)} %pad_maximum_fusion.1), channel_id=1, source_target_pairs={{0,160},{8,168},{16,176},{24,184},{32,192},{40,200},{48,208},{56,2... | collective-permute-start | bytes 184328 | tf_op jit(solution)/shard_map/cond/branch_1_fun/ppermute | solution.py:410
  13.3 6.6 %collective-permute-start.3 = (f32[2,5,8,128]{3,2,1,0:T(8,128)S(1)}, f32[2,5,8,128]{3,2,1,0:T(8,128)S(1)}, u32[]{:S(2)}, u32[]{:S(2)}) collective-permute-start(f32[2,5,8,128]{3,2,1,0:T(8,128)S(1)} %slice.2), channel_id=1, source_target_pairs={{0,64},{8,72},{16,80},{24,88},{32,96},{40,104},{48,112},{56,120},{... | collective-permute-start | bytes 122888 | tf_op jit(solution)/shard_map/cond/branch_1_fun/ppermute | solution.py:410
  15.1 5.5 %collective-permute-start.6 = (f32[3,5,8,128]{3,2,1,0:T(8,128)S(1)}, f32[3,5,8,128]{3,2,1,0:T(8,128)S(1)}, u32[]{:S(2)}, u32[]{:S(2)}) collective-permute-start(f32[3,5,8,128]{3,2,1,0:T(8,128)S(1)} %pad_maximum_fusion.1), channel_id=1, source_target_pairs={{0,16},{8,24},{16,0},{24,8},{32,48},{40,56},{48,32},{56,40},{64,80... | collective-permute-start | bytes 184328 | tf_op jit(solution)/shard_map/cond/branch_1_fun/ppermute | solution.py:413
  19.9 1.5 %collective-permute-start.8 = (f32[8,5,8,128]{3,2,1,0:T(8,128)S(1)}, f32[8,5,8,128]{3,2,1,0:T(8,128)S(1)}, u32[]{:S(2)}, u32[]{:S(2)}) collective-permute-start(f32[8,5,8,128]{3,2,1,0:T(8,128)S(1)} %constant_dynamic-update-slice_fusion.eight), channel_id=1, source_target_pairs={{0,8},{8,0},{16,24},{24,16},{32,40},{40,32},{48,56},{56,48},{64,72... | collective-permute-start | bytes 491528 | tf_op jit(solution)/shard_map/cond/branch_1_fun/ppermute | solution.py:413
  20.0 5.5 %collective-permute-start.5 = (f32[5,5,8,128]{3,2,1,0:T(8,128)S(1)}, f32[5,5,8,128]{3,2,1,0:T(8,128)S(1)}, u32[]{:S(2)}, u32[]{:S(2)}) collective-permute-start(f32[5,5,8,128]{3,2,1,0:T(8,128)S(1)} %pad_maximum_fusion), channel_id=1, source_target_pairs={{0,16},{8,24},{16,0},{24,8},{32,48},{40,56},{48,32},{56,40},{64,80... | collective-permute-start | bytes 307208 | tf_op jit(solution)/shard_map/cond/branch_1_fun/ppermute | solution.py:413
  20.6 2.0 %collective-permute-start.7 = (f32[3,5,8,128]{3,2,1,0:T(8,128)S(1)}, f32[3,5,8,128]{3,2,1,0:T(8,128)S(1)}, u32[]{:S(2)}, u32[]{:S(2)}) collective-permute-start(f32[3,5,8,128]{3,2,1,0:T(8,128)S(1)} %collective-permute-done.6.three), channel_id=1, source_target_pairs={{0,8},{8,0},{16,24},{24,16},{32,40},{40,32},{48,56},{56,48},{64,72... | collective-permute-start | bytes 184328 | tf_op jit(solution)/shard_map/cond/branch_1_fun/ppermute | solution.py:413
  25.5 1.3 %collective-permute-start.9 = (f32[5,5,8,128]{3,2,1,0:T(8,128)S(1)}, f32[5,5,8,128]{3,2,1,0:T(8,128)S(1)}, u32[]{:S(2)}, u32[]{:S(2)}) collective-permute-start(f32[5,5,8,128]{3,2,1,0:T(8,128)S(1)} %collective-permute-done.5.five), channel_id=1, source_target_pairs={{0,8},{8,0},{16,24},{24,16},{32,40},{40,32},{48,56},{56,48},{64,72... | collective-permute-start | bytes 307208 | tf_op jit(solution)/shard_map/cond/branch_1_fun/ppermute | solution.py:413
  28.2 3.7 %collective-permute-start.10 = (f32[8,128]{1,0:T(8,128)S(1)}, f32[8,128]{1,0:T(8,128)S(1)}, u32[]{:S(2)}, u32[]{:S(2)}) collective-permute-start(f32[8,128]{1,0:T(8,128)S(1)} %get-tuple-element.124), channel_id=1, source_target_pairs={{0,1},{1,0},{2,3},{3,2},{4,5},{5,4},{6,7},{7,6},{8,9},{9,8},{10,11... | collective-permute-start | bytes 12296 | tf_op jit(solution)/shard_map/ppermute | solution.py:520

commit v6 on v5

--- a/solution.py
+++ b/solution.py
@@ -13,6 +13,7 @@
 
 LANES = 128
 ROWS = 8
+DISC_FIRST = 6
 LOW = 64
 AHEAD = (-1, 0, 1, 2, 3, 4, -3, -2)
 
@@ -103,12 +104,11 @@
     corners_out[...] = corners[...]
 
 
-def element_sum(field, vertices, entries, out, coarse_at, fine_at, body=0):
+def element_total(field, vertices, entries, total, coarse_at, fine_at, body=0, chunks=range(8)):
     highs = keys(32, True)
     lows = keys(LOW)
-    total = jnp.zeros((64, LOW), jnp.float32)
     order = ((0, 4, 5, 6), (4, 1, 7, 8), (5, 7, 2, 9), (6, 8, 9, 3))
-    for j in range(8):
+    for j in chunks:
         here = slice(ROWS * j, ROWS * (j + 1))
         corner = [vertices[body, pl.ds(32 * j + c, ROWS, stride=4), :] for c in range(4)]
         picked = [lane_lookup(lambda r: wide(field, r, body), i, 16) for i in corner]
@@ -136,7 +136,11 @@
             for s in range(ROWS)
         ]
         total = total + contract(slices)
-    store_nodal(out, (), total, -1.0)
+    return total
+
+
+def nothing():
+    return jnp.zeros((64, LOW), jnp.float32)
 
 
 def disc_kernel(field, vertices, entries, partners, out, lookup, coarse_at, fine_at):
@@ -145,7 +149,20 @@
             lookup[pl.ds(64 * g + s, ROWS, stride=ROWS), :] = partners[
                 ROWS * g : ROWS * (g + 1), LANES * s : LANES * (s + 1)
             ]
-    element_sum(field, vertices, entries, out, coarse_at, fine_at)
+    out[...] = element_total(
+        field, vertices, entries, nothing(), coarse_at, fine_at, chunks=range(DISC_FIRST)
+    )
+
+
+def middle_kernel(
+    field, vertices, entries, pad_field, pad_vertices, pad_entries, disc, disc_out, pad_out, coarse_at, fine_at
+):
+    disc_out[...] = element_total(
+        field, vertices, entries, disc[...], coarse_at.at[0], fine_at.at[0], chunks=range(2)
+    )
+    pad_out[...] = element_total(
+        pad_field, pad_vertices, pad_entries, nothing(), coarse_at.at[1], fine_at.at[1], chunks=range(4)
+    )
 
 
 def rim_lookup(first_row, second_row, index):
@@ -168,15 +185,18 @@
 
 
 def pad_kernel(
-    field, vertices, entries, rims, whole, storage, disc,
+    field, vertices, entries, rims, whole, storage, disc, pad,
     out, rim_out, rims_out, slot_out, field_out, storage_out, coarse_at, fine_at,
 ):
     rims_out[...] = rims[...]
     field_out[...] = whole[...]
     storage_out[...] = storage[...]
     rim_slots(rims, slot_out)
-    element_sum(field, vertices, entries, out.at[1], coarse_at, fine_at)
-    out[0] = disc[...]
+    store_nodal(out, (0,), disc[...], -1.0)
+    total = element_total(
+        field, vertices, entries, pad[...], coarse_at, fine_at, chunks=range(4)
+    )
+    store_nodal(out, (1,), total, -1.0)
     rim_out[...] = rim_lookup(lambda r: wide(out, r, 0), lambda r: wide(out, r, 1), rims[...])
 
 
@@ -303,7 +323,8 @@
     mine[...] = faces
     rim_slots(rims, slot_out)
     for body in range(2):
-        element_sum(field, vertices, entries, out.at[body], coarse_at, fine_at, body)
+        total = element_total(field, vertices, entries, nothing(), coarse_at, fine_at, body)
+        store_nodal(out, (body,), total, -1.0)
     rim_out[...] = rim_lookup(lambda r: wide(out, r, 0), lambda r: wide(out, r, 1), rims[...])
 
 
@@ -353,9 +374,10 @@
     return Placed(array, True)
 
 
-def one_body(array, body):
-    block = (1,) + array.shape[1:]
-    return pl.BlockSpec(block, lambda i: (body,) + (0,) * (len(block) - 1), memory_space=pltpu.VMEM)
+def one_body(array, body, part=0, parts=1):
+    block = (1,) + array.shape[1:-2] + (array.shape[-2] // parts, LANES)
+    at = (body,) + (0,) * (len(block) - 3) + (part, 0)
+    return pl.BlockSpec(block, lambda i: at, memory_space=pltpu.VMEM)
 
 
 def call(body, out, arguments, scratch=(), specs=None, name=None, time=1.0):
@@ -412,20 +434,21 @@
     def across(cells, bit):
         return lax.ppermute(cells, "face", [(i, i ^ bit) for i in range(32)])
 
-    def of_body(body):
-        return {k: one_body(a, body) for k, a in enumerate((field, vertices, entries))}
-
-    parts = ((1, 4, 64, LANES),) * 2
+    def of_body(body, part=0, parts=1):
+        return (one_body(field, body), one_body(vertices, body, part, parts), one_body(entries, body, part, parts))
+
+    bodies = (field, vertices, entries)
+    partial = here(64, LOW)
 
     def elements_and_eight(own):
         behind = along(own, 1)
         ahead = along(own, -1)
         disc, lookup = call(
             disc_kernel,
-            (nodes, here(256, LANES, dtype=jnp.int32)),
-            (field, vertices, entries, partner_lookup),
-            scratch=parts,
-            specs=of_body(0),
+            (partial, here(256, LANES, dtype=jnp.int32)),
+            (*bodies, partner_lookup),
+            scratch=((1, 4, 64, LANES),) * 2,
+            specs=dict(enumerate(of_body(0))),
             name="disc_element",
             time=2.2,
         )
@@ -435,22 +458,21 @@
         far_ahead = along(three, -3)
         far_behind = along(three[:2], 2)
         other_three = across(three, 2)
-        element, rim_element, rims_near, *kept = call(
-            pad_kernel,
-            (here(2, 16, LANES), tile, here(ROWS, LANES, dtype=jnp.int32))
-            + (here(2, 16, LANES),) * 3,
-            (again, vertices, entries, rims, field, storage, near(disc)),
-            scratch=parts,
-            specs=of_body(1),
-            name="pad_element",
-            time=2.5,
-        )
-        far_behind, far_ahead, element, rim_element = lax.optimization_barrier(
-            (far_behind, far_ahead, element, rim_element)
+        disc, pad = call(
+            middle_kernel,
+            (partial, partial),
+            (again, vertices, entries, *bodies, near(disc)),
+            scratch=((2, 1, 4, 32, LANES),) * 2,
+            specs=dict(enumerate(of_body(0, 3, 4) + of_body(1, 0, 2))),
+            name="middle_element",
+            time=2.2,
+        )
+        far_ahead, far_behind, disc, pad = lax.optimization_barrier(
+            (far_ahead, far_behind, disc, pad)
         )
         five = jnp.concatenate([far_ahead, far_behind], axis=0)
         eight = jnp.concatenate([three, five], axis=0)
-        return eight, five, other_three, lookup, element, rim_element, rims_near, kept
+        return eight, five, other_three, lookup, disc, pad
 
     def surface_block():
         own, own_corners = call(
@@ -459,9 +481,7 @@
             (field, corners, motion, engaged, gaps, factor),
             name="packet",
         )
-        eight, five, other_three, lookup, element, rim_element, rims_near, kept = (
-            elements_and_eight(own)
-        )
+        eight, five, other_three, lookup, disc, pad = elements_and_eight(own)
         other_five = across(five, 2)
         twin = across(eight, 1)
         last_three = across(other_three, 1)
@@ -473,7 +493,20 @@
             name="first_packets",
             time=1.5,
         )
-        other_five, last_three, done = lax.optimization_barrier((other_five, last_three, done))
+        again, disc, done = lax.optimization_barrier((field, disc, done))
+        element, rim_element, rims_near, *kept = call(
+            pad_kernel,
+            (here(2, 16, LANES), tile, here(ROWS, LANES, dtype=jnp.int32))
+            + (here(2, 16, LANES),) * 3,
+            (again, vertices, entries, rims, field, storage, near(disc), near(pad)),
+            scratch=((1, 4, 32, LANES),) * 2,
+            specs=dict(enumerate(of_body(1, 1, 2))),
+            name="pad_element",
+            time=2.2,
+        )
+        other_five, last_three, done, element = lax.optimization_barrier(
+            (other_five, last_three, done, element)
+        )
         last = across(other_five, 1)
         done = call(
             second_kernel,

time: 32.8 us -> 32.8 us (level)
  waiting for transfers between devices: 8.8 us -> 7.17 us
  Pallas kernels: 9.87 us -> 11.1 us
    ppermute x5, waiting for transfers between devices: 4.2 us -> 2.06 us  [across(): return lax.ppermute(cells, 'face', [(i, i ^ bit) for i in range(32)])]
    pallas_call x7 -> x8, Pallas kernels: 9.87 us -> 11.1 us  [call(): pl.pallas_call(body, out_shape=out, in_specs=[specs.get(i, whole) for i i...]
    ppermute x4, waiting for transfers between devices: 1.61 us -> 2.11 us  [along(): lax.ppermute(cells, 'face', [(i, (i + 4 * step) % 32) for i in range(32)])]
    ppermute x4, starting transfers between devices: 10.8 us -> 11.1 us  [along(): lax.ppermute(cells, 'face', [(i, (i + 4 * step) % 32) for i in range(32)])]
  transfers between devices with their start and end apart: 10 -> 10, of which waited for: 5 -> 5; matrix products, arithmetic and copies ran while one was open for 2% -> 2% of each run, Pallas kernels for 22% -> 25%
where the time goes in v6:
time: 32.8 us; the launch traced here: 32.6 us
  starting transfers between devices  12.6 us (38%)
  Pallas kernels  11.1 us (34%)
  waiting for transfers between devices  7.17 us (22%)
  between operations  0.65 us (2%)
  local copies, waits for them, and re-layouts  0.62 us (2%)
  loops' own time  0.35 us (1%)
    ppermute x4, starting transfers between devices, along(): lax.ppermute(cells, 'face', [(i, (i + 4 * step) % 32) for i in range(32)])  11.1 us
    pallas_call x8, Pallas kernels, call(): pl.pallas_call(body, out_shape=out, in_specs=[specs.get(i, whole) for i i...  11.1 us
    ppermute x1, waiting for transfers between devices, local(): late = lax.ppermute(rim_total, 'depth', [(i, i ^ 1) for i in range(8)])  3 us
    ppermute x4, waiting for transfers between devices, along(): lax.ppermute(cells, 'face', [(i, (i + 4 * step) % 32) for i in range(32)])  2.11 us
    ppermute x5, waiting for transfers between devices, across(): return lax.ppermute(cells, 'face', [(i, i ^ bit) for i in range(32)])  2.06 us
    ppermute x5, starting transfers between devices, across(): return lax.ppermute(cells, 'face', [(i, i ^ bit) for i in range(32)])  1.41 us
  transfers between devices with their start and end apart: 10, of which 5 were waited for; matrix products, arithmetic and copies ran while one was open for 2% of the time, Pallas kernels for 25%

profile of v6, /device:TPU:8, one launch (start us, length us, event | category | flops | bytes accessed | tf_op | source)
XLA Modules:
  0.0 32.6 jit_solution(18034144970010627976)
XLA Ops:
  0.6 27.5 %conditional.1 = (f32[2,16,128]{2,1,0:T(8,128)S(1)}, f32[8,128]{1,0:T(8,128)S(1)}, f32[8,128]{1,0:T(8,128)S(1)}, f32[2,16,128]{2,1,0:T(8,128)S(1)}, f32[2,16,128...) conditional(s32[]{:T(128)} %convert_element_type.3, (f32[2,16,128]{2,1,0:T(8,128)}, ...), branch_computations={%region_0.0_spmd, %region_1.0_spmd} | conditional | flops 56320 | bytes 45037216 | solution.py:550
  0.7 1.0 %packet.1 = (f32[1,5,8,128]{3,2,1,0:T(8,128)S(1)}, s32[2,3,8,128]{3,2,1,0:T(8,128)S(1)}) custom-call(f32[2,16,128]{2,1,0:T(8,128)} %get-tuple-element.90.field.pad_field.whole, s32[2,3,8,128]{3,2,1,0:T(8,128)} %bitcast.33, f32[8,128]{1,0:T(8,128)} %get-tuple-element.63.motion, s32[8,128]{1,0:T(8,128)} %get-tuple-element.64.engaged, ...), custom_call_target="tpu_custom_call" | custom-call | bytes 3600000 | tf_op jit(solution)/shard_map/cond/branch_1_fun/packet/pallas_call | solution.py:390
  1.6 2.0 %collective-permute-start.1 = (f32[1,5,8,128]{3,2,1,0:T(8,128)S(1)}, f32[1,5,8,128]{3,2,1,0:T(8,128)S(1)}, u32[]{:S(2)}, u32[]{:S(2)}) collective-permute-start(f32[1,5,8,128]{3,2,1,0:T(8,128)S(1)} %get-tuple-element.67.own), channel_id=1, source_target_pairs={{0,32},{8,40},{16,48},{24,56},{32,64},{40,72},{48,80},{56,88},{64,... | collective-permute-start | bytes 61448 | tf_op jit(solution)/shard_map/cond/branch_1_fun/ppermute | solution.py:432
  3.6 4.0 %collective-permute-start.2 = (f32[1,5,8,128]{3,2,1,0:T(8,128)S(1)}, f32[1,5,8,128]{3,2,1,0:T(8,128)S(1)}, u32[]{:S(2)}, u32[]{:S(2)}) collective-permute-start(f32[1,5,8,128]{3,2,1,0:T(8,128)S(1)} %get-tuple-element.67.own), channel_id=1, source_target_pairs={{0,224},{8,232},{16,240},{24,248},{32,0},{40,8},{48,16},{56,24},{6... | collective-permute-start | bytes 61448 | tf_op jit(solution)/shard_map/cond/branch_1_fun/ppermute | solution.py:432
  7.7 2.3 %disc_element.1 = (f32[64,64]{1,0:T(8,128)S(1)}, s32[256,128]{1,0:T(8,128)S(1)}) custom-call(f32[2,16,128]{2,1,0:T(8,128)} %get-tuple-element.90.field.pad_field.whole, s32[2,256,128]{2,1,0:T(8,128)} %get-tuple-element.68.vertices.pad_vertices, f32[2,10,64,128]{3,2,1,0:T(8,128)} %get-tuple-element.69.entries.pad_entries, s32[32,1024]{1,0:T(8,128)} %get-tuple-element.70.partners), custom_call_target="tpu_custom_call" | custom-call | bytes 7920000 | tf_op jit(solution)/shard_map/cond/branch_1_fun/disc_element/pallas_call | solution.py:390
  9.9 0.0 collective-permute-done.1
  9.9 0.0 collective-permute-done.2
  10.0 3.4 %collective-permute-start.3 = (f32[3,5,8,128]{3,2,1,0:T(8,128)S(1)}, f32[3,5,8,128]{3,2,1,0:T(8,128)S(1)}, u32[]{:S(2)}, u32[]{:S(2)}) collective-permute-start(f32[3,5,8,128]{3,2,1,0:T(8,128)S(1)} %pad_maximum_fusion.1), channel_id=1, source_target_pairs={{0,160},{8,168},{16,176},{24,184},{32,192},{40,200},{48,208},{56,2... | collective-permute-start | bytes 184328 | tf_op jit(solution)/shard_map/cond/branch_1_fun/ppermute | solution.py:432
  13.3 1.8 %collective-permute-start.4 = (f32[2,5,8,128]{3,2,1,0:T(8,128)S(1)}, f32[2,5,8,128]{3,2,1,0:T(8,128)S(1)}, u32[]{:S(2)}, u32[]{:S(2)}) collective-permute-start(f32[2,5,8,128]{3,2,1,0:T(8,128)S(1)} %slice.2), channel_id=1, source_target_pairs={{0,64},{8,72},{16,80},{24,88},{32,96},{40,104},{48,112},{56,120},{... | collective-permute-start | bytes 122888 | tf_op jit(solution)/shard_map/cond/branch_1_fun/ppermute | solution.py:432
  15.1 0.4 %collective-permute-start.6 = (f32[3,5,8,128]{3,2,1,0:T(8,128)S(1)}, f32[3,5,8,128]{3,2,1,0:T(8,128)S(1)}, u32[]{:S(2)}, u32[]{:S(2)}) collective-permute-start(f32[3,5,8,128]{3,2,1,0:T(8,128)S(1)} %pad_maximum_fusion.1), channel_id=1, source_target_pairs={{0,16},{8,24},{16,0},{24,8},{32,48},{40,56},{48,32},{56,40},{64,80... | collective-permute-start | bytes 184328 | tf_op jit(solution)/shard_map/cond/branch_1_fun/ppermute | solution.py:435
  15.6 2.2 %middle_element.1 = (f32[64,64]{1,0:T(8,128)S(1)}, f32[64,64]{1,0:T(8,128)S(1)}) custom-call(f32[2,16,128]{2,1,0:T(8,128)} %get-tuple-element.90.field.pad_field.whole, s32[2,256,128]{2,1,0:T(8,128)} %get-tuple-element.68.vertices.pad_vertices, f32[2,10,64,128]{3,2,1,0:T(8,128)} %get-tuple-element.69.entries.pad_entries, ...), custom_call_target="tpu_custom_call" | custom-call | bytes 7920000 | tf_op jit(solution)/shard_map/cond/branch_1_fun/middle_element/pallas_call | solution.py:390
  17.8 2.1 %collective-permute-done.4 = f32[2,5,8,128]{3,2,1,0:T(8,128)S(1)} collective-permute-done((f32[2,5,8,128]{3,2,1,0:T(8,128)S(1)}, f32[2,5,8,128]{3,2,1,0:T(8,128)S(1)}, u32[]{:S(2)}, u32[]{:S(2)}) %collective-permute-start.4) | collective-permute-done | bytes 40992 | tf_op jit(solution)/shard_map/cond/branch_1_fun/ppermute | solution.py:432
  19.9 0.0 collective-permute-done.3
  19.9 0.1 collective-permute-start.8
  20.0 0.5 %collective-permute-start.5 = (f32[5,5,8,128]{3,2,1,0:T(8,128)S(1)}, f32[5,5,8,128]{3,2,1,0:T(8,128)S(1)}, u32[]{:S(2)}, u32[]{:S(2)}) collective-permute-start(f32[5,5,8,128]{3,2,1,0:T(8,128)S(1)} %pad_maximum_fusion), channel_id=1, source_target_pairs={{0,16},{8,24},{16,0},{24,8},{32,48},{40,56},{48,32},{56,40},{64,80... | collective-permute-start | bytes 307208 | tf_op jit(solution)/shard_map/cond/branch_1_fun/ppermute | solution.py:435
  20.6 0.0 collective-permute-done.6.three
  20.6 0.3 %collective-permute-start.7 = (f32[3,5,8,128]{3,2,1,0:T(8,128)S(1)}, f32[3,5,8,128]{3,2,1,0:T(8,128)S(1)}, u32[]{:S(2)}, u32[]{:S(2)}) collective-permute-start(f32[3,5,8,128]{3,2,1,0:T(8,128)S(1)} %collective-permute-done.6.three), channel_id=1, source_target_pairs={{0,8},{8,0},{16,24},{24,16},{32,40},{40,32},{48,56},{56,48},{64,72... | collective-permute-start | bytes 184328 | tf_op jit(solution)/shard_map/cond/branch_1_fun/ppermute | solution.py:435
  20.9 0.5 %collective-permute-done.8.twin = f32[8,5,8,128]{3,2,1,0:T(8,128)S(1)} collective-permute-done((f32[8,5,8,128]{3,2,1,0:T(8,128)S(1)}, f32[8,5,8,128]{3,2,1,0:T(8,128)S(1)}, u32[]{:S(2)}, u32[]{:S(2)}) %collective-permute-start.8) | collective-permute-done | bytes 163872 | tf_op jit(solution)/shard_map/cond/branch_1_fun/ppermute | solution.py:435
  21.4 1.1 %first_packets.1 = (f32[8,128]{1,0:T(8,128)S(1)}, f32[8,128]{1,0:T(8,128)S(1)}, f32[32,64]{1,0:T(8,128)S(1)}) custom-call(f32[8,5,8,128]{3,2,1,0:T(8,128)S(1)} %constant_dynamic-update-slice_fusion.eight, f32[8,5,8,128]{3,2,1,0:T(8,128)S(1)} %collective-permute-done.8.twin, f32[3,5,8,128]{3,2,1,0:T(8,128)S(1)} %collective-permute-done.6.three, ...), custom_call_target="tpu_custom_call" | custom-call | bytes 5400000 | tf_op jit(solution)/shard_map/cond/branch_1_fun/first_packets/pallas_call | solution.py:390
  22.5 2.1 %pad_element.1 = (f32[2,16,128]{2,1,0:T(8,128)S(1)}, f32[8,128]{1,0:T(8,128)S(1)}, s32[8,128]{1,0:T(8,128)S(1)}, f32[2,16,128]{2,1,0:T(8,128)S(1)}, f32[2,16,128...) custom-call(f32[2,16,128]{2,1,0:T(8,128)} %get-tuple-element.90.field.pad_field.whole, ...), custom_call_target="tpu_custom_call" | custom-call | bytes 7920000 | tf_op jit(solution)/shard_map/cond/branch_1_fun/pad_element/pallas_call | solution.py:390
  24.7 0.0 collective-permute-done.7.three
  24.7 0.8 %collective-permute-done.5.five = f32[5,5,8,128]{3,2,1,0:T(8,128)S(1)} collective-permute-done((f32[5,5,8,128]{3,2,1,0:T(8,128)S(1)}, f32[5,5,8,128]{3,2,1,0:T(8,128)S(1)}, u32[]{:S(2)}, u32[]{:S(2)}) %collective-permute-start.5) | collective-permute-done | bytes 102432 | tf_op jit(solution)/shard_map/cond/branch_1_fun/ppermute | solution.py:435
  25.5 0.0 collective-permute-start.9
  25.5 0.5 %second_packets.1 = (f32[8,128]{1,0:T(8,128)S(1)}, f32[8,128]{1,0:T(8,128)S(1)}, f32[32,64]{1,0:T(8,128)S(1)}) custom-call(f32[3,5,8,128]{3,2,1,0:T(8,128)S(1)} %collective-permute-done.7.three, f32[5,5,8,128]{3,2,1,0:T(8,128)S(1)} %collective-permute-done.5.five, s32[256,128]{1,0:T(8,128)S(1)} %get-tuple-element.83.lookup, ...), custom_call_target="tpu_custom_call" | custom-call | bytes 3600000 | tf_op jit(solution)/shard_map/cond/branch_1_fun/second_packets/pallas_call | solution.py:390
  26.0 0.8 %collective-permute-done.9.last = f32[5,5,8,128]{3,2,1,0:T(8,128)S(1)} collective-permute-done((f32[5,5,8,128]{3,2,1,0:T(8,128)S(1)}, f32[5,5,8,128]{3,2,1,0:T(8,128)S(1)}, u32[]{:S(2)}, u32[]{:S(2)}) %collective-permute-start.9) | collective-permute-done | bytes 102432 | tf_op jit(solution)/shard_map/cond/branch_1_fun/ppermute | solution.py:435
  26.8 1.1 %contact.1 = (f32[8,128]{1,0:T(8,128)S(1)}, f32[2,16,128]{2,1,0:T(8,128)S(1)}, f32[8,128]{1,0:T(8,128)S(1)}) custom-call(f32[5,5,8,128]{3,2,1,0:T(8,128)S(1)} %collective-permute-done.9.last, s32[256,128]{1,0:T(8,128)S(1)} %get-tuple-element.83.lookup, f32[1,5,8,128]{3,2,1,0:T(8,128)S(1)} %get-tuple-element.67.own, f32[8,128]{1,0:T(8,128)S(1)} %get-tuple-element.105.normal, ...), custom_call_target="tpu_custom_call" | custom-call | bytes 5400000 | tf_op jit(solution)/shard_map/cond/branch_1_fun/contact/pallas_call | solution.py:390
  28.1 0.1 collective-permute-start.10
  28.2 0.6 %copy.41 = f32[1,1024]{1,0:T(1,128)} copy(f32[1,1024]{1,0:T(1,128)S(1)} %get-tuple-element.179) | data formatting | bytes 8192
  28.8 3.0 %collective-permute-done.10.late = f32[8,128]{1,0:T(8,128)S(1)} collective-permute-done((f32[8,128]{1,0:T(8,128)S(1)}, f32[8,128]{1,0:T(8,128)S(1)}, u32[]{:S(2)}, u32[]{:S(2)}) %collective-permute-start.10) | collective-permute-done | bytes 4128 | tf_op jit(solution)/shard_map/ppermute | solution.py:553
  31.8 0.7 %advance.1 = f32[2,16,128]{2,1,0:T(8,128)} custom-call(f32[2,16,128]{2,1,0:T(8,128)S(1)} %get-tuple-element.127.field, f32[2,16,128]{2,1,0:T(8,128)S(1)} %get-tuple-element.128.storage, f32[2,16,128]{2,1,0:T(8,128)S(1)} %get-tuple-element.129.nodal, f32[2,16,128]{2,1,0:T(8,128)S(1)} %get-tuple-element.130.slots, f32[8,128]{1,0:T(8,128)S(1)} %get-tuple-element.131.early, ...), custom_call_target="tpu_custom_call" | custom-call | bytes 3600000 | tf_op jit(solution)/shard_map/advance/pallas_call | solution.py:390
  (6 shorter events, 0.0 us)
Async XLA Ops:
  1.6 8.3 %collective-permute-start.1 = (f32[1,5,8,128]{3,2,1,0:T(8,128)S(1)}, f32[1,5,8,128]{3,2,1,0:T(8,128)S(1)}, u32[]{:S(2)}, u32[]{:S(2)}) collective-permute-start(f32[1,5,8,128]{3,2,1,0:T(8,128)S(1)} %get-tuple-element.67.own), channel_id=1, source_target_pairs={{0,32},{8,40},{16,48},{24,56},{32,64},{40,72},{48,80},{56,88},{64,... | collective-permute-start | bytes 61448 | tf_op jit(solution)/shard_map/cond/branch_1_fun/ppermute | solution.py:432
  3.6 6.3 %collective-permute-start.2 = (f32[1,5,8,128]{3,2,1,0:T(8,128)S(1)}, f32[1,5,8,128]{3,2,1,0:T(8,128)S(1)}, u32[]{:S(2)}, u32[]{:S(2)}) collective-permute-start(f32[1,5,8,128]{3,2,1,0:T(8,128)S(1)} %get-tuple-element.67.own), channel_id=1, source_target_pairs={{0,224},{8,232},{16,240},{24,248},{32,0},{40,8},{48,16},{56,24},{6... | collective-permute-start | bytes 61448 | tf_op jit(solution)/shard_map/cond/branch_1_fun/ppermute | solution.py:432
  10.0 9.9 %collective-permute-start.3 = (f32[3,5,8,128]{3,2,1,0:T(8,128)S(1)}, f32[3,5,8,128]{3,2,1,0:T(8,128)S(1)}, u32[]{:S(2)}, u32[]{:S(2)}) collective-permute-start(f32[3,5,8,128]{3,2,1,0:T(8,128)S(1)} %pad_maximum_fusion.1), channel_id=1, source_target_pairs={{0,160},{8,168},{16,176},{24,184},{32,192},{40,200},{48,208},{56,2... | collective-permute-start | bytes 184328 | tf_op jit(solution)/shard_map/cond/branch_1_fun/ppermute | solution.py:432
  13.3 6.5 %collective-permute-start.4 = (f32[2,5,8,128]{3,2,1,0:T(8,128)S(1)}, f32[2,5,8,128]{3,2,1,0:T(8,128)S(1)}, u32[]{:S(2)}, u32[]{:S(2)}) collective-permute-start(f32[2,5,8,128]{3,2,1,0:T(8,128)S(1)} %slice.2), channel_id=1, source_target_pairs={{0,64},{8,72},{16,80},{24,88},{32,96},{40,104},{48,112},{56,120},{... | collective-permute-start | bytes 122888 | tf_op jit(solution)/shard_map/cond/branch_1_fun/ppermute | solution.py:432
  15.1 5.5 %collective-permute-start.6 = (f32[3,5,8,128]{3,2,1,0:T(8,128)S(1)}, f32[3,5,8,128]{3,2,1,0:T(8,128)S(1)}, u32[]{:S(2)}, u32[]{:S(2)}) collective-permute-start(f32[3,5,8,128]{3,2,1,0:T(8,128)S(1)} %pad_maximum_fusion.1), channel_id=1, source_target_pairs={{0,16},{8,24},{16,0},{24,8},{32,48},{40,56},{48,32},{56,40},{64,80... | collective-permute-start | bytes 184328 | tf_op jit(solution)/shard_map/cond/branch_1_fun/ppermute | solution.py:435
  19.9 1.5 %collective-permute-start.8 = (f32[8,5,8,128]{3,2,1,0:T(8,128)S(1)}, f32[8,5,8,128]{3,2,1,0:T(8,128)S(1)}, u32[]{:S(2)}, u32[]{:S(2)}) collective-permute-start(f32[8,5,8,128]{3,2,1,0:T(8,128)S(1)} %constant_dynamic-update-slice_fusion.eight), channel_id=1, source_target_pairs={{0,8},{8,0},{16,24},{24,16},{32,40},{40,32},{48,56},{56,48},{64,72... | collective-permute-start | bytes 491528 | tf_op jit(solution)/shard_map/cond/branch_1_fun/ppermute | solution.py:435
  20.0 5.5 %collective-permute-start.5 = (f32[5,5,8,128]{3,2,1,0:T(8,128)S(1)}, f32[5,5,8,128]{3,2,1,0:T(8,128)S(1)}, u32[]{:S(2)}, u32[]{:S(2)}) collective-permute-start(f32[5,5,8,128]{3,2,1,0:T(8,128)S(1)} %pad_maximum_fusion), channel_id=1, source_target_pairs={{0,16},{8,24},{16,0},{24,8},{32,48},{40,56},{48,32},{56,40},{64,80... | collective-permute-start | bytes 307208 | tf_op jit(solution)/shard_map/cond/branch_1_fun/ppermute | solution.py:435
  20.6 4.1 %collective-permute-start.7 = (f32[3,5,8,128]{3,2,1,0:T(8,128)S(1)}, f32[3,5,8,128]{3,2,1,0:T(8,128)S(1)}, u32[]{:S(2)}, u32[]{:S(2)}) collective-permute-start(f32[3,5,8,128]{3,2,1,0:T(8,128)S(1)} %collective-permute-done.6.three), channel_id=1, source_target_pairs={{0,8},{8,0},{16,24},{24,16},{32,40},{40,32},{48,56},{56,48},{64,72... | collective-permute-start | bytes 184328 | tf_op jit(solution)/shard_map/cond/branch_1_fun/ppermute | solution.py:435
  25.5 1.3 %collective-permute-start.9 = (f32[5,5,8,128]{3,2,1,0:T(8,128)S(1)}, f32[5,5,8,128]{3,2,1,0:T(8,128)S(1)}, u32[]{:S(2)}, u32[]{:S(2)}) collective-permute-start(f32[5,5,8,128]{3,2,1,0:T(8,128)S(1)} %collective-permute-done.5.five), channel_id=1, source_target_pairs={{0,8},{8,0},{16,24},{24,16},{32,40},{40,32},{48,56},{56,48},{64,72... | collective-permute-start | bytes 307208 | tf_op jit(solution)/shard_map/cond/branch_1_fun/ppermute | solution.py:435
  28.1 3.7 %collective-permute-start.10 = (f32[8,128]{1,0:T(8,128)S(1)}, f32[8,128]{1,0:T(8,128)S(1)}, u32[]{:S(2)}, u32[]{:S(2)}) collective-permute-start(f32[8,128]{1,0:T(8,128)S(1)} %get-tuple-element.132), channel_id=1, source_target_pairs={{0,1},{1,0},{2,3},{3,2},{4,5},{5,4},{6,7},{7,6},{8,9},{9,8},{10,11... | collective-permute-start | bytes 12296 | tf_op jit(solution)/shard_map/ppermute | solution.py:553
